TPU v7x, 32 devices: a whole 2x2x4 slice. The times are simulated.
32 devices in a mesh: dp: 8 (over y, x, core), tensor: 4 (over z).
Axes of the slice: x: 2, y: 2, z: 4, core: 2. Of those that a mesh axis runs over, the one named last changes fastest.
Arguments:
- tokens: bfloat16 [8192, 2048], P('dp'), may hold values from -6 to 6
- positions: int32 [8, 1024], P('dp'), may hold values from 0 to 2046, as said below
- span_starts: int32 [8, 2], P('dp'), may hold values from 0 to 768, as said below
- attention_gain: bfloat16 [2048], replicated, may hold values from 0.099609375 to 1.8984375
- query_weight: bfloat16 [2048, 2048], P(None, 'tensor'), may hold values from -0.125 to 0.125
- key_matrix: bfloat16 [2048, 1024], P(None, 'tensor'), may hold values from -0.125 to 0.125
- value_matrix: bfloat16 [2048, 1024], P(None, 'tensor'), may hold values from -0.125 to 0.125
- query_gain: bfloat16 [128], replicated, may hold values from 0.5 to 2
- key_gain: bfloat16 [128], replicated, may hold values from 0.5 to 2
- output_weight: bfloat16 [2048, 2048], P('tensor'), may hold values from -1 to 1
- feedforward_gain: bfloat16 [2048], replicated, may hold values from 0.099609375 to 1.8984375
- gate_weight: bfloat16 [2048, 6144], P(None, 'tensor'), may hold values from -0.125 to 0.125
- up_weight: bfloat16 [2048, 6144], P(None, 'tensor'), may hold values from -0.125 to 0.125
- down_weight: bfloat16 [6144, 2048], P('tensor'), may hold values from -0.078125 to 0.078125
- cotangent: bfloat16 [8192, 2048], P('dp'), may hold values from -6 to 6
Outputs:
- block_output: bfloat16 [8192, 2048], P('dp')
- tokens_grad: bfloat16 [8192, 2048], P('dp')
- attention_gain_grad: float32 [2048], P('dp')
- query_weight_grad: float32 [2048, 2048], P('dp', 'tensor')
- key_weight_grad: float32 [2048, 1024], P('dp', 'tensor')
- value_weight_grad: float32 [2048, 1024], P('dp', 'tensor')
- query_gain_grad: float32 [128], P('dp')
- key_gain_grad: float32 [128], P('dp')
- output_weight_grad: float32 [2048, 2048], P('tensor', 'dp')
- feedforward_gain_grad: float32 [2048], P('dp')
- gate_weight_grad: float32 [2048, 6144], P('dp', 'tensor')
- up_weight_grad: float32 [2048, 6144], P('dp', 'tensor')
- down_weight_grad: float32 [6144, 2048], P('tensor', 'dp')
Inputs may be any that keep to these rules, and one draw needn't show every extreme that they name: Within each sequence positions start at 0 and rise by 1 or 2 from one token to the next. `span_starts`: each sequence has two picture spans of 256 tokens: the first starts and ends within the first 512 tokens, the second starts at 512 or later and ends inside the sequence.
All inputs are finite; a program needn't handle non-finite values.
Results may differ from a plain program's by a relative error of at most 0.015.
Values sent between devices are 32-bit elements; how exact they have to be, the bound alone decides.
No kernel may reach another device: no remote copies, remote signals or barrier semaphores. Data moves between devices by JAX's collectives and lax.ppermute only.
A program may use at most 256 MiB of HBM per device.

v0:
```python
import math

import jax
import jax.numpy as jnp
from jax import lax
from jax.sharding import PartitionSpec as P

SPAN = 256


epsilon = 1e-06
rope_base = 1000000.0


def contract(left, right, left_dim, right_dim):
    return lax.dot_general(
        left, right, (((left_dim,), (right_dim,)), ((), ())), preferred_element_type=jnp.float32
    )


def norm_rows(values, gain):
    factor = lax.rsqrt(jnp.mean(values * values, axis=-1, keepdims=True) + epsilon)
    return (values * factor * gain, factor)


def norm_back(values, factor, gain, grad_out):
    scaled = grad_out * gain
    inner_sum = jnp.sum(scaled * values, axis=-1, keepdims=True)
    grad_in = factor * scaled - values * (factor * factor * factor) * inner_sum / values.shape[-1]
    return (grad_in, grad_out * values * factor)


def rotate_half(values, cosine, sine):
    half_size = values.shape[-1] // 2
    first_half = values[..., :half_size]
    second_half = values[..., half_size:]
    return jnp.concatenate(
        [first_half * cosine - second_half * sine, second_half * cosine + first_half * sine],
        axis=-1,
    )


def rotate_back(values, cosine, sine):
    half_size = values.shape[-1] // 2
    first_half = values[..., :half_size]
    second_half = values[..., half_size:]
    return jnp.concatenate(
        [first_half * cosine + second_half * sine, second_half * cosine - first_half * sine],
        axis=-1,
    )


def span_mask(starts, seq_length):
    token_index = jnp.arange(seq_length, dtype=jnp.int32)
    inside = (token_index[None, :] >= starts[:, None]) & (
        token_index[None, :] < starts[:, None] + SPAN
    )
    span_number = jnp.arange(starts.shape[0], dtype=jnp.int32)[:, None] + 1
    span_label = jnp.sum(inside.astype(jnp.int32) * span_number, axis=0)
    causal = token_index[:, None] >= token_index[None, :]
    same_span = (span_label[:, None] == span_label[None, :]) & (span_label[:, None] > 0)
    return causal | same_span


def score_block(query_rows, key_heads, allowed, score_scale):
    scores = (
        jnp.einsum("qhgd,khd->hgqk", query_rows, key_heads, preferred_element_type=jnp.float32)
        * score_scale
    )
    return jnp.where(allowed, scores, -jnp.inf)


def attend(query_rows, key_heads, heads_value, allowed, score_scale):
    scores = score_block(query_rows, key_heads, allowed, score_scale)
    highest = jnp.max(scores, axis=-1, keepdims=True)
    exponent = jnp.exp(scores - highest)
    denominator = jnp.sum(exponent, axis=-1, keepdims=True)
    probability = (exponent / denominator).astype(jnp.bfloat16)
    mixed_heads = jnp.einsum(
        "hgqk,khd->qhgd", probability, heads_value, preferred_element_type=jnp.float32
    )
    return (mixed_heads.astype(jnp.bfloat16), (highest + jnp.log(denominator))[..., 0])


def attend_back(query_rows, key_heads, heads_value, allowed, log_total, grad_mixed, score_scale):
    scores = score_block(query_rows, key_heads, allowed, score_scale)
    probability = jnp.exp(scores - log_total[..., None])
    grad_value = jnp.einsum(
        "hgqk,qhgd->khd",
        probability.astype(jnp.bfloat16),
        grad_mixed,
        preferred_element_type=jnp.float32,
    )
    grad_prob = jnp.einsum(
        "qhgd,khd->hgqk", grad_mixed, heads_value, preferred_element_type=jnp.float32
    )
    grad_scores = probability * (
        grad_prob - jnp.sum(probability * grad_prob, axis=-1, keepdims=True)
    )
    grad_low = grad_scores.astype(jnp.bfloat16)
    grad_queries = (
        jnp.einsum("hgqk,khd->qhgd", grad_low, key_heads, preferred_element_type=jnp.float32)
        * score_scale
    )
    grad_keys = (
        jnp.einsum("hgqk,qhgd->khd", grad_low, query_rows, preferred_element_type=jnp.float32)
        * score_scale
    )
    return (grad_queries, grad_keys, grad_value.astype(jnp.bfloat16))


def shards(
    tokens,
    positions,
    span_starts,
    attention_gain,
    query_weight,
    key_matrix,
    value_matrix,
    query_gain,
    key_gain,
    output_weight,
    feedforward_gain,
    gate_weight,
    up_weight,
    down_weight,
    cotangent,
):
    seq_count, seq_length = positions.shape
    head_size = query_gain.shape[0]
    query_heads = query_weight.shape[1] // head_size
    kv_heads = key_matrix.shape[1] // head_size
    group_size = query_heads // kv_heads
    token_count = seq_count * seq_length
    score_scale = head_size ** (-0.5)
    attention_gain_f = attention_gain.astype(jnp.float32)
    feedforward_gain_f = feedforward_gain.astype(jnp.float32)
    query_gain_f = query_gain.astype(jnp.float32)
    key_gain_f = key_gain.astype(jnp.float32)
    inputs = tokens.astype(jnp.float32)
    normalized_rows, factor_one = norm_rows(inputs, attention_gain_f)
    normed_low = normalized_rows.astype(jnp.bfloat16)
    query_raw = jnp.dot(normed_low, query_weight, preferred_element_type=jnp.float32).reshape(
        token_count, query_heads, head_size
    )
    key_unrotated = jnp.dot(normed_low, key_matrix, preferred_element_type=jnp.float32).reshape(
        token_count, kv_heads, head_size
    )
    value_low = jnp.dot(normed_low, value_matrix, preferred_element_type=jnp.float32).astype(
        jnp.bfloat16
    )
    frequency = jnp.exp(
        jnp.arange(head_size // 2, dtype=jnp.float32) * (-2.0 * math.log(rope_base) / head_size)
    )
    angles = positions.astype(jnp.float32).reshape(token_count)[:, None] * frequency
    cosine = jnp.cos(angles)[:, None, :]
    sine = jnp.sin(angles)[:, None, :]
    query_normed, query_factor = norm_rows(query_raw, query_gain_f)
    key_normed, key_factor = norm_rows(key_unrotated, key_gain_f)
    query_low = rotate_half(query_normed, cosine, sine).astype(jnp.bfloat16)
    key_low = rotate_half(key_normed, cosine, sine).astype(jnp.bfloat16)
    query_seqs = query_low.reshape(seq_count, seq_length, kv_heads, group_size, head_size)
    key_seqs = key_low.reshape(seq_count, seq_length, kv_heads, head_size)
    value_seqs = value_low.reshape(seq_count, seq_length, kv_heads, head_size)

    def forward_one(sequence_items):
        sequence_queries, sequence_keys, sequence_values, sequence_starts = sequence_items
        allowed = span_mask(sequence_starts, seq_length)
        return attend(sequence_queries, sequence_keys, sequence_values, allowed, score_scale)

    mixed_seqs, log_total = lax.map(forward_one, (query_seqs, key_seqs, value_seqs, span_starts))
    mixed_low = mixed_seqs.reshape(token_count, query_heads * head_size)
    attention_part = jnp.dot(mixed_low, output_weight, preferred_element_type=jnp.float32)
    attention_full = lax.psum(attention_part, "tensor")
    residual = inputs + attention_full
    normed_two, factor_two = norm_rows(residual, feedforward_gain_f)
    normed_two_low = normed_two.astype(jnp.bfloat16)
    gate_values = jnp.dot(normed_two_low, gate_weight, preferred_element_type=jnp.float32)
    up_values = jnp.dot(normed_two_low, up_weight, preferred_element_type=jnp.float32)
    hidden_low = (jax.nn.silu(gate_values) * up_values).astype(jnp.bfloat16)
    feedforward_part = jnp.dot(hidden_low, down_weight, preferred_element_type=jnp.float32)
    feedforward_full = lax.psum(feedforward_part, "tensor")
    block_output = (residual + feedforward_full).astype(jnp.bfloat16)
    grad_output = cotangent.astype(jnp.float32)
    down_grad = contract(hidden_low, cotangent, 0, 0)
    grad_hidden = contract(cotangent, down_weight, 1, 1)
    sigmoid_gate = jax.nn.sigmoid(gate_values)
    grad_gate = (
        grad_hidden * up_values * sigmoid_gate * (1.0 + gate_values * (1.0 - sigmoid_gate))
    ).astype(jnp.bfloat16)
    grad_up = (grad_hidden * (gate_values * sigmoid_gate)).astype(jnp.bfloat16)
    gate_grad = contract(normed_two_low, grad_gate, 0, 0)
    up_grad = contract(normed_two_low, grad_up, 0, 0)
    grad_normed_part = contract(grad_gate, gate_weight, 1, 1) + contract(grad_up, up_weight, 1, 1)
    grad_normed_two = lax.psum(grad_normed_part, "tensor")
    grad_residual_norm, feedforward_gain_rows = norm_back(
        residual, factor_two, feedforward_gain_f, grad_normed_two
    )
    feedforward_gain_part = jnp.sum(feedforward_gain_rows, axis=0)
    grad_residual = grad_output + grad_residual_norm
    grad_residual_low = grad_residual.astype(jnp.bfloat16)
    output_grad = contract(mixed_low, grad_residual_low, 0, 0)
    grad_mixed = contract(grad_residual_low, output_weight, 1, 1).astype(jnp.bfloat16)
    grad_mixed_seqs = grad_mixed.reshape(seq_count, seq_length, kv_heads, group_size, head_size)

    def backward_one(sequence_items):
        (
            sequence_queries,
            sequence_keys,
            sequence_values,
            sequence_starts,
            sequence_total,
            sequence_grad,
        ) = sequence_items
        allowed = span_mask(sequence_starts, seq_length)
        return attend_back(
            sequence_queries,
            sequence_keys,
            sequence_values,
            allowed,
            sequence_total,
            sequence_grad,
            score_scale,
        )

    grad_query_rot, grad_key_rot, grad_value_low = lax.map(
        backward_one, (query_seqs, key_seqs, value_seqs, span_starts, log_total, grad_mixed_seqs)
    )
    grad_query_norm = rotate_back(
        grad_query_rot.reshape(token_count, query_heads, head_size), cosine, sine
    )
    grad_key_norm = rotate_back(
        grad_key_rot.reshape(token_count, kv_heads, head_size), cosine, sine
    )
    grad_query_raw, query_gain_rows = norm_back(
        query_raw, query_factor, query_gain_f, grad_query_norm
    )
    grad_key_raw, key_gain_rows = norm_back(key_unrotated, key_factor, key_gain_f, grad_key_norm)
    query_gain_part = jnp.sum(query_gain_rows, axis=(0, 1))
    key_gain_part = jnp.sum(key_gain_rows, axis=(0, 1))
    grad_query_low = grad_query_raw.reshape(token_count, query_heads * head_size).astype(
        jnp.bfloat16
    )
    grad_key_low = grad_key_raw.reshape(token_count, kv_heads * head_size).astype(jnp.bfloat16)
    grad_value_flat = grad_value_low.reshape(token_count, kv_heads * head_size)
    query_grad = contract(normed_low, grad_query_low, 0, 0)
    key_grad = contract(normed_low, grad_key_low, 0, 0)
    value_grad = contract(normed_low, grad_value_flat, 0, 0)
    grad_input_part = (
        contract(grad_query_low, query_weight, 1, 1)
        + contract(grad_key_low, key_matrix, 1, 1)
        + contract(grad_value_flat, value_matrix, 1, 1)
    )
    grad_normed_one, query_gain_sum, key_gain_sum = lax.psum(
        (grad_input_part, query_gain_part, key_gain_part), "tensor"
    )
    grad_input_norm, attention_gain_rows = norm_back(
        inputs, factor_one, attention_gain_f, grad_normed_one
    )
    attention_gain_part = jnp.sum(attention_gain_rows, axis=0)
    tokens_grad = (grad_residual + grad_input_norm).astype(jnp.bfloat16)
    (
        attention_gain_share,
        query_share,
        key_share,
        value_share,
        query_gain_share,
        key_gain_share,
        output_share,
        feedforward_gain_share,
        gate_share,
        up_share,
        down_share,
    ) = (
        lax.psum_scatter(attention_gain_part, "dp", scatter_dimension=0, tiled=True),
        lax.psum_scatter(query_grad, "dp", scatter_dimension=0, tiled=True),
        lax.psum_scatter(key_grad, "dp", scatter_dimension=0, tiled=True),
        lax.psum_scatter(value_grad, "dp", scatter_dimension=0, tiled=True),
        lax.psum_scatter(query_gain_sum, "dp", scatter_dimension=0, tiled=True),
        lax.psum_scatter(key_gain_sum, "dp", scatter_dimension=0, tiled=True),
        lax.psum_scatter(output_grad, "dp", scatter_dimension=1, tiled=True),
        lax.psum_scatter(feedforward_gain_part, "dp", scatter_dimension=0, tiled=True),
        lax.psum_scatter(gate_grad, "dp", scatter_dimension=0, tiled=True),
        lax.psum_scatter(up_grad, "dp", scatter_dimension=0, tiled=True),
        lax.psum_scatter(down_grad, "dp", scatter_dimension=1, tiled=True),
    )
    return (
        block_output,
        tokens_grad,
        attention_gain_share,
        query_share,
        key_share,
        value_share,
        query_gain_share,
        key_gain_share,
        output_share,
        feedforward_gain_share,
        gate_share,
        up_share,
        down_share,
    )


def solution(mesh):
    return jax.shard_map(
        shards,
        mesh=mesh,
        in_specs=(
            P("dp", None),
            P("dp", None),
            P("dp", None),
            P(),
            P(None, "tensor"),
            P(None, "tensor"),
            P(None, "tensor"),
            P(),
            P(),
            P("tensor", None),
            P(),
            P(None, "tensor"),
            P(None, "tensor"),
            P("tensor", None),
            P("dp", None),
        ),
        out_specs=(
            P("dp", None),
            P("dp", None),
            P("dp"),
            P("dp", "tensor"),
            P("dp", "tensor"),
            P("dp", "tensor"),
            P("dp"),
            P("dp"),
            P("tensor", "dp"),
            P("dp"),
            P("dp", "tensor"),
            P("dp", "tensor"),
            P("tensor", "dp"),
        ),
        check_vma=False,
    )
```

profile of v0, /device:TPU:0, one launch (start us, length us, event | category | flops | bytes accessed | tf_op | source)
XLA Modules:
  0.0 1855.1 jit_solution(10099514420445605962)
XLA Ops:
  76.5 293.1 %all-reduce.11.cloned.1.call-done = f32[1024,2048]{1,0:T(8,128)} async-done(((f32[1024,2048]{1,0:T(8,128)}), f32[1024,2048]{1,0:T(8,128)}) %all-reduce.11.cloned.1.call-update) | async-done | bytes 8388624 | tf_op jit(solution)/shard_map/psum | solution.py:174
  378.5 12.0 fusion.57
  390.5 10.7 fusion.56
  401.2 15.3 multiply_convert_fusion.1
  416.5 10.0 fusion.59
  426.5 11.0 convolution_add_fusion
  438.7 11.9 fusion.58
  450.7 276.8 %all-reduce.13.cloned.1.call-done = f32[1024,2048]{1,0:T(8,128)} async-done(((f32[1024,2048]{1,0:T(8,128)}), f32[1024,2048]{1,0:T(8,128)}) %all-reduce.13.cloned.1.call-update) | async-done | bytes 8388624 | tf_op jit(solution)/shard_map/psum | solution.py:195
  734.7 9.7 subtract_add_fusion
  757.2 9.5 fusion.1
  824.4 12.3 fusion.67
  836.7 12.6 fusion.66
  849.4 12.6 fusion.65
  864.6 496.0 %all-reduce.15.cloned.1.call-done = (f32[1024,2048]{1,0:T(8,128)}, f32[1024,2048]{1,0:T(8,128)}) async-done(((f32[1024,2048]{1,0:T(8,128)}, f32[1024,2048]{1,0:T(8,128)}), (f32[1024,2048]{1,0:T(8,128)}, f32[1024,2048]{1,0:T(8,128)})) %all-reduce.15.cloned.1.call-update) | async-done | bytes 16777232 | tf_op jit(solution)/shard_map/psum | solution.py:182
  1366.7 24.3 %all-reduce.4 = (f32[2048]{0:T(1024)S(1)}, f32[128]{0:T(128)S(1)}, f32[128]{0:T(128)S(1)}, f32[2048]{0:T(1024)S(1)}) all-reduce(f32[2048]{0:T(1024)S(1)} %get-tuple-element.56, f32[128]{0:T(128)S(1)} %bitcast_reduce_fusion, f32[128]{0:T(128)S(1)} %bitcast_reduce_fusion.1, ...), channel_id=2, replica_groups=mesh['dp'=8,'tensor'=4] {'dp'}, use_global_device_ids=true, to_apply=%region_17.18.clone | all-reduce | flops 4352 | bytes 34816
  1392.5 9.9 all-reduce.5
  1402.3 9.5 add_convert_fusion
  1411.8 10.0 fusion.15
  1421.8 27.5 %reduce-scatter.10.cloned.1.call-done = f32[256,256]{1,0:T(8,128)} async-done(((f32[2048,256]{1,0:T(8,128)}), f32[256,256]{1,0:T(8,128)}) %reduce-scatter.10.cloned.1.call-update) | async-done | bytes 262160 | tf_op jit(solution)/shard_map/reduce_scatter | solution.py:277
  1449.3 54.9 %reduce-scatter.14.cloned.1.call-done = f32[512,256]{1,0:T(8,128)} async-done(((f32[512,2048]{1,0:T(8,128)}), f32[512,256]{1,0:T(8,128)}) %reduce-scatter.14.cloned.1.call-update) | async-done | bytes 524304 | tf_op jit(solution)/shard_map/reduce_scatter | solution.py:281
  1504.2 55.1 %reduce-scatter.8.cloned.1.call-done = f32[256,512]{1,0:T(8,128)} async-done(((f32[2048,512]{1,0:T(8,128)}), f32[256,512]{1,0:T(8,128)}) %reduce-scatter.8.cloned.1.call-update) | async-done | bytes 524304 | tf_op jit(solution)/shard_map/reduce_scatter | solution.py:276
  1559.3 96.1 %reduce-scatter.20.cloned.1.call-done = f32[1536,256]{1,0:T(8,128)} async-done(((f32[1536,2048]{1,0:T(8,128)}), f32[1536,256]{1,0:T(8,128)}) %reduce-scatter.20.cloned.1.call-update) | async-done | bytes 1572880 | tf_op jit(solution)/shard_map/reduce_scatter | solution.py:285
  1655.4 96.4 %reduce-scatter.18.cloned.1.call-done = f32[256,1536]{1,0:T(8,128)} async-done(((f32[2048,1536]{1,0:T(8,128)}), f32[256,1536]{1,0:T(8,128)}) %reduce-scatter.18.cloned.1.call-update) | async-done | bytes 1572880 | tf_op jit(solution)/shard_map/reduce_scatter | solution.py:284
  1751.8 96.2 %reduce-scatter.16.cloned.1.call-done = f32[256,1536]{1,0:T(8,128)} async-done(((f32[2048,1536]{1,0:T(8,128)}), f32[256,1536]{1,0:T(8,128)}) %reduce-scatter.16.cloned.1.call-update) | async-done | bytes 1572880 | tf_op jit(solution)/shard_map/reduce_scatter | solution.py:283
  (219 shorter events, 165.2 us)
Async XLA Ops:
  7.2 22.8 %copy-start = (bf16[2048,512]{1,0:T(8,128)(2,1)S(1)}, bf16[2048,512]{1,0:T(8,128)(2,1)}, u32[]{:S(2)}) copy-start(bf16[2048,512]{1,0:T(8,128)(2,1)} %param.19) | copy-start | bytes 6291460
  7.2 362.4 %all-reduce.11.cloned.1.call-start = ((), (), s32[]{:S(2)}) async-start(), calls=%async_computation.7 | async-start | bytes 16777216 | tf_op jit(solution)/shard_map/psum | solution.py:174
  8.1 430.1 %copy-start.49 = (f32[128]{0:T(128)}, f32[128]{0:T(128)S(1)}, u32[]{:S(2)}) copy-start(f32[128]{0:T(128)S(1)} %convert_element_type.96) | copy-start | bytes 1540
  8.7 428.8 %copy-start.52 = (f32[128]{0:T(128)}, f32[128]{0:T(128)S(1)}, u32[]{:S(2)}) copy-start(f32[128]{0:T(128)S(1)} %convert_element_type.94) | copy-start | bytes 1540
  14.5 11.0 copy-start.43
  16.2 20.6 %copy-start.9 = (f32[1024,64]{0,1:T(8,128)}, f32[1024,64]{0,1:T(8,128)S(1)}, u32[]{:S(2)}) copy-start(f32[1024,64]{0,1:T(8,128)S(1)} %get-tuple-element.99) | copy-start | bytes 786436
  28.5 14.5 copy-start.41
  30.0 12.9 copy-start.5
  75.8 651.6 %all-reduce.13.cloned.1.call-start = ((), (), s32[]{:S(2)}) async-start(), calls=%async_computation.8 | async-start | bytes 16777216 | tf_op jit(solution)/shard_map/psum | solution.py:195
  378.5 12.0 copy-start.16
  390.5 10.7 copy-start.14
  437.5 923.1 %all-reduce.15.cloned.1.call-start = ((), (), s32[]{:S(2)}) async-start(), calls=%async_computation.16 | async-start | bytes 33554432 | tf_op jit(solution)/shard_map/psum | solution.py:182
  734.7 17.4 slice-start
  734.7 17.4 slice-start.1
  734.7 17.4 slice-start.2
  799.3 622.5 %reduce-scatter.12.cloned.1.call-start = ((), (), s32[]{:S(2)}) async-start(), calls=%async_computation.11 | async-start | bytes 2359296 | tf_op jit(solution)/shard_map/reduce_scatter | solution.py:278
  804.3 645.0 %reduce-scatter.10.cloned.1.call-start = ((), (), s32[]{:S(2)}) async-start(), calls=%async_computation.10 | async-start | bytes 2359296 | tf_op jit(solution)/shard_map/reduce_scatter | solution.py:277
  809.4 694.8 %reduce-scatter.14.cloned.1.call-start = ((), (), s32[]{:S(2)}) async-start(), calls=%async_computation.12 | async-start | bytes 4718592 | tf_op jit(solution)/shard_map/reduce_scatter | solution.py:281
  817.6 741.7 %reduce-scatter.8.cloned.1.call-start = ((), (), s32[]{:S(2)}) async-start(), calls=%async_computation.9 | async-start | bytes 4718592 | tf_op jit(solution)/shard_map/reduce_scatter | solution.py:276
  824.3 831.1 %reduce-scatter.20.cloned.1.call-start = ((), (), s32[]{:S(2)}) async-start(), calls=%async_computation.15 | async-start | bytes 14155776 | tf_op jit(solution)/shard_map/reduce_scatter | solution.py:285
  836.6 915.2 %reduce-scatter.18.cloned.1.call-start = ((), (), s32[]{:S(2)}) async-start(), calls=%async_computation.14 | async-start | bytes 14155776 | tf_op jit(solution)/shard_map/reduce_scatter | solution.py:284
  849.3 998.7 %reduce-scatter.16.cloned.1.call-start = ((), (), s32[]{:S(2)}) async-start(), calls=%async_computation.13 | async-start | bytes 14155776 | tf_op jit(solution)/shard_map/reduce_scatter | solution.py:283
  862.0 498.6 %copy-start.40 = (f32[2048]{0:T(1024)S(1)}, f32[2048]{0:T(1024)}, u32[]{:S(2)}) copy-start(f32[2048]{0:T(1024)} %copy-done.39) | copy-start | bytes 24580
  862.0 498.6 %copy-start.44 = (f32[1024]{0:T(1024)S(1)}, f32[1024]{0:T(1024)}, u32[]{:S(2)}) copy-start(f32[1024]{0:T(1024)} %copy-done.43) | copy-start | bytes 12292
  (51 other events, 241.4 us)
Sparse Core Ops, SparseCore 0:
  76.0 293.5 all-reduce.10
  437.6 289.7 all-reduce.12
  799.4 561.1 all-reduce.14
  1364.3 40.0 reduce-scatter.11
  1408.2 41.1 reduce-scatter.9
  1453.1 51.0 reduce-scatter.13
  1508.1 51.1 reduce-scatter.7
  1563.4 91.9 reduce-scatter.19
  1659.5 92.2 reduce-scatter.17
  1755.8 92.2 reduce-scatter.15
where the time goes:
time: 1860 us
  waiting for transfers between devices  1490 us (80%)
  matrix products  199 us (11%)
  other arithmetic  93.2 us (5%)
  blocking collectives  34.2 us (2%)
  local copies, waits for them, and re-layouts  19.7 us (1%)
    psum x1, waiting for transfers between devices, shards(): feedforward_full = lax.psum(feedforward_part, 'tensor')  496 us
    psum x1, waiting for transfers between devices, shards(): attention_full = lax.psum(attention_part, 'tensor')  293 us
    psum x1, waiting for transfers between devices, shards(): grad_normed_two = lax.psum(grad_normed_part, 'tensor')  277 us
    dot_general x14, matrix products, contract(): lax.dot_general(left, right, (((left_dim,), (right_dim,)), ((), ())), pre...  115 us
    reduce_scatter x1, waiting for transfers between devices, shards(): lax.psum_scatter(up_grad, 'dp', scatter_dimension=0, tiled=True)  96.4 us
    reduce_scatter x1, waiting for transfers between devices, shards(): lax.psum_scatter(gate_grad, 'dp', scatter_dimension=0, tiled=True)  96.2 us
    reduce_scatter x1, waiting for transfers between devices, shards(): lax.psum_scatter(down_grad, 'dp', scatter_dimension=1, tiled=True)  96.1 us
    reduce_scatter x1, waiting for transfers between devices, shards(): lax.psum_scatter(query_grad, 'dp', scatter_dimension=0, tiled=True)  55.1 us
  transfers between devices with their start and end apart: 10, of which 9 were waited for; matrix products, arithmetic and copies ran while one was open for 6% of the time, Pallas kernels for 0%

commit v1 on v0

v1 whole, which is shorter than its diff:
```python
import math

import jax
import jax.numpy as jnp
from jax import lax
from jax.sharding import PartitionSpec as P

SPAN = 256
HALF = 512

epsilon = 1e-06
rope_base = 1000000.0


def contract(left, right, left_dim, right_dim):
    return lax.dot_general(
        left, right, (((left_dim,), (right_dim,)), ((), ())), preferred_element_type=jnp.float32
    )


def norm_rows(values, gain):
    factor = lax.rsqrt(jnp.mean(values * values, axis=-1, keepdims=True) + epsilon)
    return (values * factor * gain, factor)


def norm_back(values, factor, gain, grad_out):
    scaled = grad_out * gain
    inner_sum = jnp.sum(scaled * values, axis=-1, keepdims=True)
    grad_in = factor * scaled - values * (factor * factor * factor) * inner_sum / values.shape[-1]
    return (grad_in, grad_out * values * factor)


def rotate_half(values, cosine, sine):
    half_size = values.shape[-1] // 2
    first_half = values[..., :half_size]
    second_half = values[..., half_size:]
    return jnp.concatenate(
        [first_half * cosine - second_half * sine, second_half * cosine + first_half * sine],
        axis=-1,
    )


def rotate_back(values, cosine, sine):
    half_size = values.shape[-1] // 2
    first_half = values[..., :half_size]
    second_half = values[..., half_size:]
    return jnp.concatenate(
        [first_half * cosine + second_half * sine, second_half * cosine - first_half * sine],
        axis=-1,
    )


def span_mask(starts, seq_length):
    token_index = jnp.arange(seq_length, dtype=jnp.int32)
    inside = (token_index[None, :] >= starts[:, None]) & (
        token_index[None, :] < starts[:, None] + SPAN
    )
    span_number = jnp.arange(starts.shape[0], dtype=jnp.int32)[:, None] + 1
    span_label = jnp.sum(inside.astype(jnp.int32) * span_number, axis=0)
    causal = token_index[:, None] >= token_index[None, :]
    same_span = (span_label[:, None] == span_label[None, :]) & (span_label[:, None] > 0)
    return causal | same_span


def score_block(query_rows, key_heads, allowed, score_scale):
    scores = (
        jnp.einsum("qhgd,khd->hgqk", query_rows, key_heads, preferred_element_type=jnp.float32)
        * score_scale
    )
    return jnp.where(allowed, scores, -jnp.inf)


def attend(query_rows, key_heads, heads_value, allowed, score_scale):
    scores = score_block(query_rows, key_heads, allowed, score_scale)
    highest = jnp.max(scores, axis=-1, keepdims=True)
    exponent = jnp.exp(scores - highest)
    denominator = jnp.sum(exponent, axis=-1, keepdims=True)
    probability = (exponent / denominator).astype(jnp.bfloat16)
    mixed_heads = jnp.einsum(
        "hgqk,khd->qhgd", probability, heads_value, preferred_element_type=jnp.float32
    )
    return (mixed_heads, (highest + jnp.log(denominator))[..., 0])


def attend_back(query_rows, key_heads, heads_value, allowed, log_total, grad_mixed, score_scale):
    scores = score_block(query_rows, key_heads, allowed, score_scale)
    probability = jnp.exp(scores - log_total[..., None])
    grad_value = jnp.einsum(
        "hgqk,qhgd->khd",
        probability.astype(jnp.bfloat16),
        grad_mixed,
        preferred_element_type=jnp.float32,
    )
    grad_prob = jnp.einsum(
        "qhgd,khd->hgqk", grad_mixed, heads_value, preferred_element_type=jnp.float32
    )
    grad_scores = probability * (
        grad_prob - jnp.sum(probability * grad_prob, axis=-1, keepdims=True)
    )
    grad_low = grad_scores.astype(jnp.bfloat16)
    grad_queries = (
        jnp.einsum("hgqk,khd->qhgd", grad_low, key_heads, preferred_element_type=jnp.float32)
        * score_scale
    )
    grad_keys = (
        jnp.einsum("hgqk,qhgd->khd", grad_low, query_rows, preferred_element_type=jnp.float32)
        * score_scale
    )
    return (grad_queries, grad_keys, grad_value)


def chain_gather(block, count, place):
    upward = block
    downward = block
    from_below = [block]
    from_above = [block]
    for step in range(1, count):
        upward = lax.ppermute(upward, "tensor", [(i, i + 1) for i in range(step - 1, count - 1)])
        downward = lax.ppermute(downward, "tensor", [(i, i - 1) for i in range(1, count - step + 1)])
        from_below.append(upward)
        from_above.append(downward)
    return [block] + [
        jnp.where(place >= slot, from_below[slot], from_above[count - slot])
        for slot in range(1, count)
    ]


def chain_reduce(parts, count):
    upward = parts[count - 1]
    downward = parts[1 % count]
    for step in range(1, count):
        upward = lax.ppermute(upward, "tensor", [(i, i + 1) for i in range(step)])
        downward = lax.ppermute(downward, "tensor", [(i, i - 1) for i in range(count - step, count)])
        if step < count - 1:
            upward = upward + parts[count - 1 - step]
            downward = downward + parts[step + 1]
    return parts[0] + upward + downward


def row_block(values, start, rows):
    return lax.dynamic_slice_in_dim(values, start, rows, axis=0)


def shards(
    tokens,
    positions,
    span_starts,
    attention_gain,
    query_weight,
    key_matrix,
    value_matrix,
    query_gain,
    key_gain,
    output_weight,
    feedforward_gain,
    gate_weight,
    up_weight,
    down_weight,
    cotangent,
):
    low = jnp.bfloat16
    ranks = lax.axis_size("tensor")
    groups = lax.axis_size("dp")
    place = lax.axis_index("tensor")
    group = lax.axis_index("dp")
    seq_count, seq_length = positions.shape
    head_size = query_gain.shape[0]
    local_width = query_weight.shape[1]
    model_width = query_weight.shape[0]
    query_heads = local_width // head_size
    kv_heads = key_matrix.shape[1] // head_size
    group_size = query_heads // kv_heads
    token_count = seq_count * seq_length
    score_scale = head_size ** (-0.5)
    attention_gain_f = attention_gain.astype(jnp.float32)
    feedforward_gain_f = feedforward_gain.astype(jnp.float32)
    query_gain_f = query_gain.astype(jnp.float32)
    key_gain_f = key_gain.astype(jnp.float32)

    unit = jnp.where(positions[0, 0] >= 0, 1.0, 0.0)

    weight_rows = local_width // groups
    own_rows = row_block(output_weight, group * weight_rows, weight_rows).astype(jnp.float32)
    whole_weight = lax.all_gather(own_rows, ("tensor", "dp"), axis=0, tiled=True)
    whole_weight = (whole_weight * unit).astype(low)

    inputs = tokens.astype(jnp.float32)
    normalized_rows, factor_one = norm_rows(inputs, attention_gain_f)
    normed_low = normalized_rows.astype(low)
    query_raw = jnp.dot(normed_low, query_weight, preferred_element_type=jnp.float32).reshape(
        token_count, query_heads, head_size
    )
    key_unrotated = jnp.dot(normed_low, key_matrix, preferred_element_type=jnp.float32).reshape(
        token_count, kv_heads, head_size
    )
    value_low = jnp.dot(normed_low, value_matrix, preferred_element_type=jnp.float32).astype(low)
    frequency = jnp.exp(
        jnp.arange(head_size // 2, dtype=jnp.float32) * (-2.0 * math.log(rope_base) / head_size)
    )
    angles = positions.astype(jnp.float32).reshape(token_count)[:, None] * frequency
    cosine = jnp.cos(angles)[:, None, :]
    sine = jnp.sin(angles)[:, None, :]
    query_normed, query_factor = norm_rows(query_raw, query_gain_f)
    key_normed, key_factor = norm_rows(key_unrotated, key_gain_f)
    query_low = rotate_half(query_normed, cosine, sine).astype(low)
    key_low = rotate_half(key_normed, cosine, sine).astype(low)
    query_all = query_low.reshape(token_count, kv_heads, group_size, head_size)
    key_all = key_low.reshape(token_count, kv_heads, head_size)
    value_all = value_low.reshape(token_count, kv_heads, head_size)

    streams = []
    for sequence in range(seq_count):
        base = sequence * seq_length
        streams.append((sequence, base, base + HALF, base + HALF))
        streams.append((sequence, base + HALF, base + seq_length, base + seq_length))
    masks = [span_mask(span_starts[sequence], seq_length) for sequence in range(seq_count)]

    def keys_of(stream):
        sequence, first, end, key_end = stream
        return slice(sequence * seq_length, key_end)

    def mask_of(stream):
        sequence, first, end, key_end = stream
        base = sequence * seq_length
        return masks[sequence][first - base : end - base, : key_end - base]

    state = []
    for stream in streams:
        sequence, first, end, key_end = stream
        keys = keys_of(stream)
        mixed, log_total = attend(
            query_all[first:end], key_all[keys], value_all[keys], mask_of(stream), score_scale
        )
        rows = end - first
        gathered = lax.all_gather(mixed.reshape(rows, local_width), "tensor", axis=0)
        gathered = (gathered * unit).astype(low)
        mixed_whole = gathered.transpose(1, 0, 2).reshape(rows, ranks * local_width)
        state.append({"stream": stream, "log_total": log_total, "mixed": mixed_whole})

    grad_hidden = contract(cotangent, down_weight, 1, 1)

    for item in state:
        _, first, end, _ = item["stream"]
        rows = end - first
        share = rows // ranks
        residual = inputs[first:end] + jnp.dot(
            item["mixed"], whole_weight, preferred_element_type=jnp.float32
        )
        normed_two, factor_two = norm_rows(residual, feedforward_gain_f)
        normed_two_low = normed_two.astype(low)
        gate_values = jnp.dot(normed_two_low, gate_weight, preferred_element_type=jnp.float32)
        up_values = jnp.dot(normed_two_low, up_weight, preferred_element_type=jnp.float32)
        sigmoid_gate = jax.nn.sigmoid(gate_values)
        silu_gate = gate_values * sigmoid_gate
        hidden_low = (silu_gate * up_values).astype(low)
        grad_hidden_rows = grad_hidden[first:end]
        grad_gate = (
            grad_hidden_rows * up_values * sigmoid_gate * (1.0 + gate_values * (1.0 - sigmoid_gate))
        ).astype(low)
        grad_up = (grad_hidden_rows * silu_gate).astype(low)
        grad_normed_part = contract(grad_gate, gate_weight, 1, 1) + contract(
            grad_up, up_weight, 1, 1
        )
        down_part = jnp.dot(hidden_low, down_weight, preferred_element_type=jnp.float32)

        def parts_of(values):
            return [
                row_block(values, ((place + slot) % ranks) * share, share) for slot in range(ranks)
            ]

        grad_normed_two = chain_reduce(parts_of(grad_normed_part), ranks)
        own_first = place * share
        own_residual = row_block(residual, own_first, share)
        own_factor = row_block(factor_two, own_first, share)
        own_mixed = row_block(item["mixed"], own_first, share)
        grad_norm, gain_rows = norm_back(
            own_residual, own_factor, feedforward_gain_f, grad_normed_two
        )
        grad_residual = (
            row_block(cotangent[first:end], own_first, share).astype(jnp.float32) + grad_norm
        )
        grad_residual_low = grad_residual.astype(low)
        grad_mixed_own = contract(grad_residual_low, whole_weight, 1, 1)
        pieces = []
        for slot in range(ranks):
            dest = (place + slot) % ranks
            piece = lax.dynamic_slice_in_dim(grad_mixed_own, dest * local_width, local_width, axis=1)
            if slot:
                piece = lax.ppermute(
                    piece, "tensor", [(i, (i + slot) % ranks) for i in range(ranks)]
                )
            pieces.append(piece)
        swapped = jnp.concatenate(pieces[::-1] + pieces[::-1][:-1], axis=0)
        grad_mixed = row_block(swapped, (ranks - 1 - place) * share, rows)
        grad_mixed = (grad_mixed * unit).astype(low)

        down_sum = chain_reduce(parts_of(down_part), ranks)
        block_slots = chain_gather(own_residual + down_sum, ranks, place)
        item.update(
            normed_two=normed_two_low,
            hidden=hidden_low,
            grad_gate=grad_gate,
            grad_up=grad_up,
            gain_rows=jnp.sum(gain_rows, axis=0),
            grad_residual=grad_residual,
            output_grad=(own_mixed, grad_residual_low),
            grad_mixed=grad_mixed,
            block_slots=block_slots,
        )

    def joined(name):
        return jnp.concatenate([item[name] for item in state], axis=0)

    def ordered(slots):
        share = slots[0].shape[0]
        backwards = slots[::-1]
        both = jnp.concatenate(backwards + backwards[:-1], axis=0)
        return row_block(both, (ranks - 1 - place) * share, share * ranks)

    block_output = jnp.concatenate([ordered(item["block_slots"]) for item in state], axis=0)
    block_output = (block_output * unit).astype(low)
    down_grad = contract(joined("hidden"), cotangent, 0, 0)
    down_share = lax.psum_scatter(down_grad, "dp", scatter_dimension=1, tiled=True)
    gate_up_grad = contract(
        joined("normed_two"),
        jnp.concatenate([joined("grad_gate"), joined("grad_up")], axis=1),
        0,
        0,
    )
    gate_up_share = lax.psum_scatter(gate_up_grad, "dp", scatter_dimension=0, tiled=True)
    hidden_width = gate_weight.shape[1]
    gate_share = gate_up_share[:, :hidden_width]
    up_share = gate_up_share[:, hidden_width:]

    output_grad = contract(
        jnp.concatenate([item["output_grad"][0] for item in state], axis=0),
        jnp.concatenate([item["output_grad"][1] for item in state], axis=0),
        0,
        0,
    )
    output_part = lax.psum_scatter(output_grad, "dp", scatter_dimension=1, tiled=True)
    output_share = chain_reduce(
        [
            row_block(output_part, ((place + slot) % ranks) * local_width, local_width)
            for slot in range(ranks)
        ],
        ranks,
    )

    key_back = [None] * len(state)
    value_back = [None] * len(state)
    query_gain_part = 0.0
    key_gain_part = 0.0
    for index in reversed(range(len(state))):
        item = state[index]
        sequence, first, end, key_end = item["stream"]
        rows = end - first
        base = sequence * seq_length
        keys = keys_of(item["stream"])
        grad_query_rot, grad_key_rot, grad_value = attend_back(
            query_all[first:end],
            key_all[keys],
            value_all[keys],
            mask_of(item["stream"]),
            item["log_total"],
            item["grad_mixed"].reshape(rows, kv_heads, group_size, head_size),
            score_scale,
        )
        if first > base:
            split = first - base
            key_back[index - 1] = grad_key_rot[:split]
            value_back[index - 1] = grad_value[:split]
            grad_key_rot = grad_key_rot[split:]
            grad_value = grad_value[split:]
        else:
            grad_key_rot = grad_key_rot + key_back[index]
            grad_value = grad_value + value_back[index]
        rows_slice = slice(first, end)
        grad_query_norm = rotate_back(
            grad_query_rot.reshape(rows, query_heads, head_size),
            cosine[rows_slice],
            sine[rows_slice],
        )
        grad_key_norm = rotate_back(
            grad_key_rot.reshape(rows, kv_heads, head_size), cosine[rows_slice], sine[rows_slice]
        )
        grad_query_raw, query_gain_rows = norm_back(
            query_raw[rows_slice], query_factor[rows_slice], query_gain_f, grad_query_norm
        )
        grad_key_raw, key_gain_rows = norm_back(
            key_unrotated[rows_slice], key_factor[rows_slice], key_gain_f, grad_key_norm
        )
        query_gain_part = query_gain_part + jnp.sum(query_gain_rows, axis=(0, 1))
        key_gain_part = key_gain_part + jnp.sum(key_gain_rows, axis=(0, 1))
        grad_query_low = grad_query_raw.reshape(rows, query_heads * head_size).astype(low)
        grad_key_low = grad_key_raw.reshape(rows, kv_heads * head_size).astype(low)
        grad_value_low = grad_value.reshape(rows, kv_heads * head_size).astype(low)
        grad_input_part = (
            contract(grad_query_low, query_weight, 1, 1)
            + contract(grad_key_low, key_matrix, 1, 1)
            + contract(grad_value_low, value_matrix, 1, 1)
        )
        share = rows // ranks
        grad_normed_one = chain_reduce(
            [
                row_block(grad_input_part, ((place + slot) % ranks) * share, share)
                for slot in range(ranks)
            ],
            ranks,
        )
        own_first = first + place * share
        grad_norm, gain_rows = norm_back(
            row_block(inputs, own_first, share),
            row_block(factor_one, own_first, share),
            attention_gain_f,
            grad_normed_one,
        )
        item["attention_gain_rows"] = jnp.sum(gain_rows, axis=0)
        item["tokens_slots"] = chain_gather(item["grad_residual"] + grad_norm, ranks, place)
        item["grads"] = jnp.concatenate([grad_query_low, grad_key_low, grad_value_low], axis=1)

    tokens_grad = jnp.concatenate([ordered(item["tokens_slots"]) for item in state], axis=0)
    tokens_grad = (tokens_grad * unit).astype(low)
    qkv_grad = contract(normed_low, joined("grads"), 0, 0)
    qkv_share = lax.psum_scatter(qkv_grad, "dp", scatter_dimension=0, tiled=True)
    key_width = kv_heads * head_size
    query_share = qkv_share[:, :local_width]
    key_share = qkv_share[:, local_width : local_width + key_width]
    value_share = qkv_share[:, local_width + key_width :]

    gains = lax.psum(
        jnp.concatenate(
            [
                sum(item["attention_gain_rows"] for item in state),
                sum(item["gain_rows"] for item in state),
                query_gain_part,
                key_gain_part,
            ]
        ),
        ("dp", "tensor"),
    )

    def gain_share(first, size):
        part = size // groups
        return lax.dynamic_slice_in_dim(gains, first + group * part, part, axis=0)

    return (
        block_output,
        tokens_grad,
        gain_share(0, model_width),
        query_share,
        key_share,
        value_share,
        gain_share(2 * model_width, head_size),
        gain_share(2 * model_width + head_size, head_size),
        output_share,
        gain_share(model_width, model_width),
        gate_share,
        up_share,
        down_share,
    )


def solution(mesh):
    return jax.shard_map(
        shards,
        mesh=mesh,
        in_specs=(
            P("dp", None),
            P("dp", None),
            P("dp", None),
            P(),
            P(None, "tensor"),
            P(None, "tensor"),
            P(None, "tensor"),
            P(),
            P(),
            P("tensor", None),
            P(),
            P(None, "tensor"),
            P(None, "tensor"),
            P("tensor", None),
            P("dp", None),
        ),
        out_specs=(
            P("dp", None),
            P("dp", None),
            P("dp"),
            P("dp", "tensor"),
            P("dp", "tensor"),
            P("dp", "tensor"),
            P("dp"),
            P("dp"),
            P("tensor", "dp"),
            P("dp"),
            P("dp", "tensor"),
            P("dp", "tensor"),
            P("tensor", "dp"),
        ),
        check_vma=False,
    )
```

time: 1860 us -> 1480 us (0.80)
  waiting for transfers between devices: 1490 us -> 625 us
  starting transfers between devices: 0.41 us -> 336 us
  local copies, waits for them, and re-layouts: 19.7 us -> 91.2 us
  blocking collectives: 34.2 us -> 73.5 us
  other arithmetic: 93.2 us -> 125 us
    psum x3 -> x0, waiting for transfers between devices: 1070 us -> none  [the longest x1 496 us: shards(): feedforward_full = lax.psum(feedforward_part, 'tensor')]
    ppermute x0 -> x72, waiting for transfers between devices: none -> 397 us  [the longest x21 200 us: chain_reduce(): upward = lax.ppermute(upward, 'tensor', [(i, i + 1) for i in range(step)])]
    ppermute x0 -> x72, starting transfers between devices: none -> 336 us  [the longest x21 164 us: chain_reduce(): upward = lax.ppermute(upward, 'tensor', [(i, i + 1) for i in range(step)])]
    reduce_scatter x5 -> x2, waiting for transfers between devices: 275 us -> 0.01 us  [the longest x1 0.01 us: shards(): lax.psum_scatter(qkv_grad, 'dp', scatter_dimension=0, tiled=True)]
    all_gather x0 -> x3, waiting for transfers between devices: none -> 228 us  [the longest x2 124 us: shards(): lax.all_gather(mixed.reshape(rows, local_width), 'tensor', axis=0)]
    reduce_scatter x1, waiting for transfers between devices: 96.1 us -> 0.01 us  [shards(): lax.psum_scatter(down_grad, 'dp', scatter_dimension=1, tiled=True)]
    psum x1, blocking collectives: 9.88 us -> 73.5 us  [shards(): lax.psum(jnp.concatenate([sum((item['attention_gain_rows'] for item in st...]
    reduce_scatter x1, waiting for transfers between devices: 54.9 us -> 0.01 us  [shards(): lax.psum_scatter(output_grad, 'dp', scatter_dimension=1, tiled=True)]
  transfers between devices with their start and end apart: 10 -> 79, of which waited for: 9 -> 31; matrix products, arithmetic and copies ran while one was open for 6% -> 19% of each run, Pallas kernels for 0% -> 0%
where the time goes in v1:
time: 1480 us; the launch traced here: 1470 us
  waiting for transfers between devices  625 us (42%)
  starting transfers between devices  336 us (23%)
  matrix products  199 us (13%)
  other arithmetic  125 us (8%)
  local copies, waits for them, and re-layouts  91.2 us (6%)
  blocking collectives  73.5 us (5%)
  between operations  18 us (1%)
    ppermute x21, waiting for transfers between devices, chain_reduce(): upward = lax.ppermute(upward, 'tensor', [(i, i + 1) for i in range(step)])  200 us
    ppermute x21, starting transfers between devices, chain_reduce(): upward = lax.ppermute(upward, 'tensor', [(i, i + 1) for i in range(step)])  164 us
    all_gather x2, waiting for transfers between devices, shards(): lax.all_gather(mixed.reshape(rows, local_width), 'tensor', axis=0)  124 us
    all_gather x1, waiting for transfers between devices, shards(): lax.all_gather(own_rows, ('tensor', 'dp'), axis=0, tiled=True)  104 us
    dot_general x17, matrix products, contract(): lax.dot_general(left, right, (((left_dim,), (right_dim,)), ((), ())), pre...  104 us
    ppermute x21, waiting for transfers between devices, chain_reduce(): lax.ppermute(downward, 'tensor', [(i, i - 1) for i in range(count - step,...  84.9 us
    ppermute x12, starting transfers between devices, chain_gather(): lax.ppermute(upward, 'tensor', [(i, i + 1) for i in range(step - 1, count...  75.9 us
    ppermute x12, waiting for transfers between devices, chain_gather(): lax.ppermute(downward, 'tensor', [(i, i - 1) for i in range(1, count - st...  75.5 us
  transfers between devices with their start and end apart: 79, of which 31 were waited for; matrix products, arithmetic and copies ran while one was open for 19% of the time, Pallas kernels for 0%

profile of v1, /device:TPU:0, one launch (start us, length us, event | category | flops | bytes accessed | tf_op | source)
XLA Modules:
  0.0 1467.4 jit_solution(17214039764232434190)
XLA Ops:
  79.1 47.8 %all-gather.4.cloned.1.call-done = f32[4,512,512]{2,1,0:T(8,128)} async-done(((f32[1,512,512]{2,1,0:T(8,128)}), f32[4,512,512]{2,1,0:T(8,128)}) %all-gather.4.cloned.1.call-update) | async-done | bytes 4194320 | tf_op jit(solution)/shard_map/all_gather | solution.py:235
  132.2 76.2 %all-gather.8.cloned.1.call-done = f32[4,512,512]{2,1,0:T(8,128)} async-done(((f32[1,512,512]{2,1,0:T(8,128)}), f32[4,512,512]{2,1,0:T(8,128)}) %all-gather.8.cloned.1.call-update) | async-done | bytes 4194320 | tf_op jit(solution)/shard_map/all_gather | solution.py:235
  220.6 104.0 %all-gather.6.cloned.1.call-done = f32[2048,2048]{1,0:T(8,128)} async-done(((f32[64,2048]{1,0:T(8,128)}), f32[2048,2048]{1,0:T(8,128)}) %all-gather.6.cloned.1.call-update) | async-done | bytes 16777232 | tf_op jit(solution)/shard_map/all_gather | solution.py:184
  447.9 16.6 %collective-permute-done.33 = f32[128,2048]{1,0:T(8,128)S(1)} collective-permute-done((f32[128,2048]{1,0:T(8,128)S(1)}, f32[128,2048]{1,0:T(8,128)S(1)}, u32[]{:S(2)}, u32[]{:S(2)}) %collective-permute-start.33) | collective-permute-done | bytes 1048608 | tf_op jit(solution)/shard_map/ppermute | solution.py:132
  469.1 17.9 %collective-permute-done.12 = f32[128,2048]{1,0:T(8,128)S(1)} collective-permute-done((f32[128,2048]{1,0:T(8,128)S(1)}, f32[128,2048]{1,0:T(8,128)S(1)}, u32[]{:S(2)}, u32[]{:S(2)}) %collective-permute-start.12) | collective-permute-done | bytes 1048608 | tf_op jit(solution)/shard_map/ppermute | solution.py:132
  491.5 17.9 %collective-permute-done.25 = f32[128,2048]{1,0:T(8,128)S(1)} collective-permute-done((f32[128,2048]{1,0:T(8,128)S(1)}, f32[128,2048]{1,0:T(8,128)S(1)}, u32[]{:S(2)}, u32[]{:S(2)}) %collective-permute-start.25) | collective-permute-done | bytes 1048608 | tf_op jit(solution)/shard_map/ppermute | solution.py:132
  514.7 17.1 %collective-permute-done.1 = f32[128,2048]{1,0:T(8,128)S(1)} collective-permute-done((f32[128,2048]{1,0:T(8,128)S(1)}, f32[128,2048]{1,0:T(8,128)S(1)}, u32[]{:S(2)}, u32[]{:S(2)}) %collective-permute-start.1) | collective-permute-done | bytes 1048608 | tf_op jit(solution)/shard_map/ppermute | solution.py:132
  532.8 21.6 %collective-permute-done.34 = f32[128,2048]{1,0:T(8,128)S(1)} collective-permute-done((f32[128,2048]{1,0:T(8,128)S(1)}, f32[128,2048]{1,0:T(8,128)S(1)}, u32[]{:S(2)}, u32[]{:S(2)}) %collective-permute-start.34) | collective-permute-done | bytes 1048608 | tf_op jit(solution)/shard_map/ppermute | solution.py:132
  559.0 17.8 %collective-permute-done.13 = f32[128,2048]{1,0:T(8,128)S(1)} collective-permute-done((f32[128,2048]{1,0:T(8,128)S(1)}, f32[128,2048]{1,0:T(8,128)S(1)}, u32[]{:S(2)}, u32[]{:S(2)}) %collective-permute-start.13) | collective-permute-done | bytes 1048608 | tf_op jit(solution)/shard_map/ppermute | solution.py:132
  585.1 71.8 %collective-permute-start.35 = (f32[128,2048]{1,0:T(8,128)S(1)}, f32[128,2048]{1,0:T(8,128)S(1)}, u32[]{:S(2)}, u32[]{:S(2)}) collective-permute-start(f32[128,2048]{1,0:T(8,128)S(1)} %get-tuple-element.51), channel_id=1, source_target_pairs={{0,1},{1,2},{2,3},{4,5},{5,6},{6,7},{8,9},{9,10},{10,11},{12,13},{... | collective-permute-start | bytes 3145736 | tf_op jit(solution)/shard_map/ppermute | solution.py:132
  660.9 22.5 %collective-permute-start.14 = (f32[128,2048]{1,0:T(8,128)}, f32[128,2048]{1,0:T(8,128)}, u32[]{:S(2)}, u32[]{:S(2)}) collective-permute-start(f32[128,2048]{1,0:T(8,128)} %get-tuple-element.55), channel_id=1, source_target_pairs={{0,1},{1,2},{2,3},{4,5},{5,6},{6,7},{8,9},{9,10},{10,11},{12,13},{... | collective-permute-start | bytes 3145736 | tf_op jit(solution)/shard_map/ppermute | solution.py:132
  685.9 19.1 %collective-permute-done.38 = f32[128,2048]{1,0:T(8,128)S(1)} collective-permute-done((f32[128,2048]{1,0:T(8,128)S(1)}, f32[128,2048]{1,0:T(8,128)S(1)}, u32[]{:S(2)}, u32[]{:S(2)}) %collective-permute-start.38) | collective-permute-done | bytes 1048608 | tf_op jit(solution)/shard_map/ppermute | solution.py:133
  765.1 28.8 %collective-permute-start.30 = (f32[128,512]{1,0:T(8,128)S(1)}, f32[128,512]{1,0:T(8,128)S(1)}, u32[]{:S(2)}, u32[]{:S(2)}) collective-permute-start(f32[128,512]{1,0:T(8,128)S(1)} %get-tuple-element.99), channel_id=1, source_target_pairs={{0,3},{1,0},{2,1},{3,2},{4,7},{5,4},{6,5},{7,6},{8,11},{9,8},{10,9... | collective-permute-start | bytes 786440 | tf_op jit(solution)/shard_map/ppermute | solution.py:289
  793.9 15.7 %collective-permute-start.31 = (f32[128,512]{1,0:T(8,128)S(1)}, f32[128,512]{1,0:T(8,128)S(1)}, u32[]{:S(2)}, u32[]{:S(2)}) collective-permute-start(f32[128,512]{1,0:T(8,128)S(1)} %get-tuple-element.98), channel_id=1, source_target_pairs={{0,2},{1,3},{2,0},{3,1},{4,6},{5,7},{6,4},{7,5},{8,10},{9,11},{10,... | collective-permute-start | bytes 786440 | tf_op jit(solution)/shard_map/ppermute | solution.py:289
  828.7 15.5 %collective-permute-done.31 = f32[128,512]{1,0:T(8,128)S(1)} collective-permute-done((f32[128,512]{1,0:T(8,128)S(1)}, f32[128,512]{1,0:T(8,128)S(1)}, u32[]{:S(2)}, u32[]{:S(2)}) %collective-permute-start.31) | collective-permute-done | bytes 262176 | tf_op jit(solution)/shard_map/ppermute | solution.py:289
  898.6 22.3 %fusion.11 = f32[2048,3072]{1,0:T(8,128)} fusion(bf16[512,1536]{1,0:T(8,128)(2,1)} %get-tuple-element.67, bf16[512,1536]{1,0:T(8,128)(2,1)} %get-tuple-element.57, bf16[512,1536]{1,0:T(8,128)(2,1)} %get-tuple-element.66, bf16[512,1536]{1,0:T(8,128)(2,1)} %get-tuple-element.58, bf16[512,2048]{1,0:T(8,128)(2,1)} %copy-done.66, bf16[512,2048]{1,0:T(8,128)(2,1)} %copy-done.65), kind=kOutput, calls=%fused_computation.22 | convolution fusion | flops 12918456320 | bytes 35651584 | tf_op jit(solution)/shard_map/dot_general | solution.py:16
  973.2 18.1 %collective-permute-done.42 = f32[128,2048]{1,0:T(8,128)} collective-permute-done((f32[128,2048]{1,0:T(8,128)}, f32[128,2048]{1,0:T(8,128)}, u32[]{:S(2)}, u32[]{:S(2)}) %collective-permute-start.42) | collective-permute-done | bytes 1048608 | tf_op jit(solution)/shard_map/ppermute | solution.py:132
  1087.6 16.9 %collective-permute-done.56 = f32[128,2048]{1,0:T(8,128)S(1)} collective-permute-done((f32[128,2048]{1,0:T(8,128)S(1)}, f32[128,2048]{1,0:T(8,128)S(1)}, u32[]{:S(2)}, u32[]{:S(2)}) %collective-permute-start.56) | collective-permute-done | bytes 1048608 | tf_op jit(solution)/shard_map/ppermute | solution.py:132
  1119.3 22.4 %collective-permute-done.59 = f32[128,2048]{1,0:T(8,128)S(1)} collective-permute-done((f32[128,2048]{1,0:T(8,128)S(1)}, f32[128,2048]{1,0:T(8,128)S(1)}, u32[]{:S(2)}, u32[]{:S(2)}) %collective-permute-start.59) | collective-permute-done | bytes 1048608 | tf_op jit(solution)/shard_map/ppermute | solution.py:133
  1147.2 31.2 %collective-permute-start.60 = (f32[128,2048]{1,0:T(8,128)S(1)}, f32[128,2048]{1,0:T(8,128)S(1)}, u32[]{:S(2)}, u32[]{:S(2)}) collective-permute-start(f32[128,2048]{1,0:T(8,128)S(1)} %get-tuple-element.62), channel_id=1, source_target_pairs={{0,1},{1,2},{2,3},{4,5},{5,6},{6,7},{8,9},{9,10},{10,11},{12,13},{... | collective-permute-start | bytes 3145736 | tf_op jit(solution)/shard_map/ppermute | solution.py:118
  1182.2 27.0 %collective-permute-start.48 = (f32[128,2048]{1,0:T(8,128)S(1)}, f32[128,2048]{1,0:T(8,128)}, u32[]{:S(2)}, u32[]{:S(2)}) collective-permute-start(f32[128,2048]{1,0:T(8,128)S(1)} %get-tuple-element.61), channel_id=1, source_target_pairs={{0,1},{1,2},{2,3},{4,5},{5,6},{6,7},{8,9},{9,10},{10,11},{12,13},{... | collective-permute-start | bytes 3145736 | tf_op jit(solution)/shard_map/ppermute | solution.py:118
  1233.4 19.5 %collective-permute-done.51 = f32[128,2048]{1,0:T(8,128)} collective-permute-done((f32[128,2048]{1,0:T(8,128)S(1)}, f32[128,2048]{1,0:T(8,128)}, u32[]{:S(2)}, u32[]{:S(2)}) %collective-permute-start.51) | collective-permute-done | bytes 1048608 | tf_op jit(solution)/shard_map/ppermute | solution.py:119
  1259.5 73.5 %psum.7 = f32[4352]{0:T(1024)S(1)} all-reduce(f32[4352]{0:T(1024)S(1)} %pad_maximum_fusion.5), channel_id=1, replica_groups=mesh['dp'=8,'tensor'=4] {'dp','tensor'}, use_global_device_ids=true, to_apply=%region_32.33 | all-reduce | flops 4352 | bytes 34816 | tf_op jit(solution)/shard_map/psum | solution.py:431
  1342.4 20.0 %collective-permute-done.65 = f32[128,2048]{1,0:T(8,128)S(1)} collective-permute-done((f32[128,2048]{1,0:T(8,128)}, f32[128,2048]{1,0:T(8,128)S(1)}, u32[]{:S(2)}, u32[]{:S(2)}) %collective-permute-start.65) | collective-permute-done | bytes 1048608 | tf_op jit(solution)/shard_map/ppermute | solution.py:119
  (656 shorter events, 688.1 us)
Async XLA Ops:
  7.2 119.8 %all-gather.4.cloned.1.call-start = ((), (), s32[]{:S(2)}) async-start(), calls=%async_computation.4 | async-start | bytes 5242880 | tf_op jit(solution)/shard_map/all_gather | solution.py:235
  43.3 165.0 %all-gather.8.cloned.1.call-start = ((), (), s32[]{:S(2)}) async-start(), calls=%async_computation.6 | async-start | bytes 5242880 | tf_op jit(solution)/shard_map/all_gather | solution.py:235
  53.8 270.8 %all-gather.6.cloned.1.call-start = ((), (), s32[]{:S(2)}) async-start(), calls=%async_computation.5 | async-start | bytes 17301504 | tf_op jit(solution)/shard_map/all_gather | solution.py:184
  55.7 1334.8 %reduce-scatter.7.cloned.1.call-start = ((), (), s32[]{:S(2)}) async-start(), calls=%async_computation.8 | async-start | bytes 18874368 | tf_op jit(solution)/shard_map/reduce_scatter | solution.py:341
  430.8 78.6 %collective-permute-start.25 = (f32[128,2048]{1,0:T(8,128)S(1)}, f32[128,2048]{1,0:T(8,128)S(1)}, u32[]{:S(2)}, u32[]{:S(2)}) collective-permute-start(f32[128,2048]{1,0:T(8,128)S(1)} %dynamic-slice_add_fusion.7), channel_id=1, source_target_pairs={{0,1},{1,2},{4,5},{5,6},{8,9},{9,10},{12,13},{13,14},{16,17},{17,1... | collective-permute-start | bytes 3145736 | tf_op jit(solution)/shard_map/ppermute | solution.py:132
  443.3 88.5 %collective-permute-start.1 = (f32[128,2048]{1,0:T(8,128)S(1)}, f32[128,2048]{1,0:T(8,128)S(1)}, u32[]{:S(2)}, u32[]{:S(2)}) collective-permute-start(f32[128,2048]{1,0:T(8,128)S(1)} %dynamic-slice_add_fusion.11), channel_id=1, source_target_pairs={{0,1},{1,2},{4,5},{5,6},{8,9},{9,10},{12,13},{13,14},{16,17},{17,1... | collective-permute-start | bytes 3145736 | tf_op jit(solution)/shard_map/ppermute | solution.py:132
  464.6 89.7 %collective-permute-start.34 = (f32[128,2048]{1,0:T(8,128)S(1)}, f32[128,2048]{1,0:T(8,128)S(1)}, u32[]{:S(2)}, u32[]{:S(2)}) collective-permute-start(f32[128,2048]{1,0:T(8,128)S(1)} %dynamic-slice_add_fusion.5), channel_id=1, source_target_pairs={{0,1},{1,2},{4,5},{5,6},{8,9},{9,10},{12,13},{13,14},{16,17},{17,1... | collective-permute-start | bytes 3145736 | tf_op jit(solution)/shard_map/ppermute | solution.py:132
  487.1 89.7 %collective-permute-start.13 = (f32[128,2048]{1,0:T(8,128)S(1)}, f32[128,2048]{1,0:T(8,128)S(1)}, u32[]{:S(2)}, u32[]{:S(2)}) collective-permute-start(f32[128,2048]{1,0:T(8,128)S(1)} %dynamic-slice_add_fusion.9), channel_id=1, source_target_pairs={{0,1},{1,2},{4,5},{5,6},{8,9},{9,10},{12,13},{13,14},{16,17},{17,1... | collective-permute-start | bytes 3145736 | tf_op jit(solution)/shard_map/ppermute | solution.py:132
  509.6 69.2 %collective-permute-start.27 = (f32[128,2048]{1,0:T(8,128)S(1)}, f32[128,2048]{1,0:T(8,128)S(1)}, u32[]{:S(2)}, u32[]{:S(2)}) collective-permute-start(f32[128,2048]{1,0:T(8,128)S(1)} %get-tuple-element.43), channel_id=1, source_target_pairs={{3,2},{7,6},{11,10},{15,14},{19,18},{23,22},{27,26},{31,30}} | collective-permute-start | bytes 3145736 | tf_op jit(solution)/shard_map/ppermute | solution.py:133
  510.3 146.8 %collective-permute-start.26 = (f32[128,2048]{1,0:T(8,128)S(1)}, f32[128,2048]{1,0:T(8,128)S(1)}, u32[]{:S(2)}, u32[]{:S(2)}) collective-permute-start(f32[128,2048]{1,0:T(8,128)S(1)} %get-tuple-element.42), channel_id=1, source_target_pairs={{0,1},{1,2},{2,3},{4,5},{5,6},{6,7},{8,9},{9,10},{10,11},{12,13},{... | collective-permute-start | bytes 3145736 | tf_op jit(solution)/shard_map/ppermute | solution.py:132
  554.3 106.5 %collective-permute-start.2 = (f32[128,2048]{1,0:T(8,128)S(1)}, f32[128,2048]{1,0:T(8,128)S(1)}, u32[]{:S(2)}, u32[]{:S(2)}) collective-permute-start(f32[128,2048]{1,0:T(8,128)S(1)} %get-tuple-element.53), channel_id=1, source_target_pairs={{0,1},{1,2},{2,3},{4,5},{5,6},{6,7},{8,9},{9,10},{10,11},{12,13},{... | collective-permute-start | bytes 3145736 | tf_op jit(solution)/shard_map/ppermute | solution.py:132
  582.3 76.1 %collective-permute-start.16 = (f32[128,2048]{1,0:T(8,128)S(1)}, f32[128,2048]{1,0:T(8,128)S(1)}, u32[]{:S(2)}, u32[]{:S(2)}) collective-permute-start(f32[128,2048]{1,0:T(8,128)S(1)} %dynamic-slice_add_fusion.8), channel_id=1, source_target_pairs={{2,1},{3,2},{6,5},{7,6},{10,9},{11,10},{14,13},{15,14},{18,17},{19... | collective-permute-start | bytes 3145736 | tf_op jit(solution)/shard_map/ppermute | solution.py:133
  583.6 99.8 %collective-permute-start.29 = (f32[128,2048]{1,0:T(8,128)S(1)}, f32[128,2048]{1,0:T(8,128)S(1)}, u32[]{:S(2)}, u32[]{:S(2)}) collective-permute-start(f32[128,2048]{1,0:T(8,128)S(1)} %fusion.258), channel_id=1, source_target_pairs={{1,0},{2,1},{3,2},{5,4},{6,5},{7,6},{9,8},{10,9},{11,10},{13,12},{... | collective-permute-start | bytes 3145736 | tf_op jit(solution)/shard_map/ppermute | solution.py:133
  585.1 100.8 %collective-permute-start.35 = (f32[128,2048]{1,0:T(8,128)S(1)}, f32[128,2048]{1,0:T(8,128)S(1)}, u32[]{:S(2)}, u32[]{:S(2)}) collective-permute-start(f32[128,2048]{1,0:T(8,128)S(1)} %get-tuple-element.51), channel_id=1, source_target_pairs={{0,1},{1,2},{2,3},{4,5},{5,6},{6,7},{8,9},{9,10},{10,11},{12,13},{... | collective-permute-start | bytes 3145736 | tf_op jit(solution)/shard_map/ppermute | solution.py:132
  737.4 698.0 %reduce-scatter.5.cloned.1.call-start = ((), (), s32[]{:S(2)}) async-start(), calls=%async_computation.7 | async-start | bytes 9437184 | tf_op jit(solution)/shard_map/reduce_scatter | solution.py:425
  898.5 557.9 %reduce-scatter.9.cloned.1.call-start = ((), (), s32[]{:S(2)}) async-start(), calls=%async_computation.9 | async-start | bytes 28311552 | tf_op jit(solution)/shard_map/reduce_scatter | solution.py:330
  920.9 539.2 %reduce-scatter.11.cloned.1.call-start = ((), (), s32[]{:S(2)}) async-start(), calls=%async_computation.10 | async-start | bytes 14155776 | tf_op jit(solution)/shard_map/reduce_scatter | solution.py:323
  952.7 65.8 %collective-permute-start.19 = (f32[128,2048]{1,0:T(8,128)}, f32[128,2048]{1,0:T(8,128)}, u32[]{:S(2)}, u32[]{:S(2)}) collective-permute-start(f32[128,2048]{1,0:T(8,128)} %copy-done.44), channel_id=1, source_target_pairs={{1,2},{2,3},{5,6},{6,7},{9,10},{10,11},{13,14},{14,15},{17,18},{18... | collective-permute-start | bytes 3145736 | tf_op jit(solution)/shard_map/ppermute | solution.py:118
  968.8 64.0 %collective-permute-start.22 = (f32[128,2048]{1,0:T(8,128)}, f32[128,2048]{1,0:T(8,128)}, u32[]{:S(2)}, u32[]{:S(2)}) collective-permute-start(f32[128,2048]{1,0:T(8,128)} %collective-permute-done.21), channel_id=1, source_target_pairs={{1,0},{2,1},{5,4},{6,5},{9,8},{10,9},{13,12},{14,13},{17,16},{18,1... | collective-permute-start | bytes 3145736 | tf_op jit(solution)/shard_map/ppermute | solution.py:119
  1147.2 63.3 %collective-permute-start.60 = (f32[128,2048]{1,0:T(8,128)S(1)}, f32[128,2048]{1,0:T(8,128)S(1)}, u32[]{:S(2)}, u32[]{:S(2)}) collective-permute-start(f32[128,2048]{1,0:T(8,128)S(1)} %get-tuple-element.62), channel_id=1, source_target_pairs={{0,1},{1,2},{2,3},{4,5},{5,6},{6,7},{8,9},{9,10},{10,11},{12,13},{... | collective-permute-start | bytes 3145736 | tf_op jit(solution)/shard_map/ppermute | solution.py:118
  1230.4 103.8 %collective-permute-start.64 = (f32[128,2048]{1,0:T(8,128)}, f32[128,2048]{1,0:T(8,128)}, u32[]{:S(2)}, u32[]{:S(2)}) collective-permute-start(f32[128,2048]{1,0:T(8,128)} %collective-permute-done.63), channel_id=1, source_target_pairs={{1,0},{2,1},{5,4},{6,5},{9,8},{10,9},{13,12},{14,13},{17,16},{18,1... | collective-permute-start | bytes 3145736 | tf_op jit(solution)/shard_map/ppermute | solution.py:119
  1231.7 103.9 %collective-permute-start.49 = (f32[128,2048]{1,0:T(8,128)}, f32[128,2048]{1,0:T(8,128)}, u32[]{:S(2)}, u32[]{:S(2)}) collective-permute-start(f32[128,2048]{1,0:T(8,128)} %collective-permute-done.48), channel_id=1, source_target_pairs={{1,2},{2,3},{5,6},{6,7},{9,10},{10,11},{13,14},{14,15},{17,18},{18... | collective-permute-start | bytes 3145736 | tf_op jit(solution)/shard_map/ppermute | solution.py:118
  1252.9 83.5 %collective-permute-start.52 = (f32[128,2048]{1,0:T(8,128)}, f32[128,2048]{1,0:T(8,128)}, u32[]{:S(2)}, u32[]{:S(2)}) collective-permute-start(f32[128,2048]{1,0:T(8,128)} %collective-permute-done.51), channel_id=1, source_target_pairs={{1,0},{2,1},{5,4},{6,5},{9,8},{10,9},{13,12},{14,13},{17,16},{18,1... | collective-permute-start | bytes 3145736 | tf_op jit(solution)/shard_map/ppermute | solution.py:119
  1254.2 83.5 %collective-permute-start.62 = (f32[128,2048]{1,0:T(8,128)}, f32[128,2048]{1,0:T(8,128)}, u32[]{:S(2)}, u32[]{:S(2)}) collective-permute-start(f32[128,2048]{1,0:T(8,128)} %collective-permute-done.61), channel_id=1, source_target_pairs={{2,3},{6,7},{10,11},{14,15},{18,19},{22,23},{26,27},{30,31}} | collective-permute-start | bytes 3145736 | tf_op jit(solution)/shard_map/ppermute | solution.py:118
  (196 other events, 3509.4 us)
Sparse Core Ops, SparseCore 0:
  43.5 83.4 all-gather.3
  129.1 79.2 all-gather.7
  211.8 112.8 all-gather.5
  737.5 153.4 reduce-scatter.6
  898.6 68.6 reduce-scatter.4
  970.8 156.2 reduce-scatter.8
  1131.2 91.9 reduce-scatter.10

commit v2 on v0

v2 whole, which is shorter than its diff:
```python
import math

import jax
import jax.numpy as jnp
from jax import lax
from jax.sharding import PartitionSpec as P

SPAN = 256
HALF = 512

epsilon = 1e-06
rope_base = 1000000.0


def contract(left, right, left_dim, right_dim):
    return lax.dot_general(
        left, right, (((left_dim,), (right_dim,)), ((), ())), preferred_element_type=jnp.float32
    )


def norm_rows(values, gain):
    factor = lax.rsqrt(jnp.mean(values * values, axis=-1, keepdims=True) + epsilon)
    return (values * factor * gain, factor)


def norm_back(values, factor, gain, grad_out):
    scaled = grad_out * gain
    inner_sum = jnp.sum(scaled * values, axis=-1, keepdims=True)
    grad_in = factor * scaled - values * (factor * factor * factor) * inner_sum / values.shape[-1]
    return (grad_in, grad_out * values * factor)


def rotate_half(values, cosine, sine):
    half_size = values.shape[-1] // 2
    first_half = values[..., :half_size]
    second_half = values[..., half_size:]
    return jnp.concatenate(
        [first_half * cosine - second_half * sine, second_half * cosine + first_half * sine],
        axis=-1,
    )


def rotate_back(values, cosine, sine):
    half_size = values.shape[-1] // 2
    first_half = values[..., :half_size]
    second_half = values[..., half_size:]
    return jnp.concatenate(
        [first_half * cosine + second_half * sine, second_half * cosine - first_half * sine],
        axis=-1,
    )


def span_mask(starts, seq_length):
    token_index = jnp.arange(seq_length, dtype=jnp.int32)
    inside = (token_index[None, :] >= starts[:, None]) & (
        token_index[None, :] < starts[:, None] + SPAN
    )
    span_number = jnp.arange(starts.shape[0], dtype=jnp.int32)[:, None] + 1
    span_label = jnp.sum(inside.astype(jnp.int32) * span_number, axis=0)
    causal = token_index[:, None] >= token_index[None, :]
    same_span = (span_label[:, None] == span_label[None, :]) & (span_label[:, None] > 0)
    return causal | same_span


def score_block(query_rows, key_heads, allowed, score_scale):
    scores = (
        jnp.einsum("qhgd,khd->hgqk", query_rows, key_heads, preferred_element_type=jnp.float32)
        * score_scale
    )
    return jnp.where(allowed, scores, -jnp.inf)


def attend(query_rows, key_heads, heads_value, allowed, score_scale):
    scores = score_block(query_rows, key_heads, allowed, score_scale)
    highest = jnp.max(scores, axis=-1, keepdims=True)
    exponent = jnp.exp(scores - highest)
    denominator = jnp.sum(exponent, axis=-1, keepdims=True)
    probability = (exponent / denominator).astype(jnp.bfloat16)
    mixed_heads = jnp.einsum(
        "hgqk,khd->qhgd", probability, heads_value, preferred_element_type=jnp.float32
    )
    return (mixed_heads, (highest + jnp.log(denominator))[..., 0])


def attend_back(query_rows, key_heads, heads_value, allowed, log_total, grad_mixed, score_scale):
    scores = score_block(query_rows, key_heads, allowed, score_scale)
    probability = jnp.exp(scores - log_total[..., None])
    grad_value = jnp.einsum(
        "hgqk,qhgd->khd",
        probability.astype(jnp.bfloat16),
        grad_mixed,
        preferred_element_type=jnp.float32,
    )
    grad_prob = jnp.einsum(
        "qhgd,khd->hgqk", grad_mixed, heads_value, preferred_element_type=jnp.float32
    )
    grad_scores = probability * (
        grad_prob - jnp.sum(probability * grad_prob, axis=-1, keepdims=True)
    )
    grad_low = grad_scores.astype(jnp.bfloat16)
    grad_queries = (
        jnp.einsum("hgqk,khd->qhgd", grad_low, key_heads, preferred_element_type=jnp.float32)
        * score_scale
    )
    grad_keys = (
        jnp.einsum("hgqk,qhgd->khd", grad_low, query_rows, preferred_element_type=jnp.float32)
        * score_scale
    )
    return (grad_queries, grad_keys, grad_value)


class Line:
    def __init__(self):
        self.count = lax.axis_size("tensor")
        self.place = lax.axis_index("tensor")
        self.behind = [
            jnp.where(self.place >= slot, self.place - slot, self.place - slot + self.count)
            for slot in range(self.count)
        ]

    def ahead(self, slot):
        return self.behind[(self.count - slot) % self.count]

    def gather_step(self, pair, step):
        count = self.count
        return (
            lax.ppermute(pair[0], "tensor", [(i, i + 1) for i in range(step - 1, count - 1)]),
            lax.ppermute(pair[1], "tensor", [(i, i - 1) for i in range(1, count - step + 1)]),
        )

    def reduce_step(self, pair, step):
        count = self.count
        return (
            lax.ppermute(pair[0], "tensor", [(i, i + 1) for i in range(step)]),
            lax.ppermute(pair[1], "tensor", [(i, i - 1) for i in range(count - step, count)]),
        )

    def slots(self, pairs):
        return [pairs[0][0]] + [
            jnp.where(self.place >= slot, pairs[slot][0], pairs[self.count - slot][1])
            for slot in range(1, self.count)
        ]


class Gather:
    def __init__(self, line, block):
        self.line = line
        self.pairs = [(block, block)]

    def go(self, *after):
        step = len(self.pairs)
        if step < self.line.count:
            pair = tied(self.pairs[-1], *after)
            self.pairs.append(lax.optimization_barrier(self.line.gather_step(pair, step)))

    @property
    def last(self):
        return self.pairs[-1]

    def slots(self):
        while len(self.pairs) < self.line.count:
            self.go()
        return self.line.slots(self.pairs)


class Reduce:
    def __init__(self, line, part):
        self.line = line
        self.part = part
        self.step = 0
        self.last = None

    def go(self, *after):
        count = self.line.count
        if self.step == count - 1:
            return
        pair = (self.part(count - 1 - self.step), self.part((self.step + 1) % count))
        if after:
            pair = tied(pair, *after)
        if self.last is not None:
            pair = (self.last[0] + pair[0], self.last[1] + pair[1])
        self.step += 1
        self.last = lax.optimization_barrier(self.line.reduce_step(pair, self.step))

    def total(self, *after):
        while self.step < self.line.count - 1:
            self.go()
        pair = tied(self.last, *after)
        return self.part(0) + pair[0] + pair[1]


def row_block(values, start, rows):
    return lax.dynamic_slice_in_dim(values, start, rows, axis=0)


def tied(values, *before):
    return lax.optimization_barrier((values, before))[0]


def shards(
    tokens,
    positions,
    span_starts,
    attention_gain,
    query_weight,
    key_matrix,
    value_matrix,
    query_gain,
    key_gain,
    output_weight,
    feedforward_gain,
    gate_weight,
    up_weight,
    down_weight,
    cotangent,
):
    low = jnp.bfloat16
    line = Line()
    ranks = line.count
    place = line.place
    groups = lax.axis_size("dp")
    group = lax.axis_index("dp")
    seq_length = positions.shape[1]
    head_size = query_gain.shape[0]
    model_width, local_width = query_weight.shape
    query_heads = local_width // head_size
    kv_heads = key_matrix.shape[1] // head_size
    group_size = query_heads // kv_heads
    score_scale = head_size ** (-0.5)
    attention_gain_f = attention_gain.astype(jnp.float32)
    feedforward_gain_f = feedforward_gain.astype(jnp.float32)
    query_gain_f = query_gain.astype(jnp.float32)
    key_gain_f = key_gain.astype(jnp.float32)

    unit = jnp.where(positions[0, 0] >= 0, 1.0, 0.0)

    weight_rows = local_width // groups
    own_rows = row_block(output_weight, group * weight_rows, weight_rows).astype(jnp.float32)
    gathered_weight = lax.all_gather(lax.all_gather(own_rows, "tensor", axis=0), "dp", axis=0)

    inputs = tokens.astype(jnp.float32)
    normalized_rows, factor_one = norm_rows(inputs, attention_gain_f)
    normed_low = normalized_rows.astype(low)
    query_raw = jnp.dot(normed_low, query_weight, preferred_element_type=jnp.float32).reshape(
        seq_length, query_heads, head_size
    )
    key_unrotated = jnp.dot(normed_low, key_matrix, preferred_element_type=jnp.float32).reshape(
        seq_length, kv_heads, head_size
    )
    value_low = jnp.dot(normed_low, value_matrix, preferred_element_type=jnp.float32).astype(low)
    frequency = jnp.exp(
        jnp.arange(head_size // 2, dtype=jnp.float32) * (-2.0 * math.log(rope_base) / head_size)
    )
    angles = positions.astype(jnp.float32).reshape(seq_length)[:, None] * frequency
    cosine = jnp.cos(angles)[:, None, :]
    sine = jnp.sin(angles)[:, None, :]
    query_normed, query_factor = norm_rows(query_raw, query_gain_f)
    key_normed, key_factor = norm_rows(key_unrotated, key_gain_f)
    query_low = rotate_half(query_normed, cosine, sine).astype(low)
    key_low = rotate_half(key_normed, cosine, sine).astype(low)
    query_all = query_low.reshape(seq_length, kv_heads, group_size, head_size)
    key_all = key_low.reshape(seq_length, kv_heads, head_size)
    value_all = value_low.reshape(seq_length, kv_heads, head_size)
    mask = span_mask(span_starts[0], seq_length)

    late = slice(HALF, seq_length)
    early = slice(0, HALF)
    seen = {0: slice(0, seq_length), 1: early}
    rows_of = {0: late, 1: early}
    share_of = {0: (seq_length - HALF) // ranks, 1: HALF // ranks}

    def part_of(values, share):
        return lambda slot: row_block(values, line.ahead(slot) * share, share)

    def in_order(slots, buffer=None, first=0):
        share, width = slots[0].shape
        if buffer is None:
            buffer = jnp.zeros((share * ranks, width), low)
        for slot in range(ranks):
            buffer = lax.dynamic_update_slice_in_dim(
                buffer, (slots[slot] * unit).astype(low), first + line.behind[slot] * share, axis=0
            )
        return buffer

    def forward_half(half, query_rows):
        mixed, log_total = attend(
            query_rows,
            key_all[seen[half]],
            value_all[seen[half]],
            mask[rows_of[half], seen[half]],
            score_scale,
        )
        return mixed.reshape(-1, local_width), log_total

    mixed_0, total_0 = forward_half(0, query_all[late])
    heads_0 = Gather(line, mixed_0)
    heads_0.go()
    mixed_1, total_1 = forward_half(1, tied(query_all[early], mixed_0))
    log_total = {0: total_0, 1: total_1}
    gathered_1 = lax.all_gather(mixed_1, "tensor", axis=0)
    first_step = heads_0.last
    heads_0.go()
    grad_hidden = contract(tied(cotangent, mixed_1, first_step), down_weight, 1, 1)
    heads_0.go(grad_hidden)
    gathered_weight = tied(gathered_weight, grad_hidden)
    whole_weight = (
        jnp.concatenate(
            [
                lax.dynamic_slice_in_dim(gathered_weight, line.behind[slot], 1, axis=1).reshape(
                    local_width, model_width
                )
                for slot in range(ranks)
            ],
            axis=0,
        )
        * unit
    ).astype(low)

    def whole_heads(slots):
        return jnp.concatenate([(block * unit).astype(low) for block in slots], axis=1)

    def residual_rows(half, mixed_whole):
        residual = tokens[rows_of[half]].astype(jnp.float32) + jnp.dot(
            mixed_whole, whole_weight, preferred_element_type=jnp.float32
        )
        normed_two, factor_two = norm_rows(residual, feedforward_gain_f)
        return residual, factor_two, normed_two.astype(low)

    def gate_up(normed_two_low):
        return (
            jnp.dot(normed_two_low, gate_weight, preferred_element_type=jnp.float32),
            jnp.dot(normed_two_low, up_weight, preferred_element_type=jnp.float32),
        )

    def feed_forward(half, gate_values, up_values, between=None):
        sigmoid_gate = jax.nn.sigmoid(gate_values)
        silu_gate = gate_values * sigmoid_gate
        hidden_low = (silu_gate * up_values).astype(low)
        grad_hidden_rows = grad_hidden[rows_of[half]]
        grad_gate = (
            grad_hidden_rows * up_values * sigmoid_gate * (1.0 + gate_values * (1.0 - sigmoid_gate))
        ).astype(low)
        grad_up = (grad_hidden_rows * silu_gate).astype(low)
        if between is not None:
            grad_gate, grad_up = tied((grad_gate, grad_up), between(hidden_low))
        grad_normed_part = contract(grad_gate, gate_weight, 1, 1) + contract(
            grad_up, up_weight, 1, 1
        )
        return hidden_low, grad_gate, grad_up, grad_normed_part

    def own_rows_back(half, residual, factor_two, grad_normed_two):
        share = share_of[half]
        own_first = place * share
        own_residual = row_block(residual, own_first, share)
        grad_norm, gain_rows = norm_back(
            own_residual,
            row_block(factor_two, own_first, share),
            feedforward_gain_f,
            grad_normed_two,
        )
        grad_residual = (
            row_block(cotangent[rows_of[half]], own_first, share).astype(jnp.float32) + grad_norm
        )
        grad_residual_low = grad_residual.astype(low)
        grad_mixed_own = contract(grad_residual_low, whole_weight, 1, 1)
        return grad_residual, grad_residual_low, jnp.sum(gain_rows, axis=0), grad_mixed_own

    def swap_heads(grad_mixed_own):
        blocks = []
        for slot in range(ranks):
            first = (ranks - slot) % ranks * local_width
            piece = grad_mixed_own[:, first : first + local_width]
            if slot:
                piece = lax.ppermute(
                    piece, "tensor", [(i, (i + slot) % ranks) for i in range(ranks)]
                )
            blocks.append(piece)
        return in_order(blocks)

    mixed_whole_0 = whole_heads(tied(heads_0.slots(), whole_weight))
    residual_0, factor_0, normed_0 = residual_rows(0, mixed_whole_0)
    gate_0, up_0 = gate_up(normed_0)
    hidden_0, grad_gate_0, grad_up_0, part_0 = feed_forward(0, gate_0, up_0)
    normed_sum_0 = Reduce(line, part_of(part_0, share_of[0]))
    normed_sum_0.go()
    down_part_0 = jnp.dot(tied(hidden_0, part_0), down_weight, preferred_element_type=jnp.float32)

    gathered_1 = tied(gathered_1, down_part_0)
    mixed_whole_1 = whole_heads([row_block(gathered_1, line.behind[slot], 1)[0] for slot in range(ranks)])
    first_step = normed_sum_0.last
    normed_sum_0.go()
    residual_1, factor_1, normed_1 = residual_rows(1, tied(mixed_whole_1, first_step))
    down_sum_0 = Reduce(line, part_of(down_part_0, share_of[0]))
    down_sum_0.go(first_step, normed_1)
    gate_1, up_1 = gate_up(normed_1)
    gate_1, up_1 = tied((gate_1, up_1), normed_sum_0.last)
    normed_sum_0.go()
    down_grads = []

    def all_down_grad(hidden_1):
        hidden = jnp.concatenate([hidden_1, hidden_0], axis=0)
        down_grads.append(contract(hidden, cotangent, 0, 0))
        return down_grads[0], down_sum_0.last

    hidden_1, grad_gate_1, grad_up_1, part_1 = feed_forward(1, gate_1, up_1, all_down_grad)
    down_grad = down_grads[0]
    down_share = lax.psum_scatter(down_grad, "dp", scatter_dimension=1, tiled=True)
    down_sum_0.go(down_grad)
    normed_sum_1 = Reduce(line, part_of(part_1, share_of[1]))
    normed_sum_1.go()

    back_0 = own_rows_back(0, residual_0, factor_0, normed_sum_0.total(part_1))
    grad_mixed_0 = swap_heads(tied(back_0[3], down_sum_0.last))
    down_part_1 = jnp.dot(tied(hidden_1, back_0[3]), down_weight, preferred_element_type=jnp.float32)
    normed_two = jnp.concatenate([normed_1, normed_0], axis=0)
    grad_gate_up = jnp.concatenate(
        [
            jnp.concatenate([grad_gate_1, grad_up_1], axis=1),
            jnp.concatenate([grad_gate_0, grad_up_0], axis=1),
        ],
        axis=0,
    )
    gate_up_grad = contract(tied(normed_two, down_part_1), grad_gate_up, 0, 0)
    hidden_width = gate_weight.shape[1]
    down_sum_1 = Reduce(line, part_of(down_part_1, share_of[1]))

    def attention_core(half, grad_mixed):
        rows = rows_of[half]
        count = rows.stop - rows.start
        return attend_back(
            query_all[rows],
            key_all[seen[half]],
            value_all[seen[half]],
            mask[rows, seen[half]],
            log_total[half],
            grad_mixed.reshape(count, kv_heads, group_size, head_size),
            score_scale,
        )

    def attention_rest(half, core, extra, *before):
        rows = rows_of[half]
        count = rows.stop - rows.start
        grad_query_rot, grad_key_rot, grad_value = core
        if extra is None:
            rest = (grad_key_rot[early], grad_value[early])
            grad_key_rot = grad_key_rot[late]
            grad_value = grad_value[late]
        else:
            rest = None
            grad_key_rot = grad_key_rot + extra[0]
            grad_value = grad_value + extra[1]
        grad_query_norm = rotate_back(
            grad_query_rot.reshape(count, query_heads, head_size), cosine[rows], sine[rows]
        )
        grad_key_norm = rotate_back(
            grad_key_rot.reshape(count, kv_heads, head_size), cosine[rows], sine[rows]
        )
        grad_query_raw, query_gain_rows = norm_back(
            query_raw[rows], query_factor[rows], query_gain_f, grad_query_norm
        )
        grad_key_raw, key_gain_rows = norm_back(
            key_unrotated[rows], key_factor[rows], key_gain_f, grad_key_norm
        )
        gains = (jnp.sum(query_gain_rows, axis=(0, 1)), jnp.sum(key_gain_rows, axis=(0, 1)))
        grad_query_low = grad_query_raw.reshape(count, local_width).astype(low)
        grad_key_low = grad_key_raw.reshape(count, kv_heads * head_size).astype(low)
        grad_value_low = grad_value.reshape(count, kv_heads * head_size).astype(low)
        if before:
            grad_query_low = tied(grad_query_low, *before)
        grad_input_part = (
            contract(grad_query_low, query_weight, 1, 1)
            + contract(grad_key_low, key_matrix, 1, 1)
            + contract(grad_value_low, value_matrix, 1, 1)
        )
        grads = jnp.concatenate([grad_query_low, grad_key_low, grad_value_low], axis=1)
        return rest, gains, grads, grad_input_part

    def tokens_back(half, grad_residual, grad_normed_one):
        share = share_of[half]
        own_first = rows_of[half].start + place * share
        grad_norm, gain_rows = norm_back(
            row_block(tokens, own_first, share).astype(jnp.float32),
            row_block(factor_one, own_first, share),
            attention_gain_f,
            grad_normed_one,
        )
        return grad_residual + grad_norm, jnp.sum(gain_rows, axis=0)

    def own_block(half, residual, down_sum):
        return Gather(
            line, row_block(residual, place * share_of[half], share_of[half]) + down_sum.total()
        )

    first_step = normed_sum_1.last
    normed_sum_1.go(gate_up_grad)
    down_sum_0.go(gate_up_grad)
    core_0 = attention_core(0, tied(grad_mixed_0, gate_up_grad, first_step))
    core_0 = tied(core_0, normed_sum_1.last)
    normed_sum_1.go()
    block_0 = own_block(0, residual_0, down_sum_0)
    block_0.go(core_0)
    rest, gains_0, grads_0, input_part_0 = attention_rest(0, core_0, None)
    input_sum_0 = Reduce(line, part_of(input_part_0, share_of[0]))
    gate_up_share = lax.psum_scatter(
        tied(gate_up_grad, down_share, input_part_0), "dp", scatter_dimension=0, tiled=True
    )
    back_1 = own_rows_back(1, residual_1, factor_1, normed_sum_1.total(input_part_0))
    input_sum_0.go(block_0.last)
    grad_mixed_1 = swap_heads(tied(back_1[3], block_0.last))

    def natural(mixed_whole, half):
        own = row_block(mixed_whole, place * share_of[half], share_of[half])
        return jnp.concatenate(
            [
                lax.dynamic_slice_in_dim(
                    own,
                    jnp.where(place >= rank, place - rank, place - rank + ranks) * local_width,
                    local_width,
                    axis=1,
                )
                for rank in range(ranks)
            ],
            axis=1,
        )

    output_grad = contract(
        jnp.concatenate([natural(mixed_whole_0, 0), natural(mixed_whole_1, 1)], axis=0),
        tied(jnp.concatenate([back_0[1], back_1[1]], axis=0), back_1[3]),
        0,
        0,
    )

    first_step = input_sum_0.last
    input_sum_0.go(output_grad)
    down_sum_1.go(output_grad)
    core_1 = attention_core(1, tied(grad_mixed_1, output_grad, first_step))
    core_1 = tied(core_1, input_sum_0.last)
    input_sum_0.go()
    core_1 = tied(core_1, down_sum_1.last)
    block_0.go(core_1)
    _, gains_1, grads_1, input_part_1 = attention_rest(1, core_1, rest, block_0.last)
    input_sum_1 = Reduce(line, part_of(input_part_1, share_of[1]))
    input_sum_1.go()
    tokens_own_0, attention_gain_0 = tokens_back(0, back_0[0], input_sum_0.total(input_part_1))
    down_sum_1.go(tokens_own_0)
    qkv_grad = contract(
        tied(normed_low, input_part_1, tokens_own_0),
        jnp.concatenate([grads_1, grads_0], axis=0),
        0,
        0,
    )
    key_width = kv_heads * head_size
    output_part = lax.psum_scatter(
        tied(output_grad, gate_up_share, tokens_own_0), "dp", scatter_dimension=1, tiled=True
    )
    output_share = lax.psum_scatter(output_part, "tensor", scatter_dimension=0, tiled=True)

    tokens_0 = Gather(line, tied(tokens_own_0, input_sum_1.last))
    input_sum_1.go(qkv_grad)
    tokens_0.go(qkv_grad)
    before = (input_sum_1.last, down_sum_1.last)
    input_sum_1.go(*before)
    before = (tokens_0.last,)
    tokens_0.go(*before)
    before = (input_sum_1.last,)
    down_sum_1.go(*before)
    tokens_own_1, attention_gain_1 = tokens_back(1, back_1[0], input_sum_1.total(*before))
    tokens_1 = Gather(line, tied(tokens_own_1, tokens_0.last))
    tokens_1.go()
    block_1 = own_block(1, residual_1, down_sum_1)
    tokens_0.go(tokens_1.last, block_1.last)
    block_1.go(tokens_1.last)
    before = (block_1.last, tokens_0.last)
    tokens_1.go(*before)
    block_0.go(*before)
    before = (tokens_1.last, block_0.last)
    tokens_1.go(*before)
    block_1.go(*before)
    block_1.go()
    qkv_share = lax.psum_scatter(
        tied(qkv_grad, output_part, block_1.pairs[1]), "dp", scatter_dimension=0, tiled=True
    )

    tokens_grad = jnp.zeros((seq_length, model_width), low)
    tokens_grad = in_order(tokens_0.slots(), tokens_grad, HALF)
    tokens_grad = in_order(tokens_1.slots(), tokens_grad, 0)
    block_output = jnp.zeros((seq_length, model_width), low)
    block_output = in_order(block_0.slots(), block_output, HALF)
    block_output = in_order(block_1.slots(), block_output, 0)

    gains = lax.psum(
        jnp.concatenate(
            [
                attention_gain_0 + attention_gain_1,
                back_0[2] + back_1[2],
                gains_0[0] + gains_1[0],
                gains_0[1] + gains_1[1],
            ]
        ),
        ("dp", "tensor"),
    )

    def gain_share(first, size):
        part = size // groups
        return lax.dynamic_slice_in_dim(gains, first + group * part, part, axis=0)

    return (
        block_output,
        tokens_grad,
        gain_share(0, model_width),
        qkv_share[:, :local_width],
        qkv_share[:, local_width : local_width + key_width],
        qkv_share[:, local_width + key_width :],
        gain_share(2 * model_width, head_size),
        gain_share(2 * model_width + head_size, head_size),
        output_share,
        gain_share(model_width, model_width),
        gate_up_share[:, :hidden_width],
        gate_up_share[:, hidden_width:],
        down_share,
    )


def solution(mesh):
    return jax.shard_map(
        shards,
        mesh=mesh,
        in_specs=(
            P("dp", None),
            P("dp", None),
            P("dp", None),
            P(),
            P(None, "tensor"),
            P(None, "tensor"),
            P(None, "tensor"),
            P(),
            P(),
            P("tensor", None),
            P(),
            P(None, "tensor"),
            P(None, "tensor"),
            P("tensor", None),
            P("dp", None),
        ),
        out_specs=(
            P("dp", None),
            P("dp", None),
            P("dp"),
            P("dp", "tensor"),
            P("dp", "tensor"),
            P("dp", "tensor"),
            P("dp"),
            P("dp"),
            P("tensor", "dp"),
            P("dp"),
            P("dp", "tensor"),
            P("dp", "tensor"),
            P("tensor", "dp"),
        ),
        check_vma=False,
    )
```

time: 1860 us -> 1160 us (0.62)
  waiting for transfers between devices: 1490 us -> 452 us
  starting transfers between devices: 0.41 us -> 191 us
  local copies, waits for them, and re-layouts: 19.7 us -> 93.3 us
  other arithmetic: 93.2 us -> 152 us
  blocking collectives: 34.2 us -> 63.9 us
    psum x3 -> x0, waiting for transfers between devices: 1070 us -> none  [the longest x1 496 us: shards(): feedforward_full = lax.psum(feedforward_part, 'tensor')]
    ppermute x0 -> x72, waiting for transfers between devices: none -> 403 us  [the longest x15 221 us: gather_step(): lax.ppermute(pair[1], 'tensor', [(i, i - 1) for i in range(1, count - ste...]
    reduce_scatter x6 -> x4, waiting for transfers between devices: 330 us -> 0.01 us  [the longest x1 0.01 us: shards(): lax.psum_scatter(tied(gate_up_grad, down_share, input_part_0), 'dp', scat...]
    ppermute x0 -> x72, starting transfers between devices: none -> 190 us  [the longest x18 93.7 us: reduce_step(): lax.ppermute(pair[0], 'tensor', [(i, i + 1) for i in range(step)])]
    reduce_scatter x1, waiting for transfers between devices: 96.1 us -> 0.01 us  [shards(): lax.psum_scatter(down_grad, 'dp', scatter_dimension=1, tiled=True)]
    psum x1, blocking collectives: 9.88 us -> 63.9 us  [shards(): lax.psum(jnp.concatenate([attention_gain_0 + attention_gain_1, back_0[2]...]
    all_gather x0 -> x3, waiting for transfers between devices: none -> 49.3 us  [the longest x1 49.3 us: shards(): lax.all_gather(own_rows, 'tensor', axis=0)]
    add x2 -> x34, other arithmetic: 9.76 us -> 48.4 us  [the longest x23 40.3 us: go(): pair = (self.last[0] + pair[0], self.last[1] + pair[1])]
  transfers between devices with their start and end apart: 10 -> 80, of which waited for: 9 -> 33; matrix products, arithmetic and copies ran while one was open for 6% -> 33% of each run, Pallas kernels for 0% -> 0%
where the time goes in v2:
time: 1160 us
  waiting for transfers between devices  452 us (39%)
  starting transfers between devices  191 us (16%)
  matrix products  185 us (16%)
  other arithmetic  152 us (13%)
  local copies, waits for them, and re-layouts  93.3 us (8%)
  blocking collectives  63.9 us (6%)
  between operations  18.5 us (2%)
    ppermute x15, waiting for transfers between devices, gather_step(): lax.ppermute(pair[1], 'tensor', [(i, i - 1) for i in range(1, count - ste...  221 us
    ppermute x18, waiting for transfers between devices, reduce_step(): lax.ppermute(pair[0], 'tensor', [(i, i + 1) for i in range(step)])  119 us
    dot_general x17, matrix products, contract(): lax.dot_general(left, right, (((left_dim,), (right_dim,)), ((), ())), pre...  101 us
    ppermute x18, starting transfers between devices, reduce_step(): lax.ppermute(pair[0], 'tensor', [(i, i + 1) for i in range(step)])  93.7 us
    psum x1, blocking collectives, shards(): lax.psum(jnp.concatenate([attention_gain_0 + attention_gain_1, back_0[2]...  63.9 us
    all_gather x1, waiting for transfers between devices, shards(): lax.all_gather(own_rows, 'tensor', axis=0)  49.3 us
    ppermute x15, waiting for transfers between devices, gather_step(): lax.ppermute(pair[0], 'tensor', [(i, i + 1) for i in range(step - 1, coun...  44 us
    ppermute x15, starting transfers between devices, gather_step(): lax.ppermute(pair[0], 'tensor', [(i, i + 1) for i in range(step - 1, coun...  41.1 us
  transfers between devices with their start and end apart: 80, of which 33 were waited for; matrix products, arithmetic and copies ran while one was open for 33% of the time, Pallas kernels for 0%

profile of v2, /device:TPU:0, one launch (start us, length us, event | category | flops | bytes accessed | tf_op | source)
XLA Modules:
  0.0 1155.4 jit_solution(1205326808314836599)
XLA Ops:
  9.2 49.3 %all-gather.8.cloned.1.call-done = f32[256,2048]{1,0:T(8,128)} async-done(((f32[64,2048]{1,0:T(8,128)}), f32[256,2048]{1,0:T(8,128)}) %all-gather.8.cloned.1.call-update) | async-done | bytes 2097168 | tf_op jit(solution)/shard_map/all_gather | solution.py:239
  128.8 10.6 fusion.198
  139.3 15.4 %collective-permute-done.3 = f32[512,512]{1,0:T(8,128)} collective-permute-done((f32[512,512]{1,0:T(8,128)}, f32[512,512]{1,0:T(8,128)}, u32[]{:S(2)}, u32[]{:S(2)}) %collective-permute-start.3) | collective-permute-done | bytes 1048608 | tf_op jit(solution)/shard_map/ppermute | solution.py:128
  167.1 38.8 %collective-permute-done.5 = f32[512,512]{1,0:T(8,128)} collective-permute-done((f32[512,512]{1,0:T(8,128)}, f32[512,512]{1,0:T(8,128)}, u32[]{:S(2)}, u32[]{:S(2)}) %collective-permute-start.5) | collective-permute-done | bytes 1048608 | tf_op jit(solution)/shard_map/ppermute | solution.py:128
  346.6 16.1 %collective-permute-done.8 = f32[128,2048]{1,0:T(8,128)S(1)} collective-permute-done((f32[128,2048]{1,0:T(8,128)S(1)}, f32[128,2048]{1,0:T(8,128)S(1)}, u32[]{:S(2)}, u32[]{:S(2)}) %collective-permute-start.8) | collective-permute-done | bytes 1048608 | tf_op jit(solution)/shard_map/ppermute | solution.py:134
  423.7 20.6 %fusion.13 = f32[2048,3072]{1,0:T(8,128)} fusion(bf16[1024,2048]{1,0:T(8,128)(2,1)} %pad_maximum_fusion, bf16[512,1536]{1,0:T(8,128)(2,1)} %copy-done.181, bf16[512,1536]{1,0:T(8,128)(2,1)} %copy-done.184, bf16[512,1536]{1,0:T(8,128)(2,1)S(1)} %copy-done.109, bf16[512,1536]{1,0:T(8,128)(2,1)S(1)} %copy-done.110), kind=kOutput, calls=%fused_computation.22 | convolution fusion | flops 12910067712 | bytes 35651584 | tf_op jit(solution)/shard_map/dot_general | solution.py:16
  515.2 10.1 collective-permute-done.17
  560.0 14.4 %collective-permute-done.27 = f32[128,2048]{1,0:T(8,128)S(1)} collective-permute-done((f32[128,2048]{1,0:T(8,128)S(1)}, f32[128,2048]{1,0:T(8,128)S(1)}, u32[]{:S(2)}, u32[]{:S(2)}) %collective-permute-start.27) | collective-permute-done | bytes 1048608 | tf_op jit(solution)/shard_map/ppermute | solution.py:134
  637.7 16.2 %collective-permute-done.34 = f32[128,2048]{1,0:T(8,128)S(1)} collective-permute-done((f32[128,2048]{1,0:T(8,128)S(1)}, f32[128,2048]{1,0:T(8,128)S(1)}, u32[]{:S(2)}, u32[]{:S(2)}) %collective-permute-start.34) | collective-permute-done | bytes 1048608 | tf_op jit(solution)/shard_map/ppermute | solution.py:134
  702.5 13.6 %collective-permute-start.42 = (f32[128,2048]{1,0:T(8,128)}, f32[128,2048]{1,0:T(8,128)}, u32[]{:S(2)}, u32[]{:S(2)}) collective-permute-start(f32[128,2048]{1,0:T(8,128)} %add.626), channel_id=1, source_target_pairs={{0,1},{1,2},{4,5},{5,6},{8,9},{9,10},{12,13},{13,14},{16,17},{17,1... | collective-permute-start | bytes 3145736 | tf_op jit(solution)/shard_map/ppermute | solution.py:134
  726.1 14.9 %fusion.40 = f32[2048,1024]{1,0:T(8,128)} fusion(bf16[1024,2048]{1,0:T(8,128)(2,1)S(1)} %copy-done.58, bf16[512,256]{0,1:T(8,128)(2,1)S(1)} %bitcast.414, bf16[512,256]{0,1:T(8,128)(2,1)S(1)} %copy-done.108, bf16[512,512]{0,1:T(8,128)(2,1)S(1)} %copy-done.102, bf16[512,256]{0,1:T(8,128)(2,1)S(1)} %bitcast.412, bf16[512,256]{0,1:T(8,128)(2,1)S(1)} %get-tuple-element.421, ...), kind=kOutput, calls=%fused_computation.76 | convolution fusion | flops 4307550208 | bytes 14680064 | tf_op jit(solution)/shard_map/dot_general | solution.py:16
  741.0 20.5 %collective-permute-done.44 = f32[128,2048]{1,0:T(8,128)} collective-permute-done((f32[128,2048]{1,0:T(8,128)}, f32[128,2048]{1,0:T(8,128)}, u32[]{:S(2)}, u32[]{:S(2)}) %collective-permute-start.44) | collective-permute-done | bytes 1048608 | tf_op jit(solution)/shard_map/ppermute | solution.py:134
  777.5 9.9 collective-permute-done.46
  811.9 12.7 %collective-permute-done.48 = f32[128,2048]{1,0:T(8,128)S(1)} collective-permute-done((f32[128,2048]{1,0:T(8,128)S(1)}, f32[128,2048]{1,0:T(8,128)S(1)}, u32[]{:S(2)}, u32[]{:S(2)}) %collective-permute-start.48) | collective-permute-done | bytes 1048608 | tf_op jit(solution)/shard_map/ppermute | solution.py:134
  845.5 14.4 %collective-permute-start.56 = (f32[128,2048]{1,0:T(8,128)S(1)}, f32[128,2048]{1,0:T(8,128)S(1)}, u32[]{:S(2)}, u32[]{:S(2)}) collective-permute-start(f32[128,2048]{1,0:T(8,128)S(1)} %fusion.78), channel_id=1, source_target_pairs={{0,1},{1,2},{2,3},{4,5},{5,6},{6,7},{8,9},{9,10},{10,11},{12,13},{... | collective-permute-start | bytes 3145736 | tf_op jit(solution)/shard_map/ppermute | solution.py:127
  861.2 10.9 collective-permute-done.56
  873.0 14.4 %collective-permute-done.57 = f32[128,2048]{1,0:T(8,128)} collective-permute-done((f32[128,2048]{1,0:T(8,128)S(1)}, f32[128,2048]{1,0:T(8,128)}, u32[]{:S(2)}, u32[]{:S(2)}) %collective-permute-start.57) | collective-permute-done | bytes 1048608 | tf_op jit(solution)/shard_map/ppermute | solution.py:128
  892.9 10.0 collective-permute-done.58
  915.1 63.9 %psum.7 = f32[4352]{0:T(1024)S(1)} all-reduce(f32[4352]{0:T(1024)S(1)} %pad_maximum_fusion.9), channel_id=1, replica_groups=mesh['dp'=8,'tensor'=4] {'dp','tensor'}, use_global_device_ids=true, to_apply=%region_32.33 | all-reduce | flops 4352 | bytes 34816 | tf_op jit(solution)/shard_map/psum | solution.py:591
  991.7 17.6 %collective-permute-done.63 = f32[128,2048]{1,0:T(8,128)S(1)} collective-permute-done((f32[128,2048]{1,0:T(8,128)}, f32[128,2048]{1,0:T(8,128)S(1)}, u32[]{:S(2)}, u32[]{:S(2)}) %collective-permute-start.63) | collective-permute-done | bytes 1048608 | tf_op jit(solution)/shard_map/ppermute | solution.py:128
  1009.2 21.6 %collective-permute-done.65 = f32[128,2048]{1,0:T(8,128)} collective-permute-done((f32[128,2048]{1,0:T(8,128)}, f32[128,2048]{1,0:T(8,128)}, u32[]{:S(2)}, u32[]{:S(2)}) %collective-permute-start.65) | collective-permute-done | bytes 1048608 | tf_op jit(solution)/shard_map/ppermute | solution.py:128
  1040.4 45.1 %collective-permute-done.67 = f32[128,2048]{1,0:T(8,128)} collective-permute-done((f32[128,2048]{1,0:T(8,128)}, f32[128,2048]{1,0:T(8,128)}, u32[]{:S(2)}, u32[]{:S(2)}) %collective-permute-start.67) | collective-permute-done | bytes 1048608 | tf_op jit(solution)/shard_map/ppermute | solution.py:128
  1087.5 29.3 %collective-permute-done.71 = f32[128,2048]{1,0:T(8,128)} collective-permute-done((f32[128,2048]{1,0:T(8,128)}, f32[128,2048]{1,0:T(8,128)}, u32[]{:S(2)}, u32[]{:S(2)}) %collective-permute-start.71) | collective-permute-done | bytes 1048608 | tf_op jit(solution)/shard_map/ppermute | solution.py:128
  1123.3 14.1 %collective-permute-done.69 = f32[128,2048]{1,0:T(8,128)S(1)} collective-permute-done((f32[128,2048]{1,0:T(8,128)}, f32[128,2048]{1,0:T(8,128)S(1)}, u32[]{:S(2)}, u32[]{:S(2)}) %collective-permute-start.69) | collective-permute-done | bytes 1048608 | tf_op jit(solution)/shard_map/ppermute | solution.py:128
  (789 shorter events, 632.5 us)
Async XLA Ops:
  7.2 51.4 %all-gather.8.cloned.1.call-start = ((), (), s32[]{:S(2)}) async-start(), calls=%async_computation.11 | async-start | bytes 2621440 | tf_op jit(solution)/shard_map/all_gather | solution.py:239
  9.2 201.6 %all-gather.10.cloned.1.call-start = ((), (), s32[]{:S(2)}) async-start(), calls=%async_computation.12 | async-start | bytes 18874368 | tf_op jit(solution)/shard_map/all_gather | solution.py:239
  58.6 213.2 %all-gather.6.cloned.1.call-start = ((), (), s32[]{:S(2)}) async-start(), calls=%async_computation.5 | async-start | bytes 5242880 | tf_op jit(solution)/shard_map/all_gather | solution.py:300
  156.3 49.7 %collective-permute-start.5 = (f32[512,512]{1,0:T(8,128)}, f32[512,512]{1,0:T(8,128)}, u32[]{:S(2)}, u32[]{:S(2)}) collective-permute-start(f32[512,512]{1,0:T(8,128)} %collective-permute-done.3), channel_id=1, source_target_pairs={{1,0},{5,4},{9,8},{13,12},{17,16},{21,20},{25,24},{29,28}} | collective-permute-start | bytes 3145736 | tf_op jit(solution)/shard_map/ppermute | solution.py:128
  162.6 325.5 %reduce-scatter.6.cloned.1.call-start = ((), (), s32[]{:S(2)}) async-start(), calls=%async_computation.6 | async-start | bytes 14155776 | tf_op jit(solution)/shard_map/reduce_scatter | solution.py:407
  316.6 382.0 %reduce-scatter.8.cloned.1.call-start = ((), (), s32[]{:S(2)}) async-start(), calls=%async_computation.7 | async-start | bytes 28311552 | tf_op jit(solution)/shard_map/reduce_scatter | solution.py:504
  368.2 40.3 %collective-permute-start.14 = (f32[128,2048]{1,0:T(8,128)S(1)}, f32[128,2048]{1,0:T(8,128)S(1)}, u32[]{:S(2)}, u32[]{:S(2)}) collective-permute-start(f32[128,2048]{1,0:T(8,128)S(1)} %add.582), channel_id=1, source_target_pairs={{0,1},{1,2},{2,3},{4,5},{5,6},{6,7},{8,9},{9,10},{10,11},{12,13},{... | collective-permute-start | bytes 3145736 | tf_op jit(solution)/shard_map/ppermute | solution.py:134
  391.2 58.7 %collective-permute-start.21 = (f32[128,2048]{1,0:T(8,128)}, f32[128,2048]{1,0:T(8,128)}, u32[]{:S(2)}, u32[]{:S(2)}) collective-permute-start(f32[128,2048]{1,0:T(8,128)} %get-tuple-element.392), channel_id=1, source_target_pairs={{0,1},{4,5},{8,9},{12,13},{16,17},{20,21},{24,25},{28,29}} | collective-permute-start | bytes 3145736 | tf_op jit(solution)/shard_map/ppermute | solution.py:134
  397.2 52.7 %collective-permute-start.22 = (f32[128,2048]{1,0:T(8,128)}, f32[128,2048]{1,0:T(8,128)}, u32[]{:S(2)}, u32[]{:S(2)}) collective-permute-start(f32[128,2048]{1,0:T(8,128)} %get-tuple-element.391), channel_id=1, source_target_pairs={{3,2},{7,6},{11,10},{15,14},{19,18},{23,22},{27,26},{31,30}} | collective-permute-start | bytes 3145736 | tf_op jit(solution)/shard_map/ppermute | solution.py:135
  488.2 420.2 %reduce-scatter.10.cloned.1.call-start = ((), (), s32[]{:S(2)}) async-start(), calls=%async_computation.8 | async-start | bytes 18874368 | tf_op jit(solution)/shard_map/reduce_scatter | solution.py:553
  536.2 38.2 %collective-permute-start.27 = (f32[128,2048]{1,0:T(8,128)S(1)}, f32[128,2048]{1,0:T(8,128)S(1)}, u32[]{:S(2)}, u32[]{:S(2)}) collective-permute-start(f32[128,2048]{1,0:T(8,128)S(1)} %add.599), channel_id=1, source_target_pairs={{0,1},{1,2},{2,3},{4,5},{5,6},{6,7},{8,9},{9,10},{10,11},{12,13},{... | collective-permute-start | bytes 3145736 | tf_op jit(solution)/shard_map/ppermute | solution.py:134
  698.6 445.8 %reduce-scatter.12.cloned.1.call-start = ((), (), s32[]{:S(2)}) async-start(), calls=%async_computation.9 | async-start | bytes 9437184 | tf_op jit(solution)/shard_map/reduce_scatter | solution.py:580
  702.5 73.7 %collective-permute-start.42 = (f32[128,2048]{1,0:T(8,128)}, f32[128,2048]{1,0:T(8,128)}, u32[]{:S(2)}, u32[]{:S(2)}) collective-permute-start(f32[128,2048]{1,0:T(8,128)} %add.626), channel_id=1, source_target_pairs={{0,1},{1,2},{4,5},{5,6},{8,9},{9,10},{12,13},{13,14},{16,17},{17,1... | collective-permute-start | bytes 3145736 | tf_op jit(solution)/shard_map/ppermute | solution.py:134
  718.7 58.8 %collective-permute-start.43 = (f32[128,2048]{1,0:T(8,128)}, f32[128,2048]{1,0:T(8,128)}, u32[]{:S(2)}, u32[]{:S(2)}) collective-permute-start(f32[128,2048]{1,0:T(8,128)} %add.627), channel_id=1, source_target_pairs={{2,1},{3,2},{6,5},{7,6},{10,9},{11,10},{14,13},{15,14},{18,17},{19... | collective-permute-start | bytes 3145736 | tf_op jit(solution)/shard_map/ppermute | solution.py:135
  721.9 39.6 %collective-permute-start.44 = (f32[128,2048]{1,0:T(8,128)}, f32[128,2048]{1,0:T(8,128)}, u32[]{:S(2)}, u32[]{:S(2)}) collective-permute-start(f32[128,2048]{1,0:T(8,128)} %get-tuple-element.285), channel_id=1, source_target_pairs={{0,1},{4,5},{8,9},{12,13},{16,17},{20,21},{24,25},{28,29}} | collective-permute-start | bytes 3145736 | tf_op jit(solution)/shard_map/ppermute | solution.py:134
  769.8 40.1 %collective-permute-start.52 = (f32[128,2048]{1,0:T(8,128)S(1)}, f32[128,2048]{1,0:T(8,128)S(1)}, u32[]{:S(2)}, u32[]{:S(2)}) collective-permute-start(f32[128,2048]{1,0:T(8,128)S(1)} %copy-done.47), channel_id=1, source_target_pairs={{0,1},{1,2},{2,3},{4,5},{5,6},{6,7},{8,9},{9,10},{10,11},{12,13},{... | collective-permute-start | bytes 3145736 | tf_op jit(solution)/shard_map/ppermute | solution.py:127
  908.5 239.6 %reduce-scatter.14.cloned.1.call-start = ((), (), s32[]{:S(2)}) async-start(), calls=%async_computation.10 | async-start | bytes 2621440 | tf_op jit(solution)/shard_map/reduce_scatter | solution.py:556
  909.2 71.1 %collective-permute-start.60 = (f32[128,2048]{1,0:T(8,128)}, f32[128,2048]{1,0:T(8,128)}, u32[]{:S(2)}, u32[]{:S(2)}) collective-permute-start(f32[128,2048]{1,0:T(8,128)} %copy-done.138), channel_id=1, source_target_pairs={{2,3},{6,7},{10,11},{14,15},{18,19},{22,23},{26,27},{30,31}} | collective-permute-start | bytes 3145736 | tf_op jit(solution)/shard_map/ppermute | solution.py:127
  910.8 69.4 %collective-permute-start.61 = (f32[128,2048]{1,0:T(8,128)}, f32[128,2048]{1,0:T(8,128)}, u32[]{:S(2)}, u32[]{:S(2)}) collective-permute-start(f32[128,2048]{1,0:T(8,128)} %copy-done.139), channel_id=1, source_target_pairs={{1,0},{5,4},{9,8},{13,12},{17,16},{21,20},{25,24},{29,28}} | collective-permute-start | bytes 3145736 | tf_op jit(solution)/shard_map/ppermute | solution.py:128
  984.1 46.7 %collective-permute-start.65 = (f32[128,2048]{1,0:T(8,128)}, f32[128,2048]{1,0:T(8,128)}, u32[]{:S(2)}, u32[]{:S(2)}) collective-permute-start(f32[128,2048]{1,0:T(8,128)} %collective-permute-done.57), channel_id=1, source_target_pairs={{1,0},{2,1},{5,4},{6,5},{9,8},{10,9},{13,12},{14,13},{17,16},{18,1... | collective-permute-start | bytes 3145736 | tf_op jit(solution)/shard_map/ppermute | solution.py:128
  1032.4 53.0 %collective-permute-start.67 = (f32[128,2048]{1,0:T(8,128)}, f32[128,2048]{1,0:T(8,128)}, u32[]{:S(2)}, u32[]{:S(2)}) collective-permute-start(f32[128,2048]{1,0:T(8,128)} %collective-permute-done.59), channel_id=1, source_target_pairs={{1,0},{2,1},{5,4},{6,5},{9,8},{10,9},{13,12},{14,13},{17,16},{18,1... | collective-permute-start | bytes 3145736 | tf_op jit(solution)/shard_map/ppermute | solution.py:128
  1033.7 53.8 %collective-permute-start.70 = (f32[128,2048]{1,0:T(8,128)}, f32[128,2048]{1,0:T(8,128)}, u32[]{:S(2)}, u32[]{:S(2)}) collective-permute-start(f32[128,2048]{1,0:T(8,128)} %collective-permute-done.64), channel_id=1, source_target_pairs={{2,3},{6,7},{10,11},{14,15},{18,19},{22,23},{26,27},{30,31}} | collective-permute-start | bytes 3145736 | tf_op jit(solution)/shard_map/ppermute | solution.py:127
  1035.4 81.4 %collective-permute-start.71 = (f32[128,2048]{1,0:T(8,128)}, f32[128,2048]{1,0:T(8,128)}, u32[]{:S(2)}, u32[]{:S(2)}) collective-permute-start(f32[128,2048]{1,0:T(8,128)} %collective-permute-done.65), channel_id=1, source_target_pairs={{1,0},{5,4},{9,8},{13,12},{17,16},{21,20},{25,24},{29,28}} | collective-permute-start | bytes 3145736 | tf_op jit(solution)/shard_map/ppermute | solution.py:128
  1086.2 51.1 %collective-permute-start.69 = (f32[128,2048]{1,0:T(8,128)}, f32[128,2048]{1,0:T(8,128)S(1)}, u32[]{:S(2)}, u32[]{:S(2)}) collective-permute-start(f32[128,2048]{1,0:T(8,128)} %collective-permute-done.67), channel_id=1, source_target_pairs={{1,0},{5,4},{9,8},{13,12},{17,16},{21,20},{25,24},{29,28}} | collective-permute-start | bytes 3145736 | tf_op jit(solution)/shard_map/ppermute | solution.py:128
  (262 other events, 4350.2 us)
Sparse Core Ops, SparseCore 0:
  10.1 48.3 all-gather.7
  60.4 88.5 all-gather.9
  162.8 86.4 all-gather.5
  316.7 95.2 reduce-scatter.5
  488.3 157.2 reduce-scatter.7
  698.7 125.4 reduce-scatter.9
  908.6 91.5 reduce-scatter.11
  1039.6 61.8 reduce-scatter.13

commit v3 on v2

--- a/solution.py
+++ b/solution.py
@@ -143,15 +143,18 @@
 
 
 class Gather:
-    def __init__(self, line, block):
+    def __init__(self, line, block, name):
         self.line = line
+        self.name = name
         self.pairs = [(block, block)]
 
     def go(self, *after):
         step = len(self.pairs)
         if step < self.line.count:
             pair = tied(self.pairs[-1], *after)
-            self.pairs.append(lax.optimization_barrier(self.line.gather_step(pair, step)))
+            with jax.named_scope(f"{self.name}_gather_{step}"):
+                moved = self.line.gather_step(pair, step)
+            self.pairs.append(lax.optimization_barrier(moved))
 
     @property
     def last(self):
@@ -164,11 +167,13 @@
 
 
 class Reduce:
-    def __init__(self, line, part):
+    def __init__(self, line, part, name):
         self.line = line
+        self.name = name
         self.part = part
         self.step = 0
         self.last = None
+        self.sent = None
 
     def go(self, *after):
         count = self.line.count
@@ -180,7 +185,10 @@
         if self.last is not None:
             pair = (self.last[0] + pair[0], self.last[1] + pair[1])
         self.step += 1
-        self.last = lax.optimization_barrier(self.line.reduce_step(pair, self.step))
+        self.sent = pair = lax.optimization_barrier(pair)
+        with jax.named_scope(f"{self.name}_sum_{self.step}"):
+            moved = self.line.reduce_step(pair, self.step)
+        self.last = lax.optimization_barrier(moved)
 
     def total(self, *after):
         while self.step < self.line.count - 1:
@@ -236,7 +244,7 @@
 
     weight_rows = local_width // groups
     own_rows = row_block(output_weight, group * weight_rows, weight_rows).astype(jnp.float32)
-    gathered_weight = lax.all_gather(lax.all_gather(own_rows, "tensor", axis=0), "dp", axis=0)
+    weight_by_rank = lax.all_gather(own_rows, "tensor", axis=0)
 
     inputs = tokens.astype(jnp.float32)
     normalized_rows, factor_one = norm_rows(inputs, attention_gain_f)
@@ -293,28 +301,31 @@
         return mixed.reshape(-1, local_width), log_total
 
     mixed_0, total_0 = forward_half(0, query_all[late])
-    heads_0 = Gather(line, mixed_0)
+    heads_0 = Gather(line, mixed_0, "heads_0")
     heads_0.go()
     mixed_1, total_1 = forward_half(1, tied(query_all[early], mixed_0))
     log_total = {0: total_0, 1: total_1}
-    gathered_1 = lax.all_gather(mixed_1, "tensor", axis=0)
+    heads_1 = Gather(line, mixed_1, "heads_1")
+    other_rows = jnp.concatenate(
+        [row_block(tied(weight_by_rank, mixed_1), line.behind[slot], 1) for slot in range(1, ranks)]
+    )
+    gathered_weight = lax.all_gather(other_rows, "dp", axis=0)
     first_step = heads_0.last
     heads_0.go()
     grad_hidden = contract(tied(cotangent, mixed_1, first_step), down_weight, 1, 1)
+    second_step = heads_0.last
     heads_0.go(grad_hidden)
     gathered_weight = tied(gathered_weight, grad_hidden)
-    whole_weight = (
-        jnp.concatenate(
-            [
-                lax.dynamic_slice_in_dim(gathered_weight, line.behind[slot], 1, axis=1).reshape(
-                    local_width, model_width
-                )
-                for slot in range(ranks)
-            ],
-            axis=0,
-        )
-        * unit
-    ).astype(low)
+    whole_weight = jnp.concatenate(
+        [output_weight]
+        + [
+            (gathered_weight[:, slot - 1].reshape(local_width, model_width) * unit).astype(low)
+            for slot in range(1, ranks)
+        ],
+        axis=0,
+    )
+    heads_1.go(second_step, whole_weight)
+    heads_1.go(heads_0.last)
 
     def whole_heads(slots):
         return jnp.concatenate([(block * unit).astype(low) for block in slots], axis=1)
@@ -365,7 +376,7 @@
         grad_mixed_own = contract(grad_residual_low, whole_weight, 1, 1)
         return grad_residual, grad_residual_low, jnp.sum(gain_rows, axis=0), grad_mixed_own
 
-    def swap_heads(grad_mixed_own):
+    def swap_heads(grad_mixed_own, *before):
         blocks = []
         for slot in range(ranks):
             first = (ranks - slot) % ranks * local_width
@@ -375,43 +386,44 @@
                     piece, "tensor", [(i, (i + slot) % ranks) for i in range(ranks)]
                 )
             blocks.append(piece)
-        return in_order(blocks)
+        return in_order(tied(blocks, *before))
 
     mixed_whole_0 = whole_heads(tied(heads_0.slots(), whole_weight))
     residual_0, factor_0, normed_0 = residual_rows(0, mixed_whole_0)
     gate_0, up_0 = gate_up(normed_0)
+    heads_1.go(gate_0)
     hidden_0, grad_gate_0, grad_up_0, part_0 = feed_forward(0, gate_0, up_0)
-    normed_sum_0 = Reduce(line, part_of(part_0, share_of[0]))
+    normed_sum_0 = Reduce(line, part_of(part_0, share_of[0]), "normed_0")
     normed_sum_0.go()
     down_part_0 = jnp.dot(tied(hidden_0, part_0), down_weight, preferred_element_type=jnp.float32)
 
-    gathered_1 = tied(gathered_1, down_part_0)
-    mixed_whole_1 = whole_heads([row_block(gathered_1, line.behind[slot], 1)[0] for slot in range(ranks)])
-    first_step = normed_sum_0.last
+    mixed_whole_1 = whole_heads(tied(heads_1.slots(), down_part_0))
+    normed_sum_0.go(down_part_0)
+    mixed_whole_1 = tied(mixed_whole_1, normed_sum_0.last)
     normed_sum_0.go()
-    residual_1, factor_1, normed_1 = residual_rows(1, tied(mixed_whole_1, first_step))
-    down_sum_0 = Reduce(line, part_of(down_part_0, share_of[0]))
-    down_sum_0.go(first_step, normed_1)
+    residual_1, factor_1, normed_1 = residual_rows(1, tied(mixed_whole_1, normed_sum_0.sent))
     gate_1, up_1 = gate_up(normed_1)
-    gate_1, up_1 = tied((gate_1, up_1), normed_sum_0.last)
-    normed_sum_0.go()
-    down_grads = []
-
-    def all_down_grad(hidden_1):
+    down_sum_0 = Reduce(line, part_of(down_part_0, share_of[0]), "down_0")
+    stages = []
+
+    def late_sums(hidden_1):
         hidden = jnp.concatenate([hidden_1, hidden_0], axis=0)
-        down_grads.append(contract(hidden, cotangent, 0, 0))
-        return down_grads[0], down_sum_0.last
-
-    hidden_1, grad_gate_1, grad_up_1, part_1 = feed_forward(1, gate_1, up_1, all_down_grad)
-    down_grad = down_grads[0]
-    down_share = lax.psum_scatter(down_grad, "dp", scatter_dimension=1, tiled=True)
-    down_sum_0.go(down_grad)
-    normed_sum_1 = Reduce(line, part_of(part_1, share_of[1]))
-    normed_sum_1.go()
-
-    back_0 = own_rows_back(0, residual_0, factor_0, normed_sum_0.total(part_1))
-    grad_mixed_0 = swap_heads(tied(back_0[3], down_sum_0.last))
-    down_part_1 = jnp.dot(tied(hidden_1, back_0[3]), down_weight, preferred_element_type=jnp.float32)
+        down_grad = contract(hidden, cotangent, 0, 0)
+        down_sum_0.go(normed_sum_0.last)
+        back = own_rows_back(0, residual_0, factor_0, normed_sum_0.total(down_sum_0.sent))
+        stages.extend([down_grad, back])
+        return down_grad, back[3], down_sum_0.last
+
+    hidden_1, grad_gate_1, grad_up_1, part_1 = feed_forward(1, gate_1, up_1, late_sums)
+    down_grad, back_0 = stages
+    down_share = lax.psum_scatter(
+        tied(down_grad, down_sum_0.last), "dp", scatter_dimension=1, tiled=True
+    )
+    down_sum_0.go()
+    normed_sum_1 = Reduce(line, part_of(part_1, share_of[1]), "normed_1")
+    down_part_1 = jnp.dot(tied(hidden_1, part_1), down_weight, preferred_element_type=jnp.float32)
+    grad_mixed_0 = swap_heads(back_0[3], down_part_1)
+    down_sum_0.go(grad_mixed_0)
     normed_two = jnp.concatenate([normed_1, normed_0], axis=0)
     grad_gate_up = jnp.concatenate(
         [
@@ -420,9 +432,9 @@
         ],
         axis=0,
     )
-    gate_up_grad = contract(tied(normed_two, down_part_1), grad_gate_up, 0, 0)
+    gate_up_grad = contract(tied(normed_two, down_sum_0.sent), grad_gate_up, 0, 0)
     hidden_width = gate_weight.shape[1]
-    down_sum_1 = Reduce(line, part_of(down_part_1, share_of[1]))
+    down_sum_1 = Reduce(line, part_of(down_part_1, share_of[1]), "down_1")
 
     def attention_core(half, grad_mixed):
         rows = rows_of[half]
@@ -488,25 +500,32 @@
 
     def own_block(half, residual, down_sum):
         return Gather(
-            line, row_block(residual, place * share_of[half], share_of[half]) + down_sum.total()
-        )
-
-    first_step = normed_sum_1.last
-    normed_sum_1.go(gate_up_grad)
-    down_sum_0.go(gate_up_grad)
-    core_0 = attention_core(0, tied(grad_mixed_0, gate_up_grad, first_step))
-    core_0 = tied(core_0, normed_sum_1.last)
-    normed_sum_1.go()
+            line,
+            row_block(residual, place * share_of[half], share_of[half]) + down_sum.total(),
+            f"block_{half}",
+        )
+
     block_0 = own_block(0, residual_0, down_sum_0)
-    block_0.go(core_0)
-    rest, gains_0, grads_0, input_part_0 = attention_rest(0, core_0, None)
-    input_sum_0 = Reduce(line, part_of(input_part_0, share_of[0]))
+    block_0.go()
     gate_up_share = lax.psum_scatter(
-        tied(gate_up_grad, down_share, input_part_0), "dp", scatter_dimension=0, tiled=True
-    )
-    back_1 = own_rows_back(1, residual_1, factor_1, normed_sum_1.total(input_part_0))
-    input_sum_0.go(block_0.last)
-    grad_mixed_1 = swap_heads(tied(back_1[3], block_0.last))
+        tied(gate_up_grad, down_share, block_0.last), "dp", scatter_dimension=0, tiled=True
+    )
+    before = (block_0.last,)
+    normed_sum_1.go(*before)
+    block_0.go(*before)
+    core_0 = attention_core(0, tied(grad_mixed_0, gate_up_grad, normed_sum_1.sent))
+    before = (normed_sum_1.last, block_0.last)
+    normed_sum_1.go(*before)
+    block_0.go(*before)
+    rest, gains_0, grads_0, input_part_0 = attention_rest(
+        0, tied(core_0, normed_sum_1.sent), None
+    )
+    input_sum_0 = Reduce(line, part_of(input_part_0, share_of[0]), "input_0")
+    before = (normed_sum_1.last, block_0.last)
+    normed_sum_1.go(*before)
+    back_1 = own_rows_back(1, residual_1, factor_1, normed_sum_1.total())
+    grad_mixed_1 = swap_heads(back_1[3])
+    input_sum_0.go(back_1[3])
 
     def natural(mixed_whole, half):
         own = row_block(mixed_whole, place * share_of[half], share_of[half])
@@ -530,75 +549,90 @@
         0,
     )
 
-    first_step = input_sum_0.last
-    input_sum_0.go(output_grad)
-    down_sum_1.go(output_grad)
-    core_1 = attention_core(1, tied(grad_mixed_1, output_grad, first_step))
-    core_1 = tied(core_1, input_sum_0.last)
-    input_sum_0.go()
-    core_1 = tied(core_1, down_sum_1.last)
-    block_0.go(core_1)
-    _, gains_1, grads_1, input_part_1 = attention_rest(1, core_1, rest, block_0.last)
-    input_sum_1 = Reduce(line, part_of(input_part_1, share_of[1]))
-    input_sum_1.go()
-    tokens_own_0, attention_gain_0 = tokens_back(0, back_0[0], input_sum_0.total(input_part_1))
-    down_sum_1.go(tokens_own_0)
+    output_part = lax.psum_scatter(
+        tied(output_grad, gate_up_share, input_sum_0.last, grad_mixed_1),
+        "dp",
+        scatter_dimension=1,
+        tiled=True,
+    )
+    input_sum_0.go(grad_mixed_1)
+    core_1 = attention_core(1, tied(grad_mixed_1, input_sum_0.sent))
+    _, gains_1, grads_1, input_part_1 = attention_rest(1, core_1, rest)
+    input_sum_1 = Reduce(line, part_of(input_part_1, share_of[1]), "input_1")
+    tokens_own_0, attention_gain_0 = tokens_back(0, back_0[0], input_sum_0.total())
+    tokens_0 = Gather(line, tokens_own_0, "tokens_0")
+    tokens_0.go()
     qkv_grad = contract(
-        tied(normed_low, input_part_1, tokens_own_0),
+        tied(normed_low, tokens_own_0),
         jnp.concatenate([grads_1, grads_0], axis=0),
         0,
         0,
     )
     key_width = kv_heads * head_size
-    output_part = lax.psum_scatter(
-        tied(output_grad, gate_up_share, tokens_own_0), "dp", scatter_dimension=1, tiled=True
-    )
-    output_share = lax.psum_scatter(output_part, "tensor", scatter_dimension=0, tiled=True)
-
-    tokens_0 = Gather(line, tied(tokens_own_0, input_sum_1.last))
-    input_sum_1.go(qkv_grad)
-    tokens_0.go(qkv_grad)
-    before = (input_sum_1.last, down_sum_1.last)
+
+    before = (tokens_0.last,)
+    down_sum_1.go(*before)
+    tokens_0.go(*before)
+    before = (tokens_0.last, down_sum_1.last)
+    down_sum_1.go(*before)
+    tokens_0.go(*before)
+    before = (tokens_0.last, down_sum_1.last)
+    down_sum_1.go(*before)
+    qkv_share = lax.psum_scatter(
+        tied(qkv_grad, output_part, down_sum_1.last), "dp", scatter_dimension=0, tiled=True
+    )
+    block_1 = own_block(1, residual_1, down_sum_1)
+    block_1.go()
+    before = (block_1.last,)
     input_sum_1.go(*before)
-    before = (tokens_0.last,)
-    tokens_0.go(*before)
-    before = (input_sum_1.last,)
-    down_sum_1.go(*before)
-    tokens_own_1, attention_gain_1 = tokens_back(1, back_1[0], input_sum_1.total(*before))
-    tokens_1 = Gather(line, tied(tokens_own_1, tokens_0.last))
-    tokens_1.go()
-    block_1 = own_block(1, residual_1, down_sum_1)
-    tokens_0.go(tokens_1.last, block_1.last)
-    block_1.go(tokens_1.last)
-    before = (block_1.last, tokens_0.last)
-    tokens_1.go(*before)
-    block_0.go(*before)
-    before = (tokens_1.last, block_0.last)
-    tokens_1.go(*before)
     block_1.go(*before)
-    block_1.go()
-    qkv_share = lax.psum_scatter(
-        tied(qkv_grad, output_part, block_1.pairs[1]), "dp", scatter_dimension=0, tiled=True
-    )
+    before = (input_sum_1.last, block_1.last)
+    input_sum_1.go(*before)
+    block_1.go(*before)
+    before = (input_sum_1.last, block_1.last)
+    input_sum_1.go(*before)
+    tokens_own_1, attention_gain_1 = tokens_back(1, back_1[0], input_sum_1.total())
+    tokens_1 = Gather(line, tokens_own_1, "tokens_1")
+    gains = jnp.concatenate(
+        [
+            attention_gain_0 + attention_gain_1,
+            back_0[2] + back_1[2],
+            gains_0[0] + gains_1[0],
+            gains_0[1] + gains_1[1],
+        ]
+    )
+
+    exchanges = [("dp", groups, 1 << bit) for bit in range((groups - 1).bit_length())]
+    exchanges += [("tensor", ranks, 1 << bit) for bit in range((ranks - 1).bit_length())]
+    output_sum = Reduce(line, part_of(output_part, local_width), "output")
+    while len(tokens_1.pairs) < ranks or exchanges:
+        tokens_1.go()
+        if len(tokens_1.pairs) > 2:
+            output_sum.go(tokens_1.pairs[-2])
+            tokens_1.pairs[-1], output_sum.last = lax.optimization_barrier(
+                (tokens_1.last, output_sum.last)
+            )
+        for axis, size, distance in exchanges[:2]:
+            gains = gains + lax.ppermute(gains, axis, [(i, i ^ distance) for i in range(size)])
+        exchanges = exchanges[2:]
+        tokens_1.pairs[-1], gains = lax.optimization_barrier((tokens_1.last, gains))
 
     tokens_grad = jnp.zeros((seq_length, model_width), low)
     tokens_grad = in_order(tokens_0.slots(), tokens_grad, HALF)
-    tokens_grad = in_order(tokens_1.slots(), tokens_grad, 0)
     block_output = jnp.zeros((seq_length, model_width), low)
     block_output = in_order(block_0.slots(), block_output, HALF)
     block_output = in_order(block_1.slots(), block_output, 0)
-
-    gains = lax.psum(
-        jnp.concatenate(
-            [
-                attention_gain_0 + attention_gain_1,
-                back_0[2] + back_1[2],
-                gains_0[0] + gains_1[0],
-                gains_0[1] + gains_1[1],
-            ]
-        ),
-        ("dp", "tensor"),
-    )
+    shares = (
+        qkv_share[:, :local_width],
+        qkv_share[:, local_width : local_width + key_width],
+        qkv_share[:, local_width + key_width :],
+        gate_up_share[:, :hidden_width],
+        gate_up_share[:, hidden_width:],
+    )
+    output_sum.go()
+    output_share = output_sum.total(shares, block_output)
+    last_slots = tokens_1.slots()
+    tokens_grad = in_order(last_slots, tokens_grad, 0)
 
     def gain_share(first, size):
         part = size // groups
@@ -608,15 +642,15 @@
         block_output,
         tokens_grad,
         gain_share(0, model_width),
-        qkv_share[:, :local_width],
-        qkv_share[:, local_width : local_width + key_width],
-        qkv_share[:, local_width + key_width :],
+        shares[0],
+        shares[1],
+        shares[2],
         gain_share(2 * model_width, head_size),
         gain_share(2 * model_width + head_size, head_size),
         output_share,
         gain_share(model_width, model_width),
-        gate_up_share[:, :hidden_width],
-        gate_up_share[:, hidden_width:],
+        shares[3],
+        shares[4],
         down_share,
     )
 

time: 1160 us -> 1010 us (0.87); the launches traced: 1160 us -> 993 us
  waiting for transfers between devices: 452 us -> 382 us
  blocking collectives: 63.9 us -> 0 us
  local copies, waits for them, and re-layouts: 93.3 us -> 73.3 us
    ppermute x15 -> x18, waiting for transfers between devices: 221 us -> 106 us  [gather_step(): lax.ppermute(pair[1], 'tensor', [(i, i - 1) for i in range(1, count - ste...]
    psum x1 -> x0, blocking collectives: 63.9 us -> none  [shards(): lax.psum(jnp.concatenate([attention_gain_0 + attention_gain_1, back_0[2]...]
    all_gather x3 -> x2, waiting for transfers between devices: 49.3 us -> 2.21 us  [the longest x1 2.21 us: shards(): weight_by_rank = lax.all_gather(own_rows, 'tensor', axis=0)]
    ppermute x18 -> x21, waiting for transfers between devices: 119 us -> 162 us  [reduce_step(): lax.ppermute(pair[0], 'tensor', [(i, i + 1) for i in range(step)])]
    ppermute x0 -> x5, waiting for transfers between devices: none -> 16 us  [shards(): lax.ppermute(gains, axis, [(i, i ^ distance) for i in range(size)])]
    ppermute x18 -> x21, waiting for transfers between devices: 18.9 us -> 32.6 us  [reduce_step(): lax.ppermute(pair[1], 'tensor', [(i, i - 1) for i in range(count - step,...]
    ppermute x15 -> x18, waiting for transfers between devices: 44 us -> 53.3 us  [gather_step(): lax.ppermute(pair[0], 'tensor', [(i, i + 1) for i in range(step - 1, coun...]
    unnamed x410 -> x398, local copies, waits for them, and re-layouts: 26.3 us -> 17.8 us
  transfers between devices with their start and end apart: 80 -> 95, of which waited for: 33 -> 50; matrix products, arithmetic and copies ran while one was open for 33% -> 38% of each run, Pallas kernels for 0% -> 0%
where the time goes in v3:
time: 1010 us; the launch traced here: 993 us
  waiting for transfers between devices  382 us (38%)
  matrix products  188 us (19%)
  starting transfers between devices  184 us (18%)
  other arithmetic  146 us (14%)
  local copies, waits for them, and re-layouts  73.3 us (7%)
  between operations  18.6 us (2%)
    ppermute x21, waiting for transfers between devices, reduce_step(): lax.ppermute(pair[0], 'tensor', [(i, i + 1) for i in range(step)])  162 us
    ppermute x18, waiting for transfers between devices, gather_step(): lax.ppermute(pair[1], 'tensor', [(i, i - 1) for i in range(1, count - ste...  106 us
    dot_general x17, matrix products, contract(): lax.dot_general(left, right, (((left_dim,), (right_dim,)), ((), ())), pre...  102 us
    ppermute x21, starting transfers between devices, reduce_step(): lax.ppermute(pair[0], 'tensor', [(i, i + 1) for i in range(step)])  88.9 us
    ppermute x18, waiting for transfers between devices, gather_step(): lax.ppermute(pair[0], 'tensor', [(i, i + 1) for i in range(step - 1, coun...  53.3 us
    dynamic_update_slice x23, other arithmetic, in_order(): lax.dynamic_update_slice_in_dim(buffer, (slots[slot] * unit).astype(low),...  36.3 us
    add x27, other arithmetic, go(): pair = (self.last[0] + pair[0], self.last[1] + pair[1])  33.8 us
    ppermute x18, starting transfers between devices, gather_step(): lax.ppermute(pair[0], 'tensor', [(i, i + 1) for i in range(step - 1, coun...  33.2 us
  transfers between devices with their start and end apart: 95, of which 50 were waited for; matrix products, arithmetic and copies ran while one was open for 38% of the time, Pallas kernels for 0%

profile of v3, /device:TPU:0, one launch (start us, length us, event | category | flops | bytes accessed | tf_op | source)
XLA Modules:
  0.0 992.7 jit_solution(17545009772921246197)
XLA Ops:
  65.6 21.1 %collective-permute-done = f32[512,512]{0,1:T(8,128)S(1)} collective-permute-done((f32[512,512]{0,1:T(8,128)S(1)}, f32[512,512]{0,1:T(8,128)S(1)}, u32[]{:S(2)}, u32[]{:S(2)}) %collective-permute-start) | collective-permute-done | bytes 1048608 | tf_op jit(solution)/shard_map/heads_0_gather_1/ppermute | solution.py:127
  93.8 12.4 %fusion.202 = f32[1024,1536]{1,0:T(8,128)} fusion(bf16[1024,2048]{1,0:T(8,128)(2,1)} %param.29, bf16[1536,2048]{1,0:T(8,128)(2,1)} %param.28), kind=kOutput, calls=%fused_computation.402 | convolution fusion | flops 6442450944 | bytes 16777216 | tf_op jit(solution)/shard_map/dot_general | solution.py:16
  106.2 14.5 %collective-permute-done.3 = f32[512,512]{0,1:T(8,128)} collective-permute-done((f32[512,512]{0,1:T(8,128)S(1)}, f32[512,512]{0,1:T(8,128)}, u32[]{:S(2)}, u32[]{:S(2)}) %collective-permute-start.3) | collective-permute-done | bytes 1048608 | tf_op jit(solution)/shard_map/heads_0_gather_2/ppermute | solution.py:128
  127.0 20.5 %collective-permute-done.5 = f32[512,512]{0,1:T(8,128)} collective-permute-done((f32[512,512]{0,1:T(8,128)}, f32[512,512]{0,1:T(8,128)}, u32[]{:S(2)}, u32[]{:S(2)}) %collective-permute-start.5) | collective-permute-done | bytes 1048608 | tf_op jit(solution)/shard_map/heads_0_gather_3/ppermute | solution.py:128
  216.8 10.1 %collective-permute-done.6 = f32[128,2048]{1,0:T(8,128)S(1)} collective-permute-done((f32[128,2048]{1,0:T(8,128)S(1)}, f32[128,2048]{1,0:T(8,128)S(1)}, u32[]{:S(2)}, u32[]{:S(2)}) %collective-permute-start.6) | collective-permute-done | bytes 1048608 | tf_op jit(solution)/shard_map/normed_0_sum_1/ppermute | solution.py:134
  235.9 14.0 %collective-permute-done.8 = f32[128,2048]{1,0:T(8,128)S(1)} collective-permute-done((f32[128,2048]{1,0:T(8,128)S(1)}, f32[128,2048]{1,0:T(8,128)S(1)}, u32[]{:S(2)}, u32[]{:S(2)}) %collective-permute-start.8) | collective-permute-done | bytes 1048608 | tf_op jit(solution)/shard_map/normed_0_sum_2/ppermute | solution.py:134
  261.1 15.3 %collective-permute-done.10 = f32[128,2048]{1,0:T(8,128)S(1)} collective-permute-done((f32[128,2048]{1,0:T(8,128)S(1)}, f32[128,2048]{1,0:T(8,128)S(1)}, u32[]{:S(2)}, u32[]{:S(2)}) %collective-permute-start.10) | collective-permute-done | bytes 1048608 | tf_op jit(solution)/shard_map/normed_0_sum_3/ppermute | solution.py:134
  305.4 9.3 fusion.32
  367.6 9.2 collective-permute-start.25
  383.0 14.2 %collective-permute-done.25 = f32[128,2048]{1,0:T(8,128)} collective-permute-done((f32[128,2048]{1,0:T(8,128)}, f32[128,2048]{1,0:T(8,128)}, u32[]{:S(2)}, u32[]{:S(2)}) %collective-permute-start.25) | collective-permute-done | bytes 1048608 | tf_op jit(solution)/shard_map/down_0_sum_3/ppermute | solution.py:134
  414.5 21.0 %fusion.12 = f32[2048,3072]{1,0:T(8,128)} fusion(bf16[1024,2048]{1,0:T(8,128)(2,1)S(1)} %copy-done.44, bf16[512,1536]{1,0:T(8,128)(2,1)} %copy-done.177, bf16[512,1536]{1,0:T(8,128)(2,1)} %copy-done.183, bf16[512,1536]{1,0:T(8,128)(2,1)} %get-tuple-element.325, bf16[512,1536]{1,0:T(8,128)(2,1)} %get-tuple-element.324), kind=kOutput, calls=%fused_computation.21 | convolution fusion | flops 12910067712 | bytes 35651584 | tf_op jit(solution)/shard_map/dot_general | solution.py:16
  480.9 9.5 collective-permute-done.30
  501.8 11.8 %collective-permute-done.35 = f32[128,2048]{1,0:T(8,128)S(1)} collective-permute-done((f32[128,2048]{1,0:T(8,128)S(1)}, f32[128,2048]{1,0:T(8,128)S(1)}, u32[]{:S(2)}, u32[]{:S(2)}) %collective-permute-start.35) | collective-permute-done | bytes 1048608 | tf_op jit(solution)/shard_map/normed_1_sum_2/ppermute | solution.py:134
  531.1 9.6 collective-permute-done.37
  648.2 10.4 %collective-permute-done.46 = f32[128,2048]{1,0:T(8,128)} collective-permute-done((f32[128,2048]{1,0:T(8,128)}, f32[128,2048]{1,0:T(8,128)}, u32[]{:S(2)}, u32[]{:S(2)}) %collective-permute-start.46) | collective-permute-done | bytes 1048608 | tf_op jit(solution)/shard_map/input_0_sum_3/ppermute | solution.py:134
  679.4 14.0 %collective-permute-done.48 = f32[128,2048]{1,0:T(8,128)S(1)} collective-permute-done((f32[128,2048]{1,0:T(8,128)S(1)}, f32[128,2048]{1,0:T(8,128)S(1)}, u32[]{:S(2)}, u32[]{:S(2)}) %collective-permute-start.48) | collective-permute-done | bytes 1048608 | tf_op jit(solution)/shard_map/tokens_0_gather_1/ppermute | solution.py:127
  705.6 13.4 %collective-permute-done.50 = f32[128,2048]{1,0:T(8,128)S(1)} collective-permute-done((f32[128,2048]{1,0:T(8,128)S(1)}, f32[128,2048]{1,0:T(8,128)S(1)}, u32[]{:S(2)}, u32[]{:S(2)}) %collective-permute-start.50) | collective-permute-done | bytes 1048608 | tf_op jit(solution)/shard_map/down_1_sum_1/ppermute | solution.py:134
  737.1 15.0 %fusion.39 = f32[2048,1024]{1,0:T(8,128)} fusion(bf16[1024,2048]{1,0:T(8,128)(2,1)S(1)} %copy-done.41, bf16[512,256]{0,1:T(8,128)(2,1)S(1)} %bitcast.410, bf16[512,256]{0,1:T(8,128)(2,1)S(1)} %copy-done.89, bf16[512,512]{0,1:T(8,128)(2,1)S(1)} %copy-done.81, bf16[512,256]{0,1:T(8,128)(2,1)S(1)} %bitcast.422, bf16[512,256]{0,1:T(8,128)(2,1)S(1)} %get-tuple-element.596, ...), kind=kOutput, calls=%fused_computation.78 | convolution fusion | flops 4307550208 | bytes 14680064 | tf_op jit(solution)/shard_map/dot_general | solution.py:16
  772.5 10.3 %collective-permute-done.58 = f32[128,2048]{1,0:T(8,128)} collective-permute-done((f32[128,2048]{1,0:T(8,128)}, f32[128,2048]{1,0:T(8,128)}, u32[]{:S(2)}, u32[]{:S(2)}) %collective-permute-start.58) | collective-permute-done | bytes 1048608 | tf_op jit(solution)/shard_map/down_1_sum_3/ppermute | solution.py:134
  796.7 13.2 %collective-permute-done.60 = f32[128,2048]{1,0:T(8,128)S(1)} collective-permute-done((f32[128,2048]{1,0:T(8,128)S(1)}, f32[128,2048]{1,0:T(8,128)S(1)}, u32[]{:S(2)}, u32[]{:S(2)}) %collective-permute-start.60) | collective-permute-done | bytes 1048608 | tf_op jit(solution)/shard_map/block_1_gather_1/ppermute | solution.py:127
  823.0 13.6 %collective-permute-done.63 = f32[128,2048]{1,0:T(8,128)S(1)} collective-permute-done((f32[128,2048]{1,0:T(8,128)S(1)}, f32[128,2048]{1,0:T(8,128)S(1)}, u32[]{:S(2)}, u32[]{:S(2)}) %collective-permute-start.63) | collective-permute-done | bytes 1048608 | tf_op jit(solution)/shard_map/block_1_gather_2/ppermute | solution.py:128
  848.0 13.6 %collective-permute-done.68 = f32[128,2048]{1,0:T(8,128)S(1)} collective-permute-done((f32[128,2048]{1,0:T(8,128)S(1)}, f32[128,2048]{1,0:T(8,128)S(1)}, u32[]{:S(2)}, u32[]{:S(2)}) %collective-permute-start.68) | collective-permute-done | bytes 1048608 | tf_op jit(solution)/shard_map/input_1_sum_2/ppermute | solution.py:134
  929.9 12.2 %collective-permute-done.81 = f32[4352]{0:T(1024)S(1)} collective-permute-done((f32[4352]{0:T(1024)S(1)}, f32[4352]{0:T(1024)S(1)}, u32[]{:S(2)}, u32[]{:S(2)}) %collective-permute-start.81) | collective-permute-done | bytes 17440 | tf_op jit(solution)/shard_map/ppermute | solution.py:616
  952.5 9.3 collective-permute-done.84
  (809 shorter events, 656.7 us)
Async XLA Ops:
  7.2 51.4 %all-gather.5.cloned.1.call-start = ((), (), s32[]{:S(2)}) async-start(), calls=%async_computation.8 | async-start | bytes 2621440 | tf_op jit(solution)/shard_map/all_gather | solution.py:247
  9.2 141.9 %all-gather.7.cloned.1.call-start = ((), (), s32[]{:S(2)}) async-start(), calls=%async_computation.9 | async-start | bytes 14155776 | tf_op jit(solution)/shard_map/all_gather | solution.py:312
  61.3 376.3 %reduce-scatter.5.cloned.1.call-start = ((), (), s32[]{:S(2)}) async-start(), calls=%async_computation.4 | async-start | bytes 14155776 | tf_op jit(solution)/shard_map/reduce_scatter | solution.py:419
  64.3 26.5 %collective-permute-start.1 = (f32[512,512]{0,1:T(8,128)S(1)}, f32[512,512]{0,1:T(8,128)S(1)}, u32[]{:S(2)}, u32[]{:S(2)}) collective-permute-start(f32[512,512]{0,1:T(8,128)S(1)} %bitcast.420), channel_id=1, source_target_pairs={{1,0},{2,1},{3,2},{5,4},{6,5},{7,6},{9,8},{10,9},{11,10},{13,12},{... | collective-permute-start | bytes 3145736 | tf_op jit(solution)/shard_map/heads_0_gather_1/ppermute | solution.py:128
  92.5 28.2 %collective-permute-start.3 = (f32[512,512]{0,1:T(8,128)S(1)}, f32[512,512]{0,1:T(8,128)}, u32[]{:S(2)}, u32[]{:S(2)}) collective-permute-start(f32[512,512]{0,1:T(8,128)S(1)} %collective-permute-done.1), channel_id=1, source_target_pairs={{1,0},{2,1},{5,4},{6,5},{9,8},{10,9},{13,12},{14,13},{17,16},{18,1... | collective-permute-start | bytes 3145736 | tf_op jit(solution)/shard_map/heads_0_gather_2/ppermute | solution.py:128
  160.2 48.4 %collective-permute-start.19 = (f32[512,512]{0,1:T(8,128)S(1)}, f32[512,512]{0,1:T(8,128)S(1)}, u32[]{:S(2)}, u32[]{:S(2)}) collective-permute-start(f32[512,512]{0,1:T(8,128)S(1)} %bitcast.416), channel_id=1, source_target_pairs={{0,1},{1,2},{2,3},{4,5},{5,6},{6,7},{8,9},{9,10},{10,11},{12,13},{... | collective-permute-start | bytes 3145736 | tf_op jit(solution)/shard_map/heads_1_gather_1/ppermute | solution.py:127
  162.1 46.5 %collective-permute-start.20 = (f32[512,512]{0,1:T(8,128)S(1)}, f32[512,512]{0,1:T(8,128)S(1)}, u32[]{:S(2)}, u32[]{:S(2)}) collective-permute-start(f32[512,512]{0,1:T(8,128)S(1)} %bitcast.417), channel_id=1, source_target_pairs={{1,0},{2,1},{3,2},{5,4},{6,5},{7,6},{9,8},{10,9},{11,10},{13,12},{... | collective-permute-start | bytes 3145736 | tf_op jit(solution)/shard_map/heads_1_gather_1/ppermute | solution.py:128
  232.7 27.2 %collective-permute-start.23 = (f32[512,512]{0,1:T(8,128)S(1)}, f32[512,512]{0,1:T(8,128)S(1)}, u32[]{:S(2)}, u32[]{:S(2)}) collective-permute-start(f32[512,512]{0,1:T(8,128)S(1)} %collective-permute-done.21), channel_id=1, source_target_pairs={{2,3},{6,7},{10,11},{14,15},{18,19},{22,23},{26,27},{30,31}} | collective-permute-start | bytes 3145736 | tf_op jit(solution)/shard_map/heads_1_gather_3/ppermute | solution.py:127
  280.5 34.2 %collective-permute-start.12 = (f32[128,2048]{1,0:T(8,128)S(1)}, f32[128,2048]{1,0:T(8,128)}, u32[]{:S(2)}, u32[]{:S(2)}) collective-permute-start(f32[128,2048]{1,0:T(8,128)S(1)} %get-tuple-element.333), channel_id=1, source_target_pairs={{0,1},{4,5},{8,9},{12,13},{16,17},{20,21},{24,25},{28,29}} | collective-permute-start | bytes 3145736 | tf_op jit(solution)/shard_map/down_0_sum_1/ppermute | solution.py:134
  283.9 30.8 %collective-permute-start.13 = (f32[128,2048]{1,0:T(8,128)}, f32[128,2048]{1,0:T(8,128)}, u32[]{:S(2)}, u32[]{:S(2)}) collective-permute-start(f32[128,2048]{1,0:T(8,128)} %get-tuple-element.331), channel_id=1, source_target_pairs={{3,2},{7,6},{11,10},{15,14},{19,18},{23,22},{27,26},{31,30}} | collective-permute-start | bytes 3145736 | tf_op jit(solution)/shard_map/down_0_sum_1/ppermute | solution.py:135
  314.8 278.2 %reduce-scatter.7.cloned.1.call-start = ((), (), s32[]{:S(2)}) async-start(), calls=%async_computation.5 | async-start | bytes 28311552 | tf_op jit(solution)/shard_map/reduce_scatter | solution.py:510
  327.5 29.3 %collective-permute-start.18 = (f32[128,512]{1,0:T(8,128)S(1)}, f32[128,512]{1,0:T(8,128)S(1)}, u32[]{:S(2)}, u32[]{:S(2)}) collective-permute-start(f32[128,512]{1,0:T(8,128)S(1)} %get-tuple-element.611), channel_id=1, source_target_pairs={{0,3},{1,0},{2,1},{3,2},{4,7},{5,4},{6,5},{7,6},{8,11},{9,8},{10,9... | collective-permute-start | bytes 786440 | tf_op jit(solution)/shard_map/ppermute | solution.py:385
  327.5 29.3 %collective-permute-start.17 = (f32[128,512]{1,0:T(8,128)S(1)}, f32[128,512]{1,0:T(8,128)S(1)}, u32[]{:S(2)}, u32[]{:S(2)}) collective-permute-start(f32[128,512]{1,0:T(8,128)S(1)} %get-tuple-element.612), channel_id=1, source_target_pairs={{0,2},{1,3},{2,0},{3,1},{4,6},{5,7},{6,4},{7,5},{8,10},{9,11},{10,... | collective-permute-start | bytes 786440 | tf_op jit(solution)/shard_map/ppermute | solution.py:385
  327.6 29.2 %collective-permute-start.16 = (f32[128,512]{1,0:T(8,128)S(1)}, f32[128,512]{1,0:T(8,128)S(1)}, u32[]{:S(2)}, u32[]{:S(2)}) collective-permute-start(f32[128,512]{1,0:T(8,128)S(1)} %get-tuple-element.613), channel_id=1, source_target_pairs={{0,1},{1,2},{2,3},{3,0},{4,5},{5,6},{6,7},{7,4},{8,9},{9,10},{10,1... | collective-permute-start | bytes 786440 | tf_op jit(solution)/shard_map/ppermute | solution.py:385
  333.6 28.5 %collective-permute-start.14 = (f32[128,2048]{1,0:T(8,128)}, f32[128,2048]{1,0:T(8,128)}, u32[]{:S(2)}, u32[]{:S(2)}) collective-permute-start(f32[128,2048]{1,0:T(8,128)} %get-tuple-element.301), channel_id=1, source_target_pairs={{0,1},{1,2},{4,5},{5,6},{8,9},{9,10},{12,13},{13,14},{16,17},{17,1... | collective-permute-start | bytes 3145736 | tf_op jit(solution)/shard_map/down_0_sum_2/ppermute | solution.py:134
  367.6 29.6 %collective-permute-start.25 = (f32[128,2048]{1,0:T(8,128)}, f32[128,2048]{1,0:T(8,128)}, u32[]{:S(2)}, u32[]{:S(2)}) collective-permute-start(f32[128,2048]{1,0:T(8,128)} %add.617), channel_id=1, source_target_pairs={{0,1},{1,2},{2,3},{4,5},{5,6},{6,7},{8,9},{9,10},{10,11},{12,13},{... | collective-permute-start | bytes 3145736 | tf_op jit(solution)/shard_map/down_0_sum_3/ppermute | solution.py:134
  408.5 27.0 %collective-permute-start.27 = (f32[128,2048]{1,0:T(8,128)}, f32[128,2048]{1,0:T(8,128)}, u32[]{:S(2)}, u32[]{:S(2)}) collective-permute-start(f32[128,2048]{1,0:T(8,128)} %get-tuple-element.339), channel_id=1, source_target_pairs={{0,1},{1,2},{2,3},{4,5},{5,6},{6,7},{8,9},{9,10},{10,11},{12,13},{... | collective-permute-start | bytes 3145736 | tf_op jit(solution)/shard_map/block_0_gather_1/ppermute | solution.py:127
  437.7 329.5 %reduce-scatter.9.cloned.1.call-start = ((), (), s32[]{:S(2)}) async-start(), calls=%async_computation.6 | async-start | bytes 18874368 | tf_op jit(solution)/shard_map/reduce_scatter | solution.py:552
  459.3 31.2 %collective-permute-start.31 = (f32[128,2048]{1,0:T(8,128)S(1)}, f32[128,2048]{1,0:T(8,128)}, u32[]{:S(2)}, u32[]{:S(2)}) collective-permute-start(f32[128,2048]{1,0:T(8,128)S(1)} %get-tuple-element.368), channel_id=1, source_target_pairs={{0,1},{4,5},{8,9},{12,13},{16,17},{20,21},{24,25},{28,29}} | collective-permute-start | bytes 3145736 | tf_op jit(solution)/shard_map/normed_1_sum_1/ppermute | solution.py:134
  463.0 27.4 %collective-permute-start.32 = (f32[128,2048]{1,0:T(8,128)}, f32[128,2048]{1,0:T(8,128)}, u32[]{:S(2)}, u32[]{:S(2)}) collective-permute-start(f32[128,2048]{1,0:T(8,128)} %get-tuple-element.367), channel_id=1, source_target_pairs={{3,2},{7,6},{11,10},{15,14},{19,18},{23,22},{27,26},{31,30}} | collective-permute-start | bytes 3145736 | tf_op jit(solution)/shard_map/normed_1_sum_1/ppermute | solution.py:135
  557.3 31.0 %collective-permute-start.39 = (f32[128,2048]{1,0:T(8,128)}, f32[128,2048]{1,0:T(8,128)}, u32[]{:S(2)}, u32[]{:S(2)}) collective-permute-start(f32[128,2048]{1,0:T(8,128)} %get-tuple-element.375), channel_id=1, source_target_pairs={{0,1},{4,5},{8,9},{12,13},{16,17},{20,21},{24,25},{28,29}} | collective-permute-start | bytes 3145736 | tf_op jit(solution)/shard_map/input_0_sum_1/ppermute | solution.py:134
  560.5 27.8 %collective-permute-start.40 = (f32[128,2048]{1,0:T(8,128)}, f32[128,2048]{1,0:T(8,128)}, u32[]{:S(2)}, u32[]{:S(2)}) collective-permute-start(f32[128,2048]{1,0:T(8,128)} %get-tuple-element.376), channel_id=1, source_target_pairs={{3,2},{7,6},{11,10},{15,14},{19,18},{23,22},{27,26},{31,30}} | collective-permute-start | bytes 3145736 | tf_op jit(solution)/shard_map/input_0_sum_1/ppermute | solution.py:135
  593.0 387.1 %reduce-scatter.11.cloned.1.call-start = ((), (), s32[]{:S(2)}) async-start(), calls=%async_computation.7 | async-start | bytes 9437184 | tf_op jit(solution)/shard_map/reduce_scatter | solution.py:581
  629.7 28.8 %collective-permute-start.46 = (f32[128,2048]{1,0:T(8,128)}, f32[128,2048]{1,0:T(8,128)}, u32[]{:S(2)}, u32[]{:S(2)}) collective-permute-start(f32[128,2048]{1,0:T(8,128)} %add.641), channel_id=1, source_target_pairs={{0,1},{1,2},{2,3},{4,5},{5,6},{6,7},{8,9},{9,10},{10,11},{12,13},{... | collective-permute-start | bytes 3145736 | tf_op jit(solution)/shard_map/input_0_sum_3/ppermute | solution.py:134
  (270 other events, 4130.5 us)
Sparse Core Ops, SparseCore 0:
  10.2 48.3 all-gather.4
  61.4 72.6 all-gather.6
  314.9 90.0 reduce-scatter.4
  437.8 155.0 reduce-scatter.6
  596.3 115.9 reduce-scatter.8
  767.4 70.8 reduce-scatter.10

commit v4 on v3

--- a/solution.py
+++ b/solution.py
@@ -325,7 +325,6 @@
         axis=0,
     )
     heads_1.go(second_step, whole_weight)
-    heads_1.go(heads_0.last)
 
     def whole_heads(slots):
         return jnp.concatenate([(block * unit).astype(low) for block in slots], axis=1)
@@ -391,17 +390,19 @@
     mixed_whole_0 = whole_heads(tied(heads_0.slots(), whole_weight))
     residual_0, factor_0, normed_0 = residual_rows(0, mixed_whole_0)
     gate_0, up_0 = gate_up(normed_0)
+    gate_0, up_0 = tied((gate_0, up_0), heads_1.last)
     heads_1.go(gate_0)
     hidden_0, grad_gate_0, grad_up_0, part_0 = feed_forward(0, gate_0, up_0)
     normed_sum_0 = Reduce(line, part_of(part_0, share_of[0]), "normed_0")
     normed_sum_0.go()
-    down_part_0 = jnp.dot(tied(hidden_0, part_0), down_weight, preferred_element_type=jnp.float32)
+    first_step = heads_1.last
+    heads_1.go(part_0)
+    down_part_0 = jnp.dot(tied(hidden_0, part_0, first_step), down_weight, preferred_element_type=jnp.float32)
 
     mixed_whole_1 = whole_heads(tied(heads_1.slots(), down_part_0))
     normed_sum_0.go(down_part_0)
-    mixed_whole_1 = tied(mixed_whole_1, normed_sum_0.last)
-    normed_sum_0.go()
     residual_1, factor_1, normed_1 = residual_rows(1, tied(mixed_whole_1, normed_sum_0.sent))
+    normed_sum_0.go(residual_1)
     gate_1, up_1 = gate_up(normed_1)
     down_sum_0 = Reduce(line, part_of(down_part_0, share_of[0]), "down_0")
     stages = []
@@ -409,7 +410,7 @@
     def late_sums(hidden_1):
         hidden = jnp.concatenate([hidden_1, hidden_0], axis=0)
         down_grad = contract(hidden, cotangent, 0, 0)
-        down_sum_0.go(normed_sum_0.last)
+        down_sum_0.go(normed_sum_0.last, gate_1)
         back = own_rows_back(0, residual_0, factor_0, normed_sum_0.total(down_sum_0.sent))
         stages.extend([down_grad, back])
         return down_grad, back[3], down_sum_0.last
@@ -419,7 +420,7 @@
     down_share = lax.psum_scatter(
         tied(down_grad, down_sum_0.last), "dp", scatter_dimension=1, tiled=True
     )
-    down_sum_0.go()
+    down_sum_0.go(back_0[3])
     normed_sum_1 = Reduce(line, part_of(part_1, share_of[1]), "normed_1")
     down_part_1 = jnp.dot(tied(hidden_1, part_1), down_weight, preferred_element_type=jnp.float32)
     grad_mixed_0 = swap_heads(back_0[3], down_part_1)
@@ -506,7 +507,7 @@
         )
 
     block_0 = own_block(0, residual_0, down_sum_0)
-    block_0.go()
+    block_0.go(gate_up_grad)
     gate_up_share = lax.psum_scatter(
         tied(gate_up_grad, down_share, block_0.last), "dp", scatter_dimension=0, tiled=True
     )
@@ -549,17 +550,17 @@
         0,
     )
 
-    output_part = lax.psum_scatter(
-        tied(output_grad, gate_up_share, input_sum_0.last, grad_mixed_1),
-        "dp",
-        scatter_dimension=1,
-        tiled=True,
-    )
     input_sum_0.go(grad_mixed_1)
     core_1 = attention_core(1, tied(grad_mixed_1, input_sum_0.sent))
     _, gains_1, grads_1, input_part_1 = attention_rest(1, core_1, rest)
     input_sum_1 = Reduce(line, part_of(input_part_1, share_of[1]), "input_1")
     tokens_own_0, attention_gain_0 = tokens_back(0, back_0[0], input_sum_0.total())
+    output_part = lax.psum_scatter(
+        tied(output_grad, gate_up_share, tokens_own_0),
+        "dp",
+        scatter_dimension=1,
+        tiled=True,
+    )
     tokens_0 = Gather(line, tokens_own_0, "tokens_0")
     tokens_0.go()
     qkv_grad = contract(
@@ -578,11 +579,11 @@
     tokens_0.go(*before)
     before = (tokens_0.last, down_sum_1.last)
     down_sum_1.go(*before)
-    qkv_share = lax.psum_scatter(
-        tied(qkv_grad, output_part, down_sum_1.last), "dp", scatter_dimension=0, tiled=True
-    )
     block_1 = own_block(1, residual_1, down_sum_1)
     block_1.go()
+    qkv_share = lax.psum_scatter(
+        tied(qkv_grad, output_part, block_1.last), "dp", scatter_dimension=0, tiled=True
+    )
     before = (block_1.last,)
     input_sum_1.go(*before)
     block_1.go(*before)

time: 1010 us -> 995 us (0.985)
  waiting for transfers between devices: 382 us -> 370 us
    ppermute x21, waiting for transfers between devices: 162 us -> 138 us  [reduce_step(): lax.ppermute(pair[0], 'tensor', [(i, i + 1) for i in range(step)])]
    ppermute x18, waiting for transfers between devices: 106 us -> 120 us  [gather_step(): lax.ppermute(pair[1], 'tensor', [(i, i - 1) for i in range(1, count - ste...]
    add x27 -> x28, other arithmetic: 33.8 us -> 26.5 us  [go(): pair = (self.last[0] + pair[0], self.last[1] + pair[1])]
  transfers between devices with their start and end apart: 95 -> 95, of which waited for: 50 -> 49; matrix products, arithmetic and copies ran while one was open for 38% -> 37% of each run, Pallas kernels for 0% -> 0%
where the time goes in v4:
time: 995 us; the launch traced here: 982 us
  waiting for transfers between devices  370 us (37%)
  matrix products  196 us (20%)
  starting transfers between devices  194 us (19%)
  other arithmetic  140 us (14%)
  local copies, waits for them, and re-layouts  64.4 us (6%)
  between operations  18.6 us (2%)
    ppermute x21, waiting for transfers between devices, reduce_step(): lax.ppermute(pair[0], 'tensor', [(i, i + 1) for i in range(step)])  138 us
    ppermute x18, waiting for transfers between devices, gather_step(): lax.ppermute(pair[1], 'tensor', [(i, i - 1) for i in range(1, count - ste...  120 us
    dot_general x17, matrix products, contract(): lax.dot_general(left, right, (((left_dim,), (right_dim,)), ((), ())), pre...  108 us
    ppermute x21, starting transfers between devices, reduce_step(): lax.ppermute(pair[0], 'tensor', [(i, i + 1) for i in range(step)])  89.1 us
    ppermute x18, waiting for transfers between devices, gather_step(): lax.ppermute(pair[0], 'tensor', [(i, i + 1) for i in range(step - 1, coun...  52.7 us
    ppermute x18, starting transfers between devices, gather_step(): lax.ppermute(pair[0], 'tensor', [(i, i + 1) for i in range(step - 1, coun...  36.7 us
    dynamic_update_slice x23, other arithmetic, in_order(): lax.dynamic_update_slice_in_dim(buffer, (slots[slot] * unit).astype(low),...  33.4 us
    add x28, other arithmetic, go(): pair = (self.last[0] + pair[0], self.last[1] + pair[1])  26.5 us
  transfers between devices with their start and end apart: 95, of which 49 were waited for; matrix products, arithmetic and copies ran while one was open for 37% of the time, Pallas kernels for 0%

profile of v4, /device:TPU:0, one launch (start us, length us, event | category | flops | bytes accessed | tf_op | source)
XLA Modules:
  0.0 982.3 jit_solution(17777493607544494257)
XLA Ops:
  65.5 21.1 %collective-permute-done = f32[512,512]{0,1:T(8,128)S(1)} collective-permute-done((f32[512,512]{0,1:T(8,128)S(1)}, f32[512,512]{0,1:T(8,128)S(1)}, u32[]{:S(2)}, u32[]{:S(2)}) %collective-permute-start) | collective-permute-done | bytes 1048608 | tf_op jit(solution)/shard_map/heads_0_gather_1/ppermute | solution.py:127
  93.7 12.5 %fusion.202 = f32[1024,1536]{1,0:T(8,128)} fusion(bf16[1024,2048]{1,0:T(8,128)(2,1)} %param.29, bf16[1536,2048]{1,0:T(8,128)(2,1)} %param.28), kind=kOutput, calls=%fused_computation.401 | convolution fusion | flops 6442450944 | bytes 16777216 | tf_op jit(solution)/shard_map/dot_general | solution.py:16
  106.2 14.4 %collective-permute-done.3 = f32[512,512]{0,1:T(8,128)} collective-permute-done((f32[512,512]{0,1:T(8,128)S(1)}, f32[512,512]{0,1:T(8,128)}, u32[]{:S(2)}, u32[]{:S(2)}) %collective-permute-start.3) | collective-permute-done | bytes 1048608 | tf_op jit(solution)/shard_map/heads_0_gather_2/ppermute | solution.py:128
  127.1 20.3 %collective-permute-done.5 = f32[512,512]{0,1:T(8,128)} collective-permute-done((f32[512,512]{0,1:T(8,128)}, f32[512,512]{0,1:T(8,128)}, u32[]{:S(2)}, u32[]{:S(2)}) %collective-permute-start.5) | collective-permute-done | bytes 1048608 | tf_op jit(solution)/shard_map/heads_0_gather_3/ppermute | solution.py:128
  213.8 14.2 %collective-permute-done.10 = f32[128,2048]{1,0:T(8,128)S(1)} collective-permute-done((f32[128,2048]{1,0:T(8,128)S(1)}, f32[128,2048]{1,0:T(8,128)S(1)}, u32[]{:S(2)}, u32[]{:S(2)}) %collective-permute-start.10) | collective-permute-done | bytes 1048608 | tf_op jit(solution)/shard_map/normed_0_sum_1/ppermute | solution.py:134
  245.0 10.6 %collective-permute-done.12 = f32[128,2048]{1,0:T(8,128)S(1)} collective-permute-done((f32[128,2048]{1,0:T(8,128)S(1)}, f32[128,2048]{1,0:T(8,128)S(1)}, u32[]{:S(2)}, u32[]{:S(2)}) %collective-permute-start.12) | collective-permute-done | bytes 1048608 | tf_op jit(solution)/shard_map/normed_0_sum_2/ppermute | solution.py:134
  261.2 8.9 collective-permute-start.16
  271.8 8.9 fusion.208
  295.7 9.4 fusion.32
  365.3 9.6 collective-permute-start.25
  376.4 27.4 %fusion.12 = f32[2048,3072]{1,0:T(8,128)} fusion(bf16[1024,2048]{1,0:T(8,128)(2,1)} %pad_maximum_fusion.1, bf16[512,1536]{1,0:T(8,128)(2,1)S(1)} %copy-done.92, bf16[512,1536]{1,0:T(8,128)(2,1)S(1)} %copy-done.94, bf16[512,1536]{1,0:T(8,128)(2,1)} %get-tuple-element.335, bf16[512,1536]{1,0:T(8,128)(2,1)} %get-tuple-element.334), kind=kOutput, calls=%fused_computation.21 | convolution fusion | flops 12910067712 | bytes 35651584 | tf_op jit(solution)/shard_map/dot_general | solution.py:16
  416.6 16.7 %collective-permute-done.27 = f32[128,2048]{1,0:T(8,128)} collective-permute-done((f32[128,2048]{1,0:T(8,128)S(1)}, f32[128,2048]{1,0:T(8,128)}, u32[]{:S(2)}, u32[]{:S(2)}) %collective-permute-start.27) | collective-permute-done | bytes 1048608 | tf_op jit(solution)/shard_map/block_0_gather_1/ppermute | solution.py:127
  488.9 10.9 %collective-permute-done.35 = f32[128,2048]{1,0:T(8,128)S(1)} collective-permute-done((f32[128,2048]{1,0:T(8,128)S(1)}, f32[128,2048]{1,0:T(8,128)S(1)}, u32[]{:S(2)}, u32[]{:S(2)}) %collective-permute-start.35) | collective-permute-done | bytes 1048608 | tf_op jit(solution)/shard_map/normed_1_sum_2/ppermute | solution.py:134
  514.3 10.6 %collective-permute-done.37 = f32[128,2048]{1,0:T(8,128)S(1)} collective-permute-done((f32[128,2048]{1,0:T(8,128)}, f32[128,2048]{1,0:T(8,128)S(1)}, u32[]{:S(2)}, u32[]{:S(2)}) %collective-permute-start.37) | collective-permute-done | bytes 1048608 | tf_op jit(solution)/shard_map/normed_1_sum_3/ppermute | solution.py:134
  559.0 12.1 %collective-permute-done.39 = f32[128,2048]{1,0:T(8,128)S(1)} collective-permute-done((f32[128,2048]{1,0:T(8,128)S(1)}, f32[128,2048]{1,0:T(8,128)S(1)}, u32[]{:S(2)}, u32[]{:S(2)}) %collective-permute-start.39) | collective-permute-done | bytes 1048608 | tf_op jit(solution)/shard_map/input_0_sum_1/ppermute | solution.py:134
  645.6 9.2 collective-permute-done.48
  674.8 8.5 collective-permute-done.53
  701.0 10.8 %collective-permute-done.54 = f32[128,2048]{1,0:T(8,128)S(1)} collective-permute-done((f32[128,2048]{1,0:T(8,128)S(1)}, f32[128,2048]{1,0:T(8,128)S(1)}, u32[]{:S(2)}, u32[]{:S(2)}) %collective-permute-start.54) | collective-permute-done | bytes 1048608 | tf_op jit(solution)/shard_map/down_1_sum_2/ppermute | solution.py:134
  728.1 17.2 %collective-permute-done.58 = f32[128,2048]{1,0:T(8,128)S(1)} collective-permute-done((f32[128,2048]{1,0:T(8,128)S(1)}, f32[128,2048]{1,0:T(8,128)S(1)}, u32[]{:S(2)}, u32[]{:S(2)}) %collective-permute-start.58) | collective-permute-done | bytes 1048608 | tf_op jit(solution)/shard_map/down_1_sum_3/ppermute | solution.py:134
  762.8 14.9 %fusion.39 = f32[2048,1024]{1,0:T(8,128)} fusion(bf16[1024,2048]{1,0:T(8,128)(2,1)S(1)} %copy-done.45, bf16[512,256]{0,1:T(8,128)(2,1)S(1)} %bitcast.410, bf16[512,256]{0,1:T(8,128)(2,1)S(1)} %copy-done.90, bf16[512,512]{0,1:T(8,128)(2,1)S(1)} %copy-done.82, bf16[512,256]{0,1:T(8,128)(2,1)S(1)} %bitcast.426, bf16[512,256]{0,1:T(8,128)(2,1)S(1)} %get-tuple-element.605, ...), kind=kOutput, calls=%fused_computation.78 | convolution fusion | flops 4307550208 | bytes 14680064 | tf_op jit(solution)/shard_map/dot_general | solution.py:16
  798.7 19.5 %collective-permute-done.63 = f32[128,2048]{1,0:T(8,128)S(1)} collective-permute-done((f32[128,2048]{1,0:T(8,128)}, f32[128,2048]{1,0:T(8,128)S(1)}, u32[]{:S(2)}, u32[]{:S(2)}) %collective-permute-start.63) | collective-permute-done | bytes 1048608 | tf_op jit(solution)/shard_map/block_1_gather_2/ppermute | solution.py:128
  823.6 18.5 %collective-permute-done.68 = f32[128,2048]{1,0:T(8,128)S(1)} collective-permute-done((f32[128,2048]{1,0:T(8,128)S(1)}, f32[128,2048]{1,0:T(8,128)S(1)}, u32[]{:S(2)}, u32[]{:S(2)}) %collective-permute-start.68) | collective-permute-done | bytes 1048608 | tf_op jit(solution)/shard_map/input_1_sum_2/ppermute | solution.py:134
  859.8 13.6 %collective-permute-done.70 = f32[128,2048]{1,0:T(8,128)S(1)} collective-permute-done((f32[128,2048]{1,0:T(8,128)S(1)}, f32[128,2048]{1,0:T(8,128)S(1)}, u32[]{:S(2)}, u32[]{:S(2)}) %collective-permute-start.70) | collective-permute-done | bytes 1048608 | tf_op jit(solution)/shard_map/input_1_sum_3/ppermute | solution.py:134
  920.2 13.4 %collective-permute-done.81 = f32[4352]{0:T(1024)S(1)} collective-permute-done((f32[4352]{0:T(1024)S(1)}, f32[4352]{0:T(1024)S(1)}, u32[]{:S(2)}, u32[]{:S(2)}) %collective-permute-start.81) | collective-permute-done | bytes 17440 | tf_op jit(solution)/shard_map/ppermute | solution.py:617
  (791 shorter events, 630.4 us)
Async XLA Ops:
  7.2 51.4 %all-gather.5.cloned.1.call-start = ((), (), s32[]{:S(2)}) async-start(), calls=%async_computation.8 | async-start | bytes 2621440 | tf_op jit(solution)/shard_map/all_gather | solution.py:247
  9.2 141.8 %all-gather.7.cloned.1.call-start = ((), (), s32[]{:S(2)}) async-start(), calls=%async_computation.9 | async-start | bytes 14155776 | tf_op jit(solution)/shard_map/all_gather | solution.py:312
  61.3 377.1 %reduce-scatter.5.cloned.1.call-start = ((), (), s32[]{:S(2)}) async-start(), calls=%async_computation.4 | async-start | bytes 14155776 | tf_op jit(solution)/shard_map/reduce_scatter | solution.py:420
  64.2 26.6 %collective-permute-start.1 = (f32[512,512]{0,1:T(8,128)S(1)}, f32[512,512]{0,1:T(8,128)S(1)}, u32[]{:S(2)}, u32[]{:S(2)}) collective-permute-start(f32[512,512]{0,1:T(8,128)S(1)} %bitcast.424), channel_id=1, source_target_pairs={{1,0},{2,1},{3,2},{5,4},{6,5},{7,6},{9,8},{10,9},{11,10},{13,12},{... | collective-permute-start | bytes 3145736 | tf_op jit(solution)/shard_map/heads_0_gather_1/ppermute | solution.py:128
  92.4 28.2 %collective-permute-start.3 = (f32[512,512]{0,1:T(8,128)S(1)}, f32[512,512]{0,1:T(8,128)}, u32[]{:S(2)}, u32[]{:S(2)}) collective-permute-start(f32[512,512]{0,1:T(8,128)S(1)} %collective-permute-done.1), channel_id=1, source_target_pairs={{1,0},{2,1},{5,4},{6,5},{9,8},{10,9},{13,12},{14,13},{17,16},{18,1... | collective-permute-start | bytes 3145736 | tf_op jit(solution)/shard_map/heads_0_gather_2/ppermute | solution.py:128
  211.7 30.8 %collective-permute-start.14 = (f32[512,512]{0,1:T(8,128)}, f32[512,512]{0,1:T(8,128)S(1)}, u32[]{:S(2)}, u32[]{:S(2)}) collective-permute-start(f32[512,512]{0,1:T(8,128)} %collective-permute-done.8), channel_id=1, source_target_pairs={{2,3},{6,7},{10,11},{14,15},{18,19},{22,23},{26,27},{30,31}} | collective-permute-start | bytes 3145736 | tf_op jit(solution)/shard_map/heads_1_gather_3/ppermute | solution.py:127
  212.5 30.1 %collective-permute-start.15 = (f32[512,512]{0,1:T(8,128)}, f32[512,512]{0,1:T(8,128)S(1)}, u32[]{:S(2)}, u32[]{:S(2)}) collective-permute-start(f32[512,512]{0,1:T(8,128)} %collective-permute-done.9), channel_id=1, source_target_pairs={{1,0},{5,4},{9,8},{13,12},{17,16},{21,20},{25,24},{29,28}} | collective-permute-start | bytes 3145736 | tf_op jit(solution)/shard_map/heads_1_gather_3/ppermute | solution.py:128
  261.2 27.1 %collective-permute-start.16 = (f32[128,2048]{1,0:T(8,128)S(1)}, f32[128,2048]{1,0:T(8,128)}, u32[]{:S(2)}, u32[]{:S(2)}) collective-permute-start(f32[128,2048]{1,0:T(8,128)S(1)} %add.606), channel_id=1, source_target_pairs={{0,1},{1,2},{2,3},{4,5},{5,6},{6,7},{8,9},{9,10},{10,11},{12,13},{... | collective-permute-start | bytes 3145736 | tf_op jit(solution)/shard_map/normed_0_sum_3/ppermute | solution.py:134
  308.7 320.7 %reduce-scatter.7.cloned.1.call-start = ((), (), s32[]{:S(2)}) async-start(), calls=%async_computation.5 | async-start | bytes 28311552 | tf_op jit(solution)/shard_map/reduce_scatter | solution.py:511
  325.9 32.4 %collective-permute-start.24 = (f32[128,512]{1,0:T(8,128)S(1)}, f32[128,512]{1,0:T(8,128)S(1)}, u32[]{:S(2)}, u32[]{:S(2)}) collective-permute-start(f32[128,512]{1,0:T(8,128)S(1)} %get-tuple-element.620), channel_id=1, source_target_pairs={{0,3},{1,0},{2,1},{3,2},{4,7},{5,4},{6,5},{7,6},{8,11},{9,8},{10,9... | collective-permute-start | bytes 786440 | tf_op jit(solution)/shard_map/ppermute | solution.py:384
  327.7 30.5 %collective-permute-start.23 = (f32[128,512]{1,0:T(8,128)S(1)}, f32[128,512]{1,0:T(8,128)S(1)}, u32[]{:S(2)}, u32[]{:S(2)}) collective-permute-start(f32[128,512]{1,0:T(8,128)S(1)} %get-tuple-element.621), channel_id=1, source_target_pairs={{0,2},{1,3},{2,0},{3,1},{4,6},{5,7},{6,4},{7,5},{8,10},{9,11},{10,... | collective-permute-start | bytes 786440 | tf_op jit(solution)/shard_map/ppermute | solution.py:384
  330.8 27.5 %collective-permute-start.22 = (f32[128,512]{1,0:T(8,128)S(1)}, f32[128,512]{1,0:T(8,128)S(1)}, u32[]{:S(2)}, u32[]{:S(2)}) collective-permute-start(f32[128,512]{1,0:T(8,128)S(1)} %get-tuple-element.622), channel_id=1, source_target_pairs={{0,1},{1,2},{2,3},{3,0},{4,5},{5,6},{6,7},{7,4},{8,9},{9,10},{10,1... | collective-permute-start | bytes 786440 | tf_op jit(solution)/shard_map/ppermute | solution.py:384
  365.3 38.5 %collective-permute-start.25 = (f32[128,2048]{1,0:T(8,128)}, f32[128,2048]{1,0:T(8,128)}, u32[]{:S(2)}, u32[]{:S(2)}) collective-permute-start(f32[128,2048]{1,0:T(8,128)} %add.617), channel_id=1, source_target_pairs={{0,1},{1,2},{2,3},{4,5},{5,6},{6,7},{8,9},{9,10},{10,11},{12,13},{... | collective-permute-start | bytes 3145736 | tf_op jit(solution)/shard_map/down_0_sum_3/ppermute | solution.py:134
  374.9 28.9 %collective-permute-start.26 = (f32[128,2048]{1,0:T(8,128)}, f32[128,2048]{1,0:T(8,128)}, u32[]{:S(2)}, u32[]{:S(2)}) collective-permute-start(f32[128,2048]{1,0:T(8,128)} %add.618), channel_id=1, source_target_pairs={{1,0},{2,1},{3,2},{5,4},{6,5},{7,6},{9,8},{10,9},{11,10},{13,12},{... | collective-permute-start | bytes 3145736 | tf_op jit(solution)/shard_map/down_0_sum_3/ppermute | solution.py:135
  438.5 348.2 %reduce-scatter.9.cloned.1.call-start = ((), (), s32[]{:S(2)}) async-start(), calls=%async_computation.6 | async-start | bytes 18874368 | tf_op jit(solution)/shard_map/reduce_scatter | solution.py:558
  454.8 26.0 %collective-permute-start.31 = (f32[128,2048]{1,0:T(8,128)S(1)}, f32[128,2048]{1,0:T(8,128)S(1)}, u32[]{:S(2)}, u32[]{:S(2)}) collective-permute-start(f32[128,2048]{1,0:T(8,128)S(1)} %get-tuple-element.378), channel_id=1, source_target_pairs={{0,1},{4,5},{8,9},{12,13},{16,17},{20,21},{24,25},{28,29}} | collective-permute-start | bytes 3145736 | tf_op jit(solution)/shard_map/normed_1_sum_1/ppermute | solution.py:134
  541.4 29.7 %collective-permute-start.39 = (f32[128,2048]{1,0:T(8,128)S(1)}, f32[128,2048]{1,0:T(8,128)S(1)}, u32[]{:S(2)}, u32[]{:S(2)}) collective-permute-start(f32[128,2048]{1,0:T(8,128)S(1)} %get-tuple-element.385), channel_id=1, source_target_pairs={{0,1},{4,5},{8,9},{12,13},{16,17},{20,21},{24,25},{28,29}} | collective-permute-start | bytes 3145736 | tf_op jit(solution)/shard_map/input_0_sum_1/ppermute | solution.py:134
  543.7 27.4 %collective-permute-start.40 = (f32[128,2048]{1,0:T(8,128)S(1)}, f32[128,2048]{1,0:T(8,128)S(1)}, u32[]{:S(2)}, u32[]{:S(2)}) collective-permute-start(f32[128,2048]{1,0:T(8,128)S(1)} %get-tuple-element.386), channel_id=1, source_target_pairs={{3,2},{7,6},{11,10},{15,14},{19,18},{23,22},{27,26},{31,30}} | collective-permute-start | bytes 3145736 | tf_op jit(solution)/shard_map/input_0_sum_1/ppermute | solution.py:135
  629.3 340.3 %reduce-scatter.11.cloned.1.call-start = ((), (), s32[]{:S(2)}) async-start(), calls=%async_computation.7 | async-start | bytes 9437184 | tf_op jit(solution)/shard_map/reduce_scatter | solution.py:584
  686.1 25.7 %collective-permute-start.54 = (f32[128,2048]{1,0:T(8,128)S(1)}, f32[128,2048]{1,0:T(8,128)S(1)}, u32[]{:S(2)}, u32[]{:S(2)}) collective-permute-start(f32[128,2048]{1,0:T(8,128)S(1)} %add.646), channel_id=1, source_target_pairs={{0,1},{1,2},{4,5},{5,6},{8,9},{9,10},{12,13},{13,14},{16,17},{17,1... | collective-permute-start | bytes 3145736 | tf_op jit(solution)/shard_map/down_1_sum_2/ppermute | solution.py:134
  724.7 27.2 %collective-permute-start.59 = (f32[128,2048]{1,0:T(8,128)S(1)}, f32[128,2048]{1,0:T(8,128)S(1)}, u32[]{:S(2)}, u32[]{:S(2)}) collective-permute-start(f32[128,2048]{1,0:T(8,128)S(1)} %add.649), channel_id=1, source_target_pairs={{1,0},{2,1},{3,2},{5,4},{6,5},{7,6},{9,8},{10,9},{11,10},{13,12},{... | collective-permute-start | bytes 3145736 | tf_op jit(solution)/shard_map/down_1_sum_3/ppermute | solution.py:135
  761.1 25.7 %collective-permute-start.61 = (f32[128,2048]{1,0:T(8,128)}, f32[128,2048]{1,0:T(8,128)}, u32[]{:S(2)}, u32[]{:S(2)}) collective-permute-start(f32[128,2048]{1,0:T(8,128)} %get-tuple-element.434), channel_id=1, source_target_pairs={{1,0},{2,1},{3,2},{5,4},{6,5},{7,6},{9,8},{10,9},{11,10},{13,12},{... | collective-permute-start | bytes 3145736 | tf_op jit(solution)/shard_map/block_1_gather_1/ppermute | solution.py:128
  791.5 26.7 %collective-permute-start.63 = (f32[128,2048]{1,0:T(8,128)}, f32[128,2048]{1,0:T(8,128)S(1)}, u32[]{:S(2)}, u32[]{:S(2)}) collective-permute-start(f32[128,2048]{1,0:T(8,128)} %collective-permute-done.61), channel_id=1, source_target_pairs={{1,0},{2,1},{5,4},{6,5},{9,8},{10,9},{13,12},{14,13},{17,16},{18,1... | collective-permute-start | bytes 3145736 | tf_op jit(solution)/shard_map/block_1_gather_2/ppermute | solution.py:128
  847.6 25.9 %collective-permute-start.70 = (f32[128,2048]{1,0:T(8,128)S(1)}, f32[128,2048]{1,0:T(8,128)S(1)}, u32[]{:S(2)}, u32[]{:S(2)}) collective-permute-start(f32[128,2048]{1,0:T(8,128)S(1)} %add.667), channel_id=1, source_target_pairs={{0,1},{1,2},{2,3},{4,5},{5,6},{6,7},{8,9},{9,10},{10,11},{12,13},{... | collective-permute-start | bytes 3145736 | tf_op jit(solution)/shard_map/input_1_sum_3/ppermute | solution.py:134
  (259 other events, 3808.6 us)
Sparse Core Ops, SparseCore 0:
  10.2 48.3 all-gather.4
  61.4 72.5 all-gather.6
  308.8 92.4 reduce-scatter.4
  438.6 154.4 reduce-scatter.6
  629.5 115.6 reduce-scatter.8
  786.9 72.7 reduce-scatter.10

commit v5 on v4

--- a/solution.py
+++ b/solution.py
@@ -400,7 +400,7 @@
     down_part_0 = jnp.dot(tied(hidden_0, part_0, first_step), down_weight, preferred_element_type=jnp.float32)
 
     mixed_whole_1 = whole_heads(tied(heads_1.slots(), down_part_0))
-    normed_sum_0.go(down_part_0)
+    normed_sum_0.go()
     residual_1, factor_1, normed_1 = residual_rows(1, tied(mixed_whole_1, normed_sum_0.sent))
     normed_sum_0.go(residual_1)
     gate_1, up_1 = gate_up(normed_1)

time: 995 us -> 995 us (level)
    add x28 -> x27, other arithmetic: 26.5 us -> 30.4 us  [go(): pair = (self.last[0] + pair[0], self.last[1] + pair[1])]
where the time goes in v5:
time: 995 us; the launch traced here: 982 us
  waiting for transfers between devices  366 us (37%)
  matrix products  193 us (19%)
  starting transfers between devices  191 us (19%)
  other arithmetic  146 us (15%)
  local copies, waits for them, and re-layouts  68 us (7%)
  between operations  18.6 us (2%)
    ppermute x21, waiting for transfers between devices, reduce_step(): lax.ppermute(pair[0], 'tensor', [(i, i + 1) for i in range(step)])  133 us
    ppermute x18, waiting for transfers between devices, gather_step(): lax.ppermute(pair[1], 'tensor', [(i, i - 1) for i in range(1, count - ste...  122 us
    dot_general x17, matrix products, contract(): lax.dot_general(left, right, (((left_dim,), (right_dim,)), ((), ())), pre...  106 us
    ppermute x21, starting transfers between devices, reduce_step(): lax.ppermute(pair[0], 'tensor', [(i, i + 1) for i in range(step)])  87.5 us
    ppermute x18, waiting for transfers between devices, gather_step(): lax.ppermute(pair[0], 'tensor', [(i, i + 1) for i in range(step - 1, coun...  53.8 us
    ppermute x18, starting transfers between devices, gather_step(): lax.ppermute(pair[0], 'tensor', [(i, i + 1) for i in range(step - 1, coun...  38.7 us
    dynamic_update_slice x23, other arithmetic, in_order(): lax.dynamic_update_slice_in_dim(buffer, (slots[slot] * unit).astype(low),...  33.1 us
    add x27, other arithmetic, go(): pair = (self.last[0] + pair[0], self.last[1] + pair[1])  30.4 us
  transfers between devices with their start and end apart: 95, of which 49 were waited for; matrix products, arithmetic and copies ran while one was open for 37% of the time, Pallas kernels for 0%

profile of v5, /device:TPU:0, one launch (start us, length us, event | category | flops | bytes accessed | tf_op | source)
XLA Modules:
  0.0 982.3 jit_solution(4535910427410999226)
XLA Ops:
  65.5 21.1 %collective-permute-done = f32[512,512]{0,1:T(8,128)S(1)} collective-permute-done((f32[512,512]{0,1:T(8,128)S(1)}, f32[512,512]{0,1:T(8,128)S(1)}, u32[]{:S(2)}, u32[]{:S(2)}) %collective-permute-start) | collective-permute-done | bytes 1048608 | tf_op jit(solution)/shard_map/heads_0_gather_1/ppermute | solution.py:127
  93.7 12.4 %fusion.202 = f32[1024,1536]{1,0:T(8,128)} fusion(bf16[1024,2048]{1,0:T(8,128)(2,1)} %param.29, bf16[1536,2048]{1,0:T(8,128)(2,1)} %param.28), kind=kOutput, calls=%fused_computation.402 | convolution fusion | flops 6442450944 | bytes 16777216 | tf_op jit(solution)/shard_map/dot_general | solution.py:16
  106.2 14.4 %collective-permute-done.3 = f32[512,512]{0,1:T(8,128)} collective-permute-done((f32[512,512]{0,1:T(8,128)S(1)}, f32[512,512]{0,1:T(8,128)}, u32[]{:S(2)}, u32[]{:S(2)}) %collective-permute-start.3) | collective-permute-done | bytes 1048608 | tf_op jit(solution)/shard_map/heads_0_gather_2/ppermute | solution.py:128
  127.2 20.3 %collective-permute-done.5 = f32[512,512]{0,1:T(8,128)} collective-permute-done((f32[512,512]{0,1:T(8,128)}, f32[512,512]{0,1:T(8,128)}, u32[]{:S(2)}, u32[]{:S(2)}) %collective-permute-start.5) | collective-permute-done | bytes 1048608 | tf_op jit(solution)/shard_map/heads_0_gather_3/ppermute | solution.py:128
  215.2 13.4 %collective-permute-done.10 = f32[128,2048]{1,0:T(8,128)} collective-permute-done((f32[128,2048]{1,0:T(8,128)S(1)}, f32[128,2048]{1,0:T(8,128)}, u32[]{:S(2)}, u32[]{:S(2)}) %collective-permute-start.10) | collective-permute-done | bytes 1048608 | tf_op jit(solution)/shard_map/normed_0_sum_1/ppermute | solution.py:134
  262.4 10.2 %collective-permute-start.16 = (f32[128,2048]{1,0:T(8,128)S(1)}, f32[128,2048]{1,0:T(8,128)}, u32[]{:S(2)}, u32[]{:S(2)}) collective-permute-start(f32[128,2048]{1,0:T(8,128)S(1)} %add.606), channel_id=1, source_target_pairs={{0,1},{1,2},{2,3},{4,5},{5,6},{6,7},{8,9},{9,10},{10,11},{12,13},{... | collective-permute-start | bytes 3145736 | tf_op jit(solution)/shard_map/normed_0_sum_3/ppermute | solution.py:134
  274.3 8.9 fusion.208
  298.2 9.4 fusion.32
  368.0 9.6 collective-permute-start.25
  379.1 27.5 %fusion.12 = f32[2048,3072]{1,0:T(8,128)} fusion(bf16[1024,2048]{1,0:T(8,128)(2,1)} %pad_maximum_fusion.1, bf16[512,1536]{1,0:T(8,128)(2,1)S(1)} %copy-done.95, bf16[512,1536]{1,0:T(8,128)(2,1)S(1)} %copy-done.97, bf16[512,1536]{1,0:T(8,128)(2,1)} %get-tuple-element.331, bf16[512,1536]{1,0:T(8,128)(2,1)} %get-tuple-element.330), kind=kOutput, calls=%fused_computation.21 | convolution fusion | flops 12910067712 | bytes 35651584 | tf_op jit(solution)/shard_map/dot_general | solution.py:16
  419.4 16.6 %collective-permute-done.27 = f32[128,2048]{1,0:T(8,128)} collective-permute-done((f32[128,2048]{1,0:T(8,128)S(1)}, f32[128,2048]{1,0:T(8,128)}, u32[]{:S(2)}, u32[]{:S(2)}) %collective-permute-start.27) | collective-permute-done | bytes 1048608 | tf_op jit(solution)/shard_map/block_0_gather_1/ppermute | solution.py:127
  491.7 10.9 %collective-permute-done.35 = f32[128,2048]{1,0:T(8,128)S(1)} collective-permute-done((f32[128,2048]{1,0:T(8,128)S(1)}, f32[128,2048]{1,0:T(8,128)S(1)}, u32[]{:S(2)}, u32[]{:S(2)}) %collective-permute-start.35) | collective-permute-done | bytes 1048608 | tf_op jit(solution)/shard_map/normed_1_sum_2/ppermute | solution.py:134
  517.1 10.6 %collective-permute-done.37 = f32[128,2048]{1,0:T(8,128)S(1)} collective-permute-done((f32[128,2048]{1,0:T(8,128)}, f32[128,2048]{1,0:T(8,128)S(1)}, u32[]{:S(2)}, u32[]{:S(2)}) %collective-permute-start.37) | collective-permute-done | bytes 1048608 | tf_op jit(solution)/shard_map/normed_1_sum_3/ppermute | solution.py:134
  562.1 12.1 %collective-permute-done.39 = f32[128,2048]{1,0:T(8,128)S(1)} collective-permute-done((f32[128,2048]{1,0:T(8,128)S(1)}, f32[128,2048]{1,0:T(8,128)S(1)}, u32[]{:S(2)}, u32[]{:S(2)}) %collective-permute-start.39) | collective-permute-done | bytes 1048608 | tf_op jit(solution)/shard_map/input_0_sum_1/ppermute | solution.py:134
  586.9 8.8 collective-permute-done.44
  651.3 10.0 %collective-permute-done.48 = f32[128,2048]{1,0:T(8,128)} collective-permute-done((f32[128,2048]{1,0:T(8,128)S(1)}, f32[128,2048]{1,0:T(8,128)}, u32[]{:S(2)}, u32[]{:S(2)}) %collective-permute-start.48) | collective-permute-done | bytes 1048608 | tf_op jit(solution)/shard_map/tokens_0_gather_1/ppermute | solution.py:127
  681.1 9.4 collective-permute-done.53
  704.1 9.7 collective-permute-done.54
  730.4 16.3 %collective-permute-done.58 = f32[128,2048]{1,0:T(8,128)S(1)} collective-permute-done((f32[128,2048]{1,0:T(8,128)S(1)}, f32[128,2048]{1,0:T(8,128)S(1)}, u32[]{:S(2)}, u32[]{:S(2)}) %collective-permute-start.58) | collective-permute-done | bytes 1048608 | tf_op jit(solution)/shard_map/down_1_sum_3/ppermute | solution.py:134
  766.0 15.0 %fusion.39 = f32[2048,1024]{1,0:T(8,128)} fusion(bf16[1024,2048]{1,0:T(8,128)(2,1)S(1)} %copy-done.49, bf16[512,256]{0,1:T(8,128)(2,1)S(1)} %bitcast.412, bf16[512,256]{0,1:T(8,128)(2,1)S(1)} %copy-done.93, bf16[512,512]{0,1:T(8,128)(2,1)S(1)} %copy-done.85, bf16[512,256]{0,1:T(8,128)(2,1)S(1)} %bitcast.428, bf16[512,256]{0,1:T(8,128)(2,1)S(1)} %get-tuple-element.602, ...), kind=kOutput, calls=%fused_computation.78 | convolution fusion | flops 4307550208 | bytes 14680064 | tf_op jit(solution)/shard_map/dot_general | solution.py:16
  802.9 19.8 %collective-permute-done.63 = f32[128,2048]{1,0:T(8,128)S(1)} collective-permute-done((f32[128,2048]{1,0:T(8,128)}, f32[128,2048]{1,0:T(8,128)S(1)}, u32[]{:S(2)}, u32[]{:S(2)}) %collective-permute-start.63) | collective-permute-done | bytes 1048608 | tf_op jit(solution)/shard_map/block_1_gather_2/ppermute | solution.py:128
  827.4 19.4 %collective-permute-done.68 = f32[128,2048]{1,0:T(8,128)S(1)} collective-permute-done((f32[128,2048]{1,0:T(8,128)S(1)}, f32[128,2048]{1,0:T(8,128)S(1)}, u32[]{:S(2)}, u32[]{:S(2)}) %collective-permute-start.68) | collective-permute-done | bytes 1048608 | tf_op jit(solution)/shard_map/input_1_sum_2/ppermute | solution.py:134
  863.5 12.7 %collective-permute-done.70 = f32[128,2048]{1,0:T(8,128)S(1)} collective-permute-done((f32[128,2048]{1,0:T(8,128)S(1)}, f32[128,2048]{1,0:T(8,128)S(1)}, u32[]{:S(2)}, u32[]{:S(2)}) %collective-permute-start.70) | collective-permute-done | bytes 1048608 | tf_op jit(solution)/shard_map/input_1_sum_3/ppermute | solution.py:134
  920.5 12.2 %collective-permute-done.81 = f32[4352]{0:T(1024)S(1)} collective-permute-done((f32[4352]{0:T(1024)S(1)}, f32[4352]{0:T(1024)S(1)}, u32[]{:S(2)}, u32[]{:S(2)}) %collective-permute-start.81) | collective-permute-done | bytes 17440 | tf_op jit(solution)/shard_map/ppermute | solution.py:617
  (809 shorter events, 633.0 us)
Async XLA Ops:
  7.2 51.4 %all-gather.5.cloned.1.call-start = ((), (), s32[]{:S(2)}) async-start(), calls=%async_computation.8 | async-start | bytes 2621440 | tf_op jit(solution)/shard_map/all_gather | solution.py:247
  9.2 141.9 %all-gather.7.cloned.1.call-start = ((), (), s32[]{:S(2)}) async-start(), calls=%async_computation.9 | async-start | bytes 14155776 | tf_op jit(solution)/shard_map/all_gather | solution.py:312
  61.3 379.8 %reduce-scatter.5.cloned.1.call-start = ((), (), s32[]{:S(2)}) async-start(), calls=%async_computation.4 | async-start | bytes 14155776 | tf_op jit(solution)/shard_map/reduce_scatter | solution.py:420
  64.2 26.5 %collective-permute-start.1 = (f32[512,512]{0,1:T(8,128)S(1)}, f32[512,512]{0,1:T(8,128)S(1)}, u32[]{:S(2)}, u32[]{:S(2)}) collective-permute-start(f32[512,512]{0,1:T(8,128)S(1)} %bitcast.426), channel_id=1, source_target_pairs={{1,0},{2,1},{3,2},{5,4},{6,5},{7,6},{9,8},{10,9},{11,10},{13,12},{... | collective-permute-start | bytes 3145736 | tf_op jit(solution)/shard_map/heads_0_gather_1/ppermute | solution.py:128
  92.4 28.2 %collective-permute-start.3 = (f32[512,512]{0,1:T(8,128)S(1)}, f32[512,512]{0,1:T(8,128)}, u32[]{:S(2)}, u32[]{:S(2)}) collective-permute-start(f32[512,512]{0,1:T(8,128)S(1)} %collective-permute-done.1), channel_id=1, source_target_pairs={{1,0},{2,1},{5,4},{6,5},{9,8},{10,9},{13,12},{14,13},{17,16},{18,1... | collective-permute-start | bytes 3145736 | tf_op jit(solution)/shard_map/heads_0_gather_2/ppermute | solution.py:128
  187.2 25.8 %collective-permute-start.8 = (f32[512,512]{0,1:T(8,128)}, f32[512,512]{0,1:T(8,128)}, u32[]{:S(2)}, u32[]{:S(2)}) collective-permute-start(f32[512,512]{0,1:T(8,128)} %collective-permute-done.6), channel_id=1, source_target_pairs={{1,2},{2,3},{5,6},{6,7},{9,10},{10,11},{13,14},{14,15},{17,18},{18... | collective-permute-start | bytes 3145736 | tf_op jit(solution)/shard_map/heads_1_gather_2/ppermute | solution.py:127
  213.1 32.8 %collective-permute-start.14 = (f32[512,512]{0,1:T(8,128)}, f32[512,512]{0,1:T(8,128)S(1)}, u32[]{:S(2)}, u32[]{:S(2)}) collective-permute-start(f32[512,512]{0,1:T(8,128)} %collective-permute-done.8), channel_id=1, source_target_pairs={{2,3},{6,7},{10,11},{14,15},{18,19},{22,23},{26,27},{30,31}} | collective-permute-start | bytes 3145736 | tf_op jit(solution)/shard_map/heads_1_gather_3/ppermute | solution.py:127
  213.9 32.0 %collective-permute-start.15 = (f32[512,512]{0,1:T(8,128)}, f32[512,512]{0,1:T(8,128)S(1)}, u32[]{:S(2)}, u32[]{:S(2)}) collective-permute-start(f32[512,512]{0,1:T(8,128)} %collective-permute-done.9), channel_id=1, source_target_pairs={{1,0},{5,4},{9,8},{13,12},{17,16},{21,20},{25,24},{29,28}} | collective-permute-start | bytes 3145736 | tf_op jit(solution)/shard_map/heads_1_gather_3/ppermute | solution.py:128
  262.4 28.4 %collective-permute-start.16 = (f32[128,2048]{1,0:T(8,128)S(1)}, f32[128,2048]{1,0:T(8,128)}, u32[]{:S(2)}, u32[]{:S(2)}) collective-permute-start(f32[128,2048]{1,0:T(8,128)S(1)} %add.606), channel_id=1, source_target_pairs={{0,1},{1,2},{2,3},{4,5},{5,6},{6,7},{8,9},{9,10},{10,11},{12,13},{... | collective-permute-start | bytes 3145736 | tf_op jit(solution)/shard_map/normed_0_sum_3/ppermute | solution.py:134
  311.2 322.8 %reduce-scatter.7.cloned.1.call-start = ((), (), s32[]{:S(2)}) async-start(), calls=%async_computation.5 | async-start | bytes 28311552 | tf_op jit(solution)/shard_map/reduce_scatter | solution.py:511
  328.5 32.5 %collective-permute-start.24 = (f32[128,512]{1,0:T(8,128)S(1)}, f32[128,512]{1,0:T(8,128)S(1)}, u32[]{:S(2)}, u32[]{:S(2)}) collective-permute-start(f32[128,512]{1,0:T(8,128)S(1)} %get-tuple-element.617), channel_id=1, source_target_pairs={{0,3},{1,0},{2,1},{3,2},{4,7},{5,4},{6,5},{7,6},{8,11},{9,8},{10,9... | collective-permute-start | bytes 786440 | tf_op jit(solution)/shard_map/ppermute | solution.py:384
  330.3 30.6 %collective-permute-start.23 = (f32[128,512]{1,0:T(8,128)S(1)}, f32[128,512]{1,0:T(8,128)S(1)}, u32[]{:S(2)}, u32[]{:S(2)}) collective-permute-start(f32[128,512]{1,0:T(8,128)S(1)} %get-tuple-element.618), channel_id=1, source_target_pairs={{0,2},{1,3},{2,0},{3,1},{4,6},{5,7},{6,4},{7,5},{8,10},{9,11},{10,... | collective-permute-start | bytes 786440 | tf_op jit(solution)/shard_map/ppermute | solution.py:384
  333.4 27.6 %collective-permute-start.22 = (f32[128,512]{1,0:T(8,128)S(1)}, f32[128,512]{1,0:T(8,128)S(1)}, u32[]{:S(2)}, u32[]{:S(2)}) collective-permute-start(f32[128,512]{1,0:T(8,128)S(1)} %get-tuple-element.619), channel_id=1, source_target_pairs={{0,1},{1,2},{2,3},{3,0},{4,5},{5,6},{6,7},{7,4},{8,9},{9,10},{10,1... | collective-permute-start | bytes 786440 | tf_op jit(solution)/shard_map/ppermute | solution.py:384
  368.0 38.6 %collective-permute-start.25 = (f32[128,2048]{1,0:T(8,128)}, f32[128,2048]{1,0:T(8,128)}, u32[]{:S(2)}, u32[]{:S(2)}) collective-permute-start(f32[128,2048]{1,0:T(8,128)} %add.617), channel_id=1, source_target_pairs={{0,1},{1,2},{2,3},{4,5},{5,6},{6,7},{8,9},{9,10},{10,11},{12,13},{... | collective-permute-start | bytes 3145736 | tf_op jit(solution)/shard_map/down_0_sum_3/ppermute | solution.py:134
  377.6 29.0 %collective-permute-start.26 = (f32[128,2048]{1,0:T(8,128)}, f32[128,2048]{1,0:T(8,128)}, u32[]{:S(2)}, u32[]{:S(2)}) collective-permute-start(f32[128,2048]{1,0:T(8,128)} %add.618), channel_id=1, source_target_pairs={{1,0},{2,1},{3,2},{5,4},{6,5},{7,6},{9,8},{10,9},{11,10},{13,12},{... | collective-permute-start | bytes 3145736 | tf_op jit(solution)/shard_map/down_0_sum_3/ppermute | solution.py:135
  441.2 349.7 %reduce-scatter.9.cloned.1.call-start = ((), (), s32[]{:S(2)}) async-start(), calls=%async_computation.6 | async-start | bytes 18874368 | tf_op jit(solution)/shard_map/reduce_scatter | solution.py:558
  457.6 25.8 %collective-permute-start.31 = (f32[128,2048]{1,0:T(8,128)S(1)}, f32[128,2048]{1,0:T(8,128)S(1)}, u32[]{:S(2)}, u32[]{:S(2)}) collective-permute-start(f32[128,2048]{1,0:T(8,128)S(1)} %get-tuple-element.374), channel_id=1, source_target_pairs={{0,1},{4,5},{8,9},{12,13},{16,17},{20,21},{24,25},{28,29}} | collective-permute-start | bytes 3145736 | tf_op jit(solution)/shard_map/normed_1_sum_1/ppermute | solution.py:134
  544.4 29.7 %collective-permute-start.39 = (f32[128,2048]{1,0:T(8,128)S(1)}, f32[128,2048]{1,0:T(8,128)S(1)}, u32[]{:S(2)}, u32[]{:S(2)}) collective-permute-start(f32[128,2048]{1,0:T(8,128)S(1)} %get-tuple-element.381), channel_id=1, source_target_pairs={{0,1},{4,5},{8,9},{12,13},{16,17},{20,21},{24,25},{28,29}} | collective-permute-start | bytes 3145736 | tf_op jit(solution)/shard_map/input_0_sum_1/ppermute | solution.py:134
  546.7 27.4 %collective-permute-start.40 = (f32[128,2048]{1,0:T(8,128)S(1)}, f32[128,2048]{1,0:T(8,128)S(1)}, u32[]{:S(2)}, u32[]{:S(2)}) collective-permute-start(f32[128,2048]{1,0:T(8,128)S(1)} %get-tuple-element.382), channel_id=1, source_target_pairs={{3,2},{7,6},{11,10},{15,14},{19,18},{23,22},{27,26},{31,30}} | collective-permute-start | bytes 3145736 | tf_op jit(solution)/shard_map/input_0_sum_1/ppermute | solution.py:135
  634.0 335.6 %reduce-scatter.11.cloned.1.call-start = ((), (), s32[]{:S(2)}) async-start(), calls=%async_computation.7 | async-start | bytes 9437184 | tf_op jit(solution)/shard_map/reduce_scatter | solution.py:584
  727.0 26.1 %collective-permute-start.59 = (f32[128,2048]{1,0:T(8,128)S(1)}, f32[128,2048]{1,0:T(8,128)S(1)}, u32[]{:S(2)}, u32[]{:S(2)}) collective-permute-start(f32[128,2048]{1,0:T(8,128)S(1)} %add.649), channel_id=1, source_target_pairs={{1,0},{2,1},{3,2},{5,4},{6,5},{7,6},{9,8},{10,9},{11,10},{13,12},{... | collective-permute-start | bytes 3145736 | tf_op jit(solution)/shard_map/down_1_sum_3/ppermute | solution.py:135
  756.1 26.1 %collective-permute-start.60 = (f32[128,2048]{1,0:T(8,128)}, f32[128,2048]{1,0:T(8,128)}, u32[]{:S(2)}, u32[]{:S(2)}) collective-permute-start(f32[128,2048]{1,0:T(8,128)} %get-tuple-element.430), channel_id=1, source_target_pairs={{0,1},{1,2},{2,3},{4,5},{5,6},{6,7},{8,9},{9,10},{10,11},{12,13},{... | collective-permute-start | bytes 3145736 | tf_op jit(solution)/shard_map/block_1_gather_1/ppermute | solution.py:127
  764.2 26.7 %collective-permute-start.61 = (f32[128,2048]{1,0:T(8,128)}, f32[128,2048]{1,0:T(8,128)}, u32[]{:S(2)}, u32[]{:S(2)}) collective-permute-start(f32[128,2048]{1,0:T(8,128)} %get-tuple-element.430), channel_id=1, source_target_pairs={{1,0},{2,1},{3,2},{5,4},{6,5},{7,6},{9,8},{10,9},{11,10},{13,12},{... | collective-permute-start | bytes 3145736 | tf_op jit(solution)/shard_map/block_1_gather_1/ppermute | solution.py:128
  795.7 27.0 %collective-permute-start.63 = (f32[128,2048]{1,0:T(8,128)}, f32[128,2048]{1,0:T(8,128)S(1)}, u32[]{:S(2)}, u32[]{:S(2)}) collective-permute-start(f32[128,2048]{1,0:T(8,128)} %collective-permute-done.61), channel_id=1, source_target_pairs={{1,0},{2,1},{5,4},{6,5},{9,8},{10,9},{13,12},{14,13},{17,16},{18,1... | collective-permute-start | bytes 3145736 | tf_op jit(solution)/shard_map/block_1_gather_2/ppermute | solution.py:128
  (267 other events, 3745.5 us)
Sparse Core Ops, SparseCore 0:
  10.2 48.3 all-gather.4
  61.4 72.5 all-gather.6
  311.3 92.4 reduce-scatter.4
  441.3 154.4 reduce-scatter.6
  634.1 113.8 reduce-scatter.8
  791.0 70.5 reduce-scatter.10
